TPU v7x, 768 devices: a whole 4x8x12 slice. The times are simulated.
768 devices in a mesh: dom: 128 (over x, z_lo, y), band: 6 (over z_hi, core).
Axes of the slice: x: 4, y: 8, z: 12 (z_hi: 3, z_lo: 4; z = z_hi * 4 + z_lo), core: 2. Of those that a mesh axis runs over, the one named last changes fastest.
Arguments:
- wave: float32 [24, 512, 64, 128], P('band', 'dom'), parts along dimension 0, may hold values from -6 to 6
- potential: float32 [512, 64, 128], P('dom'), may hold values from -6 to 6
- energies: float32 [24], P('band'), parts along dimension 0, may hold values from -1 to 1
- proj_index: int32 [4096, 256], P('dom'), may hold values from 0 to 32767
- proj_values: float32 [4096, 8, 256], P('dom'), may hold values from -4 to 4
- slot_atom: int32 [4096], P('dom'), may hold values from 0 to 3072, as said below
- atom_rank: int32 [3072], replicated, may hold values from 0 to 3071, as said below
- d_matrix: float32 [3072, 8, 8], P('dom'), may hold values from -5 to 5
- q_matrix: float32 [3072, 8, 8], P('dom'), may hold values from -5 to 5
Outputs:
- residual: float32 [24, 512, 64, 128], P('band', 'dom'), parts along dimension 0
There are 6 independent parts, one for each index of `band`. A program takes and returns all parts, laid end to end along the dimension named above; an argument that names none is the same for every part. Nothing has to cross between parts.
Inputs may be any that keep to these rules, and one draw needn't show every extreme that they name: `slot_atom`: every device holds at least 8 live slots, live slots come first among a device's slots, and in every draw some device has all 32 slots live and some has only 8. The atom of a live slot on device d has atom_rank // 24 within 2 of d, counted cyclically over the devices. `atom_rank`: A permutation of the atoms.
All inputs are finite; a program needn't handle non-finite values.
Results may differ from a plain program's by a relative error of at most 0.00007.
Values sent between devices are 32-bit elements; how exact they have to be, the bound alone decides.
No kernel may reach another device: no remote copies, remote signals or barrier semaphores. Data moves between devices by JAX's collectives and lax.ppermute only.
A program may use at most 64 MiB of HBM per device.

v0:
```python
import jax
import jax.numpy as jnp
from jax import lax
from jax.sharding import PartitionSpec as P

HIGH = lax.Precision.HIGHEST


def extended(block, sides, width):
    for axis, dim in sides:
        count = lax.axis_size(axis)
        forward = [(i, i + 1) for i in range(count - 1)]
        forward.append((count - 1, 0))
        backward = [(target, source) for source, target in forward]
        low = lax.ppermute(
            lax.slice_in_dim(block, block.shape[dim] - width, None, axis=dim), axis, forward
        )
        high = lax.ppermute(lax.slice_in_dim(block, 0, width, axis=dim), axis, backward)
        block = jnp.concatenate([low, block, high], axis=dim)
    return block


def shifted(value, axis, steps):
    count = lax.axis_size(axis)
    pairs = [(source, (source + steps) % count) for source in range(count)]
    return lax.ppermute(value, axis, pairs)


def inner_axes(field, operator):
    total = operator
    for axis in (2, 3):
        total = total - 2.5 * field
        total = total + 4.0 / 3.0 * (jnp.roll(field, 1, axis) + jnp.roll(field, -1, axis))
        total = total - 1.0 / 12.0 * (jnp.roll(field, 2, axis) + jnp.roll(field, -2, axis))
    return total


def weigh(rows, d_part, q_part, energies, bands, nproj):
    coeffs = rows.reshape(rows.shape[0], bands, nproj)
    weight = jnp.einsum("aij,anj->ani", d_part, coeffs, precision=HIGH)
    weight = weight - energies[None, :, None] * jnp.einsum(
        "aij,anj->ani", q_part, coeffs, precision=HIGH
    )
    return weight.reshape(rows.shape[0], bands * nproj)


def per_device(
    wave, potential, energies, proj_index, proj_values, slot_atom, atom_rank, d_matrix, q_matrix
):
    bands = wave.shape[0]
    slot_count = proj_index.shape[0]
    nproj = proj_values.shape[1]
    atoms_all = atom_rank.shape[0]
    atoms_dev = d_matrix.shape[0]
    n_dom = lax.axis_size("dom")
    padded = extended(wave, (("dom", 1),), 2)
    center = padded[:, 2:-2]
    along_x = (
        -2.5 * center
        + 4.0 / 3.0 * (padded[:, 3:-1] + padded[:, 1:-3])
        - 1.0 / 12.0 * (padded[:, 4:] + padded[:, :-4])
    )
    laplace_all = inner_axes(center, along_x)
    local = -0.5 * laplace_all + (potential[None] - energies[:, None, None, None]) * center
    flat_index = proj_index.reshape(-1)
    picked = jnp.take(center.reshape(bands, -1), flat_index, axis=1).reshape(bands, slot_count, -1)
    coeff = jnp.einsum("nsp,sip->sni", picked, proj_values, precision=HIGH).reshape(
        slot_count, bands * nproj
    )
    live = slot_atom < atoms_all
    position = jnp.where(live, atom_rank[jnp.minimum(slot_atom, atoms_all - 1)], 0)
    myself = lax.axis_index("dom")
    offset = (position // atoms_dev - myself + 2 + n_dom) % n_dom
    column = jnp.where(live, offset * atoms_dev + position % atoms_dev, 5 * atoms_dev)
    table = (column[:, None] == jnp.arange(5 * atoms_dev, dtype=jnp.int32)[None, :]).astype(
        jnp.float32
    )
    partial_value = jnp.einsum("sa,sk->ak", table, coeff, precision=HIGH)

    def block(step):
        return partial_value[(step + 2) * atoms_dev : (step + 3) * atoms_dev]

    total = block(0)
    for step in (-2, -1, 1, 2):
        total = total + shifted(block(step), "dom", step)
    weighted = weigh(total, d_matrix, q_matrix, energies, bands, nproj)
    windows = {0: weighted}
    for step in (-2, -1, 1, 2):
        windows[step] = shifted(weighted, "dom", -step)
    stacked = jnp.concatenate(
        [windows[-2], windows[-1], windows[0], windows[1], windows[2]], axis=0
    )
    slot_weight = jnp.dot(table, stacked, precision=HIGH).reshape(slot_count, bands, nproj)
    back = jnp.einsum("sni,sip->nsp", slot_weight, proj_values, precision=HIGH).reshape(bands, -1)
    result = local.reshape(bands, -1).at[:, flat_index].add(back)
    return result.reshape(wave.shape)


def solution(mesh):
    placed = (
        P("band", "dom", None, None),
        P("dom", None, None),
        P("band"),
        P("dom", None),
        P("dom", None, None),
        P("dom"),
        P(),
        P("dom", None, None),
        P("dom", None, None),
    )
    return jax.shard_map(
        per_device,
        mesh=mesh,
        in_specs=placed,
        out_specs=P("band", "dom", None, None),
        check_vma=False,
    )
```

profile of v0, /device:TPU:8, one launch (start us, length us, event | category | flops | bytes accessed | tf_op | source)
XLA Modules:
  0.0 185.7 jit_solution(9046940752153944632)
XLA Ops:
  1.8 9.7 %copy.19 = f32[4,4,64,128]{0,3,2,1:T(8,128)} copy(f32[4,4,64,128]{3,2,1,0:T(8,128)} %param.9) | data formatting | bytes 1048576 | tf_op args[0]
  11.5 33.5 %gather_fusion.1 = f32[8192,4]{1,0:T(8,128)} fusion(f32[4,32768]{0,1:T(8,128)} %bitcast.34, s32[8192]{0:T(1024)S(1)} %broadcast_clamp_fusion), kind=kCustom, calls=%fused_computation.1 | custom fusion | bytes 294912 | tf_op jit(solution)/shard_map/jit(_take)/gather | solution.py:66
  45.0 2.8 %copy.20 = f32[4,32,256]{2,0,1:T(4,128)S(1)} copy(f32[4,32,256]{0,2,1:T(8,128)} %bitcast.35) | data formatting | bytes 262144 | tf_op jit(solution)/shard_map/jit(_take)/gather | solution.py:66
  50.0 12.9 %collective-permute-start.2 = (f32[24,32]{0,1:T(8,128)}, f32[24,32]{0,1:T(8,128)S(1)}, u32[]{:S(2)}, u32[]{:S(2)}) collective-permute-start(f32[24,32]{0,1:T(8,128)} %get-tuple-element.25), channel_id=1, source_target_pairs={{0,756},{6,762},{12,0},{18,6},{24,12},{30,18},{36,24},{42,30},{48,... | collective-permute-start | bytes 9224 | tf_op jit(solution)/shard_map/ppermute | solution.py:26
  62.9 3.3 %collective-permute-start.3 = (f32[24,32]{0,1:T(8,128)}, f32[24,32]{0,1:T(8,128)S(1)}, u32[]{:S(2)}, u32[]{:S(2)}) collective-permute-start(f32[24,32]{0,1:T(8,128)} %get-tuple-element.28), channel_id=1, source_target_pairs={{0,762},{6,0},{12,6},{18,12},{24,18},{30,24},{36,30},{42,36},{48,4... | collective-permute-start | bytes 9224 | tf_op jit(solution)/shard_map/ppermute | solution.py:26
  66.1 2.6 %collective-permute-start.4 = (f32[24,32]{0,1:T(8,128)}, f32[24,32]{0,1:T(8,128)S(1)}, u32[]{:S(2)}, u32[]{:S(2)}) collective-permute-start(f32[24,32]{0,1:T(8,128)} %get-tuple-element.27), channel_id=1, source_target_pairs={{0,6},{6,12},{12,18},{18,24},{24,30},{30,36},{36,42},{42,48},{48,5... | collective-permute-start | bytes 9224 | tf_op jit(solution)/shard_map/ppermute | solution.py:26
  68.7 1.9 %collective-permute-start.5 = (f32[24,32]{0,1:T(8,128)S(1)}, f32[24,32]{0,1:T(8,128)}, u32[]{:S(2)}, u32[]{:S(2)}) collective-permute-start(f32[24,32]{0,1:T(8,128)S(1)} %get-tuple-element.26), channel_id=1, source_target_pairs={{0,12},{6,18},{12,24},{18,30},{24,36},{30,42},{36,48},{42,54},{48,... | collective-permute-start | bytes 9224 | tf_op jit(solution)/shard_map/ppermute | solution.py:26
  71.5 1.9 %collective-permute-start.1 = (f32[4,2,64,128]{3,2,1,0:T(8,128)}, f32[4,2,64,128]{3,2,1,0:T(8,128)S(1)}, u32[]{:S(2)}, u32[]{:S(2)}) collective-permute-start(f32[4,2,64,128]{3,2,1,0:T(8,128)} %get-tuple-element.22), channel_id=1, source_target_pairs={{0,6},{6,12},{12,18},{18,24},{24,30},{30,36},{36,42},{42,48},{48,5... | collective-permute-start | bytes 786440 | tf_op jit(solution)/shard_map/ppermute | solution.py:15
  73.8 1.1 fusion.36
  74.9 1.0 fusion.38
  75.9 1.1 fusion.32
  77.0 1.1 fusion.33
  78.5 3.0 %collective-permute-done.5 = f32[24,32]{0,1:T(8,128)} collective-permute-done((f32[24,32]{0,1:T(8,128)S(1)}, f32[24,32]{0,1:T(8,128)}, u32[]{:S(2)}, u32[]{:S(2)}) %collective-permute-start.5) | collective-permute-done | bytes 3104 | tf_op jit(solution)/shard_map/ppermute | solution.py:26
  83.7 1.9 %collective-permute-start.6 = (f32[24,32]{0,1:T(8,128)S(1)}, f32[24,32]{0,1:T(8,128)S(1)}, u32[]{:S(2)}, u32[]{:S(2)}) collective-permute-start(f32[24,32]{0,1:T(8,128)S(1)} %bitcast.41), channel_id=1, source_target_pairs={{0,12},{6,18},{12,24},{18,30},{24,36},{30,42},{36,48},{42,54},{48,... | collective-permute-start | bytes 9224 | tf_op jit(solution)/shard_map/ppermute | solution.py:26
  85.6 1.9 %collective-permute-start.7 = (f32[24,32]{0,1:T(8,128)S(1)}, f32[24,32]{0,1:T(8,128)S(1)}, u32[]{:S(2)}, u32[]{:S(2)}) collective-permute-start(f32[24,32]{0,1:T(8,128)S(1)} %bitcast.42), channel_id=1, source_target_pairs={{0,6},{6,12},{12,18},{18,24},{24,30},{30,36},{36,42},{42,48},{48,5... | collective-permute-start | bytes 9224 | tf_op jit(solution)/shard_map/ppermute | solution.py:26
  87.5 3.9 %collective-permute-start.8 = (f32[24,32]{0,1:T(8,128)S(1)}, f32[24,32]{0,1:T(8,128)S(1)}, u32[]{:S(2)}, u32[]{:S(2)}) collective-permute-start(f32[24,32]{0,1:T(8,128)S(1)} %bitcast.43), channel_id=1, source_target_pairs={{0,762},{6,0},{12,6},{18,12},{24,18},{30,24},{36,30},{42,36},{48,4... | collective-permute-start | bytes 9224 | tf_op jit(solution)/shard_map/ppermute | solution.py:26
  91.5 10.8 %collective-permute-start.9 = (f32[24,32]{0,1:T(8,128)S(1)}, f32[24,32]{0,1:T(8,128)S(1)}, u32[]{:S(2)}, u32[]{:S(2)}) collective-permute-start(f32[24,32]{0,1:T(8,128)S(1)} %bitcast.44), channel_id=1, source_target_pairs={{0,756},{6,762},{12,0},{18,6},{24,12},{30,18},{36,24},{42,30},{48,... | collective-permute-start | bytes 9224 | tf_op jit(solution)/shard_map/ppermute | solution.py:26
  102.4 3.2 %collective-permute-start = (f32[4,2,64,128]{3,2,1,0:T(8,128)}, f32[4,2,64,128]{3,2,1,0:T(8,128)}, u32[]{:S(2)}, u32[]{:S(2)}) collective-permute-start(f32[4,2,64,128]{3,2,1,0:T(8,128)} %get-tuple-element.21), channel_id=1, source_target_pairs={{6,0},{12,6},{18,12},{24,18},{30,24},{36,30},{42,36},{48,42},{54,4... | collective-permute-start | bytes 786440 | tf_op jit(solution)/shard_map/ppermute | solution.py:18
  106.9 2.6 %copy.29 = f32[8192,4]{1,0:T(8,128)} copy(f32[8192,4]{0,1:T(4,128)S(1)} %bitcast.36) | data formatting | bytes 262144 | tf_op jit(solution)/shard_map/reshape | solution.py:94
  109.7 1.3 collective-permute-done
  111.9 3.1 %fusion.9 = f32[4,4,64,128]{3,2,1,0:T(8,128)S(1)} fusion(f32[4,6,64,128]{3,2,1,0:T(8,128)S(1)} %get-tuple-element.24, f32[4,6,64,128]{3,2,1,0:T(8,128)S(1)} %constant_dynamic-update-slice_fusion, f32[4,4,63,128]{3,2,1,0:T(8,128)} %get-tuple-element.18, f32[4,4,1,128]{3,2,1,0:T(1,128)S(1)} %get-tuple-element.20, f32[4,4,1,128]{3,2,1,0:T(1,128)S(1)} %get-tuple-element.19, ...), kind=kLoop, calls=%fused_computation.16 | loop fusion | flops 4456448 | bytes 7471120 | tf_op jit(solution)/shard_map/add | solution.py:64
  115.0 8.7 %copy.18 = f32[4,4,64,128]{0,3,2,1:T(8,128)} copy(f32[4,4,64,128]{3,2,1,0:T(8,128)S(1)} %fusion.9) | data formatting | bytes 1048576 | tf_op jit(solution)/shard_map/add | solution.py:64
  123.7 51.3 %scatter_fusion = f32[4,32768]{0,1:T(8,128)} fusion(f32[4,32768]{0,1:T(8,128)} %bitcast.32, s32[8192]{0:T(1024)S(1)} %bitcast.38, f32[8192,4]{1,0:T(8,128)} %copy.29), kind=kCustom, calls=%fused_computation.2 | custom fusion | flops 32768 | bytes 425984 | tf_op jit(solution)/shard_map/scatter-add | solution.py:95
  175.0 10.7 %copy.30 = f32[4,4,64,128]{3,2,1,0:T(8,128)} copy(f32[4,4,64,128]{0,3,2,1:T(8,128)} %bitcast.33) | data formatting | bytes 1048576 | tf_op jit(solution)/shard_map/reshape | solution.py:96
  (53 shorter events, 9.9 us)
Async XLA Ops:
  0.0 47.8 %copy-start = (f32[32,8,256]{2,1,0:T(8,128)S(1)}, f32[32,8,256]{2,1,0:T(8,128)}, u32[]{:S(2)}) copy-start(f32[32,8,256]{2,1,0:T(8,128)} %param.13) | copy-start | bytes 786436
  0.0 70.6 %copy-start.1 = (f32[4,4,64,128]{3,2,1,0:T(8,128)S(1)}, f32[4,4,64,128]{3,2,1,0:T(8,128)}, u32[]{:S(2)}) copy-start(f32[4,4,64,128]{3,2,1,0:T(8,128)} %param.9) | copy-start | bytes 1572868
  0.0 48.3 %copy-start.5 = (s32[32]{0:T(128)S(1)}, s32[32]{0:T(128)}, u32[]{:S(2)}) copy-start(s32[32]{0:T(128)} %param.14) | copy-start | bytes 388
  0.0 48.3 %copy-start.2 = (s32[3072]{0:T(1024)S(1)}, s32[3072]{0:T(1024)}, u32[]{:S(2)}) copy-start(s32[3072]{0:T(1024)} %param.15) | copy-start | bytes 36868
  1.7 76.5 %copy-start.3 = (f32[24,8,8]{0,2,1:T(8,128)S(1)}, f32[24,8,8]{0,2,1:T(8,128)}, u32[]{:S(2)}) copy-start(f32[24,8,8]{0,2,1:T(8,128)} %param.17) | copy-start | bytes 18436
  1.7 76.6 %copy-start.4 = (f32[24,8,8]{0,2,1:T(8,128)S(1)}, f32[24,8,8]{0,2,1:T(8,128)}, u32[]{:S(2)}) copy-start(f32[24,8,8]{0,2,1:T(8,128)} %param.16) | copy-start | bytes 18436
  49.1 28.0 %copy-start.6 = (s32[32]{0:T(128)}, s32[32]{0:T(128)S(1)}, u32[]{:S(2)}) copy-start(s32[32]{0:T(128)S(1)} %compare_select_fusion.5) | copy-start | bytes 388
  50.0 28.4 %collective-permute-start.2 = (f32[24,32]{0,1:T(8,128)}, f32[24,32]{0,1:T(8,128)S(1)}, u32[]{:S(2)}, u32[]{:S(2)}) collective-permute-start(f32[24,32]{0,1:T(8,128)} %get-tuple-element.25), channel_id=1, source_target_pairs={{0,756},{6,762},{12,0},{18,6},{24,12},{30,18},{36,24},{42,30},{48,... | collective-permute-start | bytes 9224 | tf_op jit(solution)/shard_map/ppermute | solution.py:26
  62.9 15.6 %collective-permute-start.3 = (f32[24,32]{0,1:T(8,128)}, f32[24,32]{0,1:T(8,128)S(1)}, u32[]{:S(2)}, u32[]{:S(2)}) collective-permute-start(f32[24,32]{0,1:T(8,128)} %get-tuple-element.28), channel_id=1, source_target_pairs={{0,762},{6,0},{12,6},{18,12},{24,18},{30,24},{36,30},{42,36},{48,4... | collective-permute-start | bytes 9224 | tf_op jit(solution)/shard_map/ppermute | solution.py:26
  66.1 12.3 %collective-permute-start.4 = (f32[24,32]{0,1:T(8,128)}, f32[24,32]{0,1:T(8,128)S(1)}, u32[]{:S(2)}, u32[]{:S(2)}) collective-permute-start(f32[24,32]{0,1:T(8,128)} %get-tuple-element.27), channel_id=1, source_target_pairs={{0,6},{6,12},{12,18},{18,24},{24,30},{30,36},{36,42},{42,48},{48,5... | collective-permute-start | bytes 9224 | tf_op jit(solution)/shard_map/ppermute | solution.py:26
  68.7 12.8 %collective-permute-start.5 = (f32[24,32]{0,1:T(8,128)S(1)}, f32[24,32]{0,1:T(8,128)}, u32[]{:S(2)}, u32[]{:S(2)}) collective-permute-start(f32[24,32]{0,1:T(8,128)S(1)} %get-tuple-element.26), channel_id=1, source_target_pairs={{0,12},{6,18},{12,24},{18,30},{24,36},{30,42},{36,48},{42,54},{48,... | collective-permute-start | bytes 9224 | tf_op jit(solution)/shard_map/ppermute | solution.py:26
  71.5 38.0 %collective-permute-start.1 = (f32[4,2,64,128]{3,2,1,0:T(8,128)}, f32[4,2,64,128]{3,2,1,0:T(8,128)S(1)}, u32[]{:S(2)}, u32[]{:S(2)}) collective-permute-start(f32[4,2,64,128]{3,2,1,0:T(8,128)} %get-tuple-element.22), channel_id=1, source_target_pairs={{0,6},{6,12},{12,18},{18,24},{24,30},{30,36},{36,42},{42,48},{48,5... | collective-permute-start | bytes 786440 | tf_op jit(solution)/shard_map/ppermute | solution.py:15
  83.7 18.7 %collective-permute-start.6 = (f32[24,32]{0,1:T(8,128)S(1)}, f32[24,32]{0,1:T(8,128)S(1)}, u32[]{:S(2)}, u32[]{:S(2)}) collective-permute-start(f32[24,32]{0,1:T(8,128)S(1)} %bitcast.41), channel_id=1, source_target_pairs={{0,12},{6,18},{12,24},{18,30},{24,36},{30,42},{36,48},{42,54},{48,... | collective-permute-start | bytes 9224 | tf_op jit(solution)/shard_map/ppermute | solution.py:26
  85.6 19.9 %collective-permute-start.7 = (f32[24,32]{0,1:T(8,128)S(1)}, f32[24,32]{0,1:T(8,128)S(1)}, u32[]{:S(2)}, u32[]{:S(2)}) collective-permute-start(f32[24,32]{0,1:T(8,128)S(1)} %bitcast.42), channel_id=1, source_target_pairs={{0,6},{6,12},{12,18},{18,24},{24,30},{30,36},{36,42},{42,48},{48,5... | collective-permute-start | bytes 9224 | tf_op jit(solution)/shard_map/ppermute | solution.py:26
  87.5 18.0 %collective-permute-start.8 = (f32[24,32]{0,1:T(8,128)S(1)}, f32[24,32]{0,1:T(8,128)S(1)}, u32[]{:S(2)}, u32[]{:S(2)}) collective-permute-start(f32[24,32]{0,1:T(8,128)S(1)} %bitcast.43), channel_id=1, source_target_pairs={{0,762},{6,0},{12,6},{18,12},{24,18},{30,24},{36,30},{42,36},{48,4... | collective-permute-start | bytes 9224 | tf_op jit(solution)/shard_map/ppermute | solution.py:26
  91.5 14.1 %collective-permute-start.9 = (f32[24,32]{0,1:T(8,128)S(1)}, f32[24,32]{0,1:T(8,128)S(1)}, u32[]{:S(2)}, u32[]{:S(2)}) collective-permute-start(f32[24,32]{0,1:T(8,128)S(1)} %bitcast.44), channel_id=1, source_target_pairs={{0,756},{6,762},{12,0},{18,6},{24,12},{30,18},{36,24},{42,30},{48,... | collective-permute-start | bytes 9224 | tf_op jit(solution)/shard_map/ppermute | solution.py:26
  102.4 8.6 %collective-permute-start = (f32[4,2,64,128]{3,2,1,0:T(8,128)}, f32[4,2,64,128]{3,2,1,0:T(8,128)}, u32[]{:S(2)}, u32[]{:S(2)}) collective-permute-start(f32[4,2,64,128]{3,2,1,0:T(8,128)} %get-tuple-element.21), channel_id=1, source_target_pairs={{6,0},{12,6},{18,12},{24,18},{30,24},{36,30},{42,36},{48,42},{54,4... | collective-permute-start | bytes 786440 | tf_op jit(solution)/shard_map/ppermute | solution.py:18
where the time goes:
time: 187 us; the launch traced here: 186 us
  local copies, waits for them, and re-layouts  77.7 us (42%)
  other arithmetic  56.1 us (30%)
  starting transfers between devices  44.3 us (24%)
  waiting for transfers between devices  4.31 us (2%)
  matrix products  2.96 us (2%)
    scatter-add x1, other arithmetic, per_device(): result = local.reshape(bands, -1).at[:, flat_index].add(back)  51.3 us
    ppermute x8, starting transfers between devices, shifted(): return lax.ppermute(value, axis, pairs)  39.2 us
    gather x2, local copies, waits for them, and re-layouts, per_device(): jnp.take(center.reshape(bands, -1), flat_index, axis=1)  36.3 us
    unnamed x20, local copies, waits for them, and re-layouts  10.9 us
    reshape x1, local copies, waits for them, and re-layouts, per_device(): return result.reshape(wave.shape)  10.7 us
    add x1, local copies, waits for them, and re-layouts, per_device(): -0.5 * laplace_all  8.67 us
  transfers between devices with their start and end apart: 10, of which 2 were waited for; matrix products, arithmetic and copies ran while one was open for 7% of the time, Pallas kernels for 0%

commit v1 on v0

v1 whole, which is shorter than its diff:
```python
import functools

import jax
import jax.numpy as jnp
from jax import lax
from jax.experimental import pallas as pl
from jax.experimental.pallas import tpu as pltpu
from jax.sharding import PartitionSpec as P

HIGH = lax.Precision.HIGHEST
F32 = jnp.float32
BF16 = jnp.bfloat16
VMEM = pl.BlockSpec(memory_space=pltpu.VMEM)
SMEM = pl.BlockSpec(memory_space=pltpu.SMEM)
LANES = 128


def bf(x):
    return x.astype(F32).astype(BF16)


def gather_kernel(
    reach, n_dom, atoms_dev, me_ref, slot_ref, rank_ref, idx_ref, val_ref, wave_ref, out_ref, pos_ref, col_ref
):
    slots, points = idx_ref.shape
    nproj = val_ref.shape[1]
    bands, rows, _ = wave_ref.shape
    atoms_all = rank_ref.shape[0]
    kinds = bands * nproj
    halves = [slice(j, j + LANES) for j in range(0, points, LANES)]
    lane = lax.broadcasted_iota(jnp.int32, (kinds, LANES), 1)
    lane_row = lax.broadcasted_iota(jnp.int32, (8, LANES), 1)
    out_ref[...] = jnp.zeros_like(out_ref)
    me = me_ref[0]

    def body(s, carry):
        atom = slot_ref[s]
        live = atom < atoms_all
        pos = rank_ref[jnp.minimum(atom, atoms_all - 1)]
        owner = pos // atoms_dev
        off = owner - me + reach
        off = jnp.where(off < 0, off + n_dom, off)
        off = jnp.where(off >= n_dom, off - n_dom, off)
        column = jnp.where(live, off * atoms_dev + pos - owner * atoms_dev, -1).astype(F32)
        place = jnp.where(live, pos + 1, 0).astype(F32)
        pos_ref[pl.ds(s, 1), :] = jnp.full((1, LANES), place, F32)
        col_ref[pl.ds(s, 1), :] = jnp.full((1, LANES), column, F32)
        out_ref[kinds:, :] = jnp.where(lane_row == s, place, out_ref[kinds:, :])
        idx = jnp.broadcast_to(idx_ref[pl.ds(s, 1), :], (8, points))
        hb = idx >> 10
        hs = (idx >> 7) & 7
        lo = idx & 127
        accs = [[None] * len(halves) for _ in range(bands)]
        for k in range(rows // 8):
            hit = [hb[:, h] == k for h in halves]
            for n in range(bands):
                tbl = wave_ref[n, 8 * k : 8 * k + 8, :]
                for j, h in enumerate(halves):
                    g = jnp.take_along_axis(tbl, lo[:, h], axis=1, mode="promise_in_bounds")
                    accs[n][j] = g if k == 0 else jnp.where(hit[j], g, accs[n][j])
        cols = []
        for n in range(bands):
            total = None
            for j, h in enumerate(halves):
                pick = jnp.take_along_axis(accs[n][j], hs[:, h], axis=0, mode="promise_in_bounds")
                prod = pick * val_ref[s, :, h]
                total = prod if total is None else total + prod
            cols.append(jnp.sum(total, axis=1, keepdims=True))
        col = jnp.concatenate(cols, axis=0)
        out_ref[:kinds, :] = jnp.where(lane == s, col, out_ref[:kinds, :])
        return carry

    lax.fori_loop(0, slots, body, 0)


def local_kernel(energy_ref, wave_ref, low_ref, high_ref, pot_ref, out_ref):
    bands, planes, ny, nz = wave_ref.shape
    for n in range(bands):
        def plane(x):
            if x < 0:
                return low_ref[n, 2 + x]
            if x >= planes:
                return high_ref[n, x - planes]
            return wave_ref[n, x]

        for x in range(planes):
            f = wave_ref[n, x]
            near = plane(x - 1) + plane(x + 1)
            far = plane(x - 2) + plane(x + 2)
            near += pltpu.roll(f, 1, 0) + pltpu.roll(f, ny - 1, 0)
            near += pltpu.roll(f, 1, 1) + pltpu.roll(f, nz - 1, 1)
            far += pltpu.roll(f, 2, 0) + pltpu.roll(f, ny - 2, 0)
            far += pltpu.roll(f, 2, 1) + pltpu.roll(f, nz - 2, 1)
            scale = pot_ref[x] + (3.75 - energy_ref[n])
            out_ref[n, x] = scale * f - (2.0 / 3.0) * near + (1.0 / 24.0) * far


def scatter_kernel(
    chunk, energy_ref, own_ref, below_ref, above_ref, pos_ref, col_ref, dq_ref,
    idx_ref, val_ref, loc_ref, out_ref, a_ref, b_ref, acc_ref, w_ref
):
    slots, points = idx_ref.shape
    nproj = val_ref.shape[1]
    bands, rows, _ = loc_ref.shape
    kinds = bands * nproj
    total = None
    for ref in (own_ref, below_ref, above_ref):
        same = jnp.where(pos_ref[...] == ref[kinds : kinds + 1, :], 1.0, 0.0).astype(F32)
        part = lax.dot_general(
            ref[:kinds, :], same, (((1,), (1,)), ((), ())), precision=HIGH, preferred_element_type=F32
        )
        total = part if total is None else total + part
    window = dq_ref.shape[0]
    place = lax.broadcasted_iota(jnp.int32, (slots, LANES), 1).astype(F32)
    mine = jnp.where(col_ref[...] == place, 1.0, 0.0).astype(F32)[:, :window]
    picked = jnp.dot(mine, dq_ref[...], precision=HIGH, preferred_element_type=F32)
    matrices = picked.T
    square = nproj * nproj
    for n in range(bands):
        energy = energy_ref[n]
        mine_n = total[nproj * n : nproj * n + nproj]
        for i in range(nproj):
            at = nproj * i
            mixed = matrices[at : at + nproj] - energy * matrices[square + at : square + at + nproj]
            w_ref[nproj * n + i : nproj * n + i + 1, 0:slots] = jnp.sum(mixed * mine_n, axis=0, keepdims=True)

    lane = lax.broadcasted_iota(jnp.int32, (kinds, slots), 1)
    sub_lo = bf(lax.broadcasted_iota(jnp.int32, (LANES, points), 0))
    sub_hi = bf(lax.broadcasted_iota(jnp.int32, (rows, points), 0))
    zero = jnp.zeros((), BF16)
    one = jnp.ones((), BF16)
    piece = bands * LANES

    def build(s, base):
        idx = idx_ref[pl.ds(s, 1), :]
        lo = bf(idx & 127)
        hi = bf(idx >> 7)
        a_ref[:, base : base + points] = jnp.where(sub_hi == hi, one, zero)
        col = jnp.sum(jnp.where(lane == s, w_ref[:, 0:slots], 0.0), axis=1, keepdims=True)
        v = val_ref[s]
        hit = sub_lo == lo
        for n in range(bands):
            back = jnp.sum(col[nproj * n : nproj * n + nproj] * v, axis=0, keepdims=True)
            big = back.astype(BF16)
            small = (back - big.astype(F32)).astype(BF16)
            at = LANES * n
            b_ref[at : at + LANES, base : base + points] = jnp.where(hit, big, zero)
            b_ref[piece + at : piece + at + LANES, base : base + points] = jnp.where(hit, small, zero)

    acc_ref[...] = jnp.zeros_like(acc_ref)

    def body(c, carry):
        for j in range(chunk):
            build(c * chunk + j, points * j)
        acc_ref[...] += lax.dot_general(
            b_ref[...], a_ref[...], (((1,), (1,)), ((), ())), preferred_element_type=F32
        )
        return carry

    lax.fori_loop(0, slots // chunk, body, 0)
    for n in range(bands):
        at = LANES * n
        added = acc_ref[at : at + LANES] + acc_ref[piece + at : piece + at + LANES]
        out_ref[n] = loc_ref[n] + added.T


def shifted(value, axis, steps):
    count = lax.axis_size(axis)
    return lax.ppermute(value, axis, [(s, (s + steps) % count) for s in range(count)])


def per_device(
    wave, potential, energies, proj_index, proj_values, slot_atom, atom_rank, d_matrix, q_matrix
):
    bands, planes, ny, nz = wave.shape
    slots, points = proj_index.shape
    nproj = proj_values.shape[1]
    atoms_dev = d_matrix.shape[0]
    kinds = bands * nproj
    rows = planes * ny
    n_dom = lax.axis_size("dom")
    me = lax.axis_index("dom").astype(jnp.int32).reshape(1)
    reach = 2

    matrices = jnp.concatenate(
        [d_matrix.reshape(atoms_dev, -1), q_matrix.reshape(atoms_dev, -1)], axis=1
    )
    edge = bands * 2 * ny

    def halo(part):
        return jnp.concatenate([part.reshape(edge, nz), matrices], axis=0)

    from_low = shifted(halo(wave[:, planes - 2 :]), "dom", 1)
    from_high = shifted(halo(wave[:, :2]), "dom", -1)
    low = from_low[:edge].reshape(bands, 2, ny, nz)
    high = from_high[:edge].reshape(bands, 2, ny, nz)
    dq_low, dq_high = from_low[edge:], from_high[edge:]

    flat = wave.reshape(bands, rows, nz)
    mine, pos, col = pl.pallas_call(
        functools.partial(gather_kernel, reach, n_dom, atoms_dev),
        out_shape=(
            jax.ShapeDtypeStruct((kinds + 8, LANES), F32),
            jax.ShapeDtypeStruct((slots, LANES), F32),
            jax.ShapeDtypeStruct((slots, LANES), F32),
        ),
        in_specs=[SMEM, SMEM, SMEM, VMEM, VMEM, VMEM],
        out_specs=(VMEM, VMEM, VMEM),
        name="gather",
    )(me, slot_atom, atom_rank, proj_index, proj_values, flat)

    local = pl.pallas_call(
        local_kernel,
        out_shape=jax.ShapeDtypeStruct(wave.shape, F32),
        in_specs=[SMEM, VMEM, VMEM, VMEM, VMEM],
        out_specs=VMEM,
        name="local",
    )(energies, wave, low, high, potential)

    height = kinds + 8
    got_low = shifted(jnp.concatenate([mine, dq_low], axis=0), "dom", 1)
    got_high = shifted(jnp.concatenate([mine, dq_high], axis=0), "dom", -1)
    window = jnp.concatenate([got_low[height:], dq_low, matrices, dq_high, got_high[height:]], axis=0)
    triple = jnp.concatenate(
        [mine[:, :slots], got_low[:height, :slots], got_high[:height, :slots], jnp.zeros((height, LANES - 3 * slots), F32)],
        axis=1,
    )
    below = shifted(triple, "dom", 3)
    above = shifted(triple, "dom", -3)

    chunk = 4
    result = pl.pallas_call(
        functools.partial(scatter_kernel, chunk),
        out_shape=jax.ShapeDtypeStruct((bands, rows, nz), F32),
        in_specs=[SMEM] + [VMEM] * 9,
        out_specs=VMEM,
        scratch_shapes=[
            pltpu.VMEM((rows, points * chunk), BF16),
            pltpu.VMEM((2 * bands * LANES, points * chunk), BF16),
            pltpu.VMEM((2 * bands * LANES, rows), F32),
            pltpu.VMEM((kinds, LANES), F32),
        ],
        name="scatter",
    )(energies, triple, below, above, pos, col, window, proj_index, proj_values, local.reshape(bands, rows, nz))
    return result.reshape(wave.shape)


def solution(mesh):
    placed = (
        P("band", "dom", None, None),
        P("dom", None, None),
        P("band"),
        P("dom", None),
        P("dom", None, None),
        P("dom"),
        P(),
        P("dom", None, None),
        P("dom", None, None),
    )
    return jax.shard_map(
        per_device,
        mesh=mesh,
        in_specs=placed,
        out_specs=P("band", "dom", None, None),
        check_vma=False,
    )
```

time: 187 us -> 92.7 us (0.50)
  the two profiles are of different devices: /device:TPU:8 before, /device:TPU:16 now
where the time goes in v1:
time: 92.7 us; the launch traced here: 92.2 us
  starting transfers between devices  38.7 us (42%)
  Pallas kernels  29.1 us (31%)
  waiting for transfers between devices  19.1 us (21%)
  local copies, waits for them, and re-layouts  4.85 us (5%)
    ppermute x6, starting transfers between devices, shifted(): lax.ppermute(value, axis, [(s, (s + steps) % count) for s in range(count)])  38.7 us
    ppermute x6, waiting for transfers between devices, shifted(): lax.ppermute(value, axis, [(s, (s + steps) % count) for s in range(count)])  19.1 us
    pallas_call x1, Pallas kernels, per_device(): pl.pallas_call(functools.partial(gather_kernel, reach, n_dom, atoms_dev),...  17.6 us
    pallas_call x1, Pallas kernels, per_device(): pl.pallas_call(functools.partial(scatter_kernel, chunk), out_shape=jax.Sh...  8.9 us
    pallas_call x1, Pallas kernels, per_device(): pl.pallas_call(local_kernel, out_shape=jax.ShapeDtypeStruct(wave.shape, F...  2.63 us
  transfers between devices with their start and end apart: 6, of which 2 were waited for; matrix products, arithmetic and copies ran while one was open for 2% of the time, Pallas kernels for 22%

profile of v1, /device:TPU:16, one launch (start us, length us, event | category | flops | bytes accessed | tf_op | source)
XLA Modules:
  0.0 92.2 jit_solution(10238740949218424738)
XLA Ops:
  0.0 0.8 copy.12
  0.8 0.1 copy.13
  0.9 1.1 %fusion.2 = (f32[4,2,64,128]{3,2,1,0:T(8,128)S(1)}, f32[4,2,64,128]{3,2,1,0:T(8,128)S(1)}) fusion(f32[4,4,64,128]{3,2,1,0:T(8,128)} %wave_ref.1), kind=kLoop, calls=%fused_computation.11 | loop fusion | bytes 1048576 | tf_op jit(solution)/shard_map/slice | solution.py:193
  2.0 0.1 fusion.1
  2.1 3.5 %collective-permute-start = (f32[536,128]{1,0:T(8,128)S(1)}, f32[536,128]{1,0:T(8,128)S(1)}, u32[]{:S(2)}, u32[]{:S(2)}) collective-permute-start(f32[536,128]{1,0:T(8,128)S(1)} %get-tuple-element.15), channel_id=1, source_target_pairs={{0,6},{6,12},{12,18},{18,24},{24,30},{30,36},{36,42},{42,48},{48,5... | collective-permute-start | bytes 823304 | tf_op jit(solution)/shard_map/ppermute | solution.py:169
  5.6 17.6 %gather.1 = (f32[40,128]{1,0:T(8,128)}, f32[32,128]{1,0:T(8,128)}, f32[32,128]{1,0:T(8,128)}) custom-call(s32[1]{0:T(128)} %bitcast.me_ref, s32[32]{0:T(128)} %slot_ref.1, s32[3072]{0:T(1024)} %rank_ref.1, s32[32,256]{1,0:T(8,128)} %idx_ref.3, f32[32,8,256]{2,1,0:T(8,128)} %val_ref.3, f32[4,256,128]{2,1,0:T(8,128)} %bitcast.11), custom_call_target="tpu_custom_call" | custom-call | tf_op jit(solution)/shard_map/gather/pallas_call | solution.py:200
  23.1 0.0 collective-permute-done
  23.1 0.7 copy-done
  23.9 4.7 %collective-permute-start.1 = (f32[64,128]{1,0:T(8,128)S(1)}, f32[64,128]{1,0:T(8,128)S(1)}, u32[]{:S(2)}, u32[]{:S(2)}) collective-permute-start(f32[64,128]{1,0:T(8,128)S(1)} %pad_maximum_fusion.2), channel_id=1, source_target_pairs={{0,6},{6,12},{12,18},{18,24},{24,30},{30,36},{36,42},{42,48},{48,5... | collective-permute-start | bytes 98312 | tf_op jit(solution)/shard_map/ppermute | solution.py:169
  28.5 1.9 %collective-permute-start.2 = (f32[536,128]{1,0:T(8,128)S(1)}, f32[536,128]{1,0:T(8,128)S(1)}, u32[]{:S(2)}, u32[]{:S(2)}) collective-permute-start(f32[536,128]{1,0:T(8,128)S(1)} %get-tuple-element.16), channel_id=1, source_target_pairs={{0,762},{6,0},{12,6},{18,12},{24,18},{30,24},{36,30},{42,36},{48,4... | collective-permute-start | bytes 823304 | tf_op jit(solution)/shard_map/ppermute | solution.py:169
  30.5 0.1 maximum_dynamic-update-slice_fusion
  30.6 7.6 %collective-permute-done.2 = f32[536,128]{1,0:T(8,128)S(1)} collective-permute-done((f32[536,128]{1,0:T(8,128)S(1)}, f32[536,128]{1,0:T(8,128)S(1)}, u32[]{:S(2)}, u32[]{:S(2)}) %collective-permute-start.2) | collective-permute-done | bytes 274464 | tf_op jit(solution)/shard_map/ppermute | solution.py:169
  38.2 3.7 %collective-permute-start.3 = (f32[64,128]{1,0:T(8,128)S(1)}, f32[64,128]{1,0:T(8,128)S(1)}, u32[]{:S(2)}, u32[]{:S(2)}) collective-permute-start(f32[64,128]{1,0:T(8,128)S(1)} %pad_maximum_fusion.1), channel_id=1, source_target_pairs={{0,762},{6,0},{12,6},{18,12},{24,18},{30,24},{36,30},{42,36},{48,4... | collective-permute-start | bytes 98312 | tf_op jit(solution)/shard_map/ppermute | solution.py:169
  41.9 0.1 pad.5.clone
  42.0 0.7 slice.50
  42.7 0.7 slice.51
  43.5 2.6 %local.1 = f32[4,4,64,128]{3,2,1,0:T(8,128)} custom-call(f32[4]{0:T(128)} %energy_ref.3, f32[4,4,64,128]{3,2,1,0:T(8,128)} %wave_ref.1, f32[4,2,64,128]{3,2,1,0:T(8,128)} %bitcast.13, f32[4,2,64,128]{3,2,1,0:T(8,128)} %bitcast.14, f32[4,64,128]{2,1,0:T(8,128)} %pot_ref.1), custom_call_target="tpu_custom_call" | custom-call | tf_op jit(solution)/shard_map/local/pallas_call | solution.py:212
  46.1 0.0 collective-permute-done.3
  46.1 0.1 maximum_maximum_fusion.own_ref
  46.2 23.0 %collective-permute-start.5 = (f32[40,128]{1,0:T(8,128)S(1)}, f32[40,128]{1,0:T(8,128)S(1)}, u32[]{:S(2)}, u32[]{:S(2)}) collective-permute-start(f32[40,128]{1,0:T(8,128)S(1)} %maximum_maximum_fusion.own_ref), channel_id=1, source_target_pairs={{0,750},{6,756},{12,762},{18,0},{24,6},{30,12},{36,18},{42,24},{48... | collective-permute-start | bytes 61448 | tf_op jit(solution)/shard_map/ppermute | solution.py:169
  69.2 1.9 %collective-permute-start.4 = (f32[40,128]{1,0:T(8,128)S(1)}, f32[40,128]{1,0:T(8,128)S(1)}, u32[]{:S(2)}, u32[]{:S(2)}) collective-permute-start(f32[40,128]{1,0:T(8,128)S(1)} %maximum_maximum_fusion.own_ref), channel_id=1, source_target_pairs={{0,18},{6,24},{12,30},{18,36},{24,42},{30,48},{36,54},{42,60},{48,... | collective-permute-start | bytes 61448 | tf_op jit(solution)/shard_map/ppermute | solution.py:169
  71.2 11.5 %collective-permute-done.4.below_ref = f32[40,128]{1,0:T(8,128)S(1)} collective-permute-done((f32[40,128]{1,0:T(8,128)S(1)}, f32[40,128]{1,0:T(8,128)S(1)}, u32[]{:S(2)}, u32[]{:S(2)}) %collective-permute-start.4) | collective-permute-done | bytes 20512 | tf_op jit(solution)/shard_map/ppermute | solution.py:169
  82.7 0.6 copy-done.5
  83.3 8.9 %scatter.1 = f32[4,256,128]{2,1,0:T(8,128)} custom-call(f32[4]{0:T(128)} %energy_ref.3, f32[40,128]{1,0:T(8,128)} %copy-done.2, f32[40,128]{1,0:T(8,128)} %copy-done.5, f32[40,128]{1,0:T(8,128)} %copy-done.4, f32[32,128]{1,0:T(8,128)} %get-tuple-element.9.pos_ref, f32[32,128]{1,0:T(8,128)} %get-tuple-element.10.col_ref, f32[120,128]{1,0:T(8,128)} %copy-done.1, ...), custom_call_target="tpu_custom_call" | custom-call | tf_op jit(solution)/shard_map/scatter/pallas_call | solution.py:232
  (22 shorter events, 0.1 us)
Async XLA Ops:
  0.0 0.8 copy-start.3
  2.1 21.0 %collective-permute-start = (f32[536,128]{1,0:T(8,128)S(1)}, f32[536,128]{1,0:T(8,128)S(1)}, u32[]{:S(2)}, u32[]{:S(2)}) collective-permute-start(f32[536,128]{1,0:T(8,128)S(1)} %get-tuple-element.15), channel_id=1, source_target_pairs={{0,6},{6,12},{12,18},{18,24},{24,30},{30,36},{36,42},{42,48},{48,5... | collective-permute-start | bytes 823304 | tf_op jit(solution)/shard_map/ppermute | solution.py:169
  23.1 0.7 copy-start
  23.9 6.6 %collective-permute-start.1 = (f32[64,128]{1,0:T(8,128)S(1)}, f32[64,128]{1,0:T(8,128)S(1)}, u32[]{:S(2)}, u32[]{:S(2)}) collective-permute-start(f32[64,128]{1,0:T(8,128)S(1)} %pad_maximum_fusion.2), channel_id=1, source_target_pairs={{0,6},{6,12},{12,18},{18,24},{24,30},{30,36},{36,42},{42,48},{48,5... | collective-permute-start | bytes 98312 | tf_op jit(solution)/shard_map/ppermute | solution.py:169
  28.5 9.6 %collective-permute-start.2 = (f32[536,128]{1,0:T(8,128)S(1)}, f32[536,128]{1,0:T(8,128)S(1)}, u32[]{:S(2)}, u32[]{:S(2)}) collective-permute-start(f32[536,128]{1,0:T(8,128)S(1)} %get-tuple-element.16), channel_id=1, source_target_pairs={{0,762},{6,0},{12,6},{18,12},{24,18},{30,24},{36,30},{42,36},{48,4... | collective-permute-start | bytes 823304 | tf_op jit(solution)/shard_map/ppermute | solution.py:169
  38.2 7.9 %collective-permute-start.3 = (f32[64,128]{1,0:T(8,128)S(1)}, f32[64,128]{1,0:T(8,128)S(1)}, u32[]{:S(2)}, u32[]{:S(2)}) collective-permute-start(f32[64,128]{1,0:T(8,128)S(1)} %pad_maximum_fusion.1), channel_id=1, source_target_pairs={{0,762},{6,0},{12,6},{18,12},{24,18},{30,24},{36,30},{42,36},{48,4... | collective-permute-start | bytes 98312 | tf_op jit(solution)/shard_map/ppermute | solution.py:169
  46.2 36.5 %copy-start.2 = (f32[40,128]{1,0:T(8,128)}, f32[40,128]{1,0:T(8,128)S(1)}, u32[]{:S(2)}) copy-start(f32[40,128]{1,0:T(8,128)S(1)} %maximum_maximum_fusion.own_ref) | copy-start | bytes 61444
  46.2 25.0 %collective-permute-start.5 = (f32[40,128]{1,0:T(8,128)S(1)}, f32[40,128]{1,0:T(8,128)S(1)}, u32[]{:S(2)}, u32[]{:S(2)}) collective-permute-start(f32[40,128]{1,0:T(8,128)S(1)} %maximum_maximum_fusion.own_ref), channel_id=1, source_target_pairs={{0,750},{6,756},{12,762},{18,0},{24,6},{30,12},{36,18},{42,24},{48... | collective-permute-start | bytes 61448 | tf_op jit(solution)/shard_map/ppermute | solution.py:169
  69.2 13.5 %collective-permute-start.4 = (f32[40,128]{1,0:T(8,128)S(1)}, f32[40,128]{1,0:T(8,128)S(1)}, u32[]{:S(2)}, u32[]{:S(2)}) collective-permute-start(f32[40,128]{1,0:T(8,128)S(1)} %maximum_maximum_fusion.own_ref), channel_id=1, source_target_pairs={{0,18},{6,24},{12,30},{18,36},{24,42},{30,48},{36,54},{42,60},{48,... | collective-permute-start | bytes 61448 | tf_op jit(solution)/shard_map/ppermute | solution.py:169
  71.2 11.6 %copy-start.1 = (f32[120,128]{1,0:T(8,128)}, f32[120,128]{1,0:T(8,128)S(1)}, u32[]{:S(2)}) copy-start(f32[120,128]{1,0:T(8,128)S(1)} %slice_dynamic-update-slice_fusion.dq_ref) | copy-start | bytes 184324
  71.2 11.5 %copy-start.4 = (f32[40,128]{1,0:T(8,128)}, f32[40,128]{1,0:T(8,128)S(1)}, u32[]{:S(2)}) copy-start(f32[40,128]{1,0:T(8,128)S(1)} %collective-permute-done.5.above_ref) | copy-start | bytes 61444
  82.7 0.6 copy-start.5

commit v2 on v1

v2 whole, which is shorter than its diff:
```python
import functools

import jax
import jax.numpy as jnp
from jax import lax
from jax.experimental import pallas as pl
from jax.experimental.pallas import tpu as pltpu
from jax.sharding import PartitionSpec as P

HIGH = lax.Precision.HIGHEST
F32 = jnp.float32
BF16 = jnp.bfloat16
VMEM = pl.BlockSpec(memory_space=pltpu.VMEM)
SMEM = pl.BlockSpec(memory_space=pltpu.SMEM)
LANES = 128
HALF = 4
RING = 8
MIB = 1 << 20


def bf(x):
    return x.astype(F32).astype(BF16)


def pack_kernel(me_ref, d_ref, q_ref, wave_ref, inner_ref, outer_ref, sems):
    bands = wave_ref.shape[0]
    edge = wave_ref.shape[1] // 2
    even = (me_ref[0] & 1) == 0
    copies = []
    for index, (ref, upper) in enumerate(((inner_ref, even), (outer_ref, jnp.logical_not(even)))):
        start = pl.multiple_of(jnp.where(upper, edge, 0), edge)
        for n in range(bands):
            copy = pltpu.make_async_copy(
                wave_ref.at[n, pl.ds(start, edge), :],
                ref.at[pl.ds(n * edge, edge), :],
                sems.at[index, n],
            )
            copy.start()
            copies.append(copy)
    atoms_dev = d_ref.shape[1]
    matrices = jnp.concatenate([d_ref[...], q_ref[...]], axis=0)
    matrices = jnp.concatenate(
        [matrices, jnp.zeros((matrices.shape[0], LANES - atoms_dev), F32)], axis=1
    ).T[:atoms_dev]
    for ref in (inner_ref, outer_ref):
        ref[bands * edge :, :] = matrices
    for copy in copies:
        copy.wait()


def gather_kernel(
    chunk, n_dom, atoms_dev, me_ref, slot_ref, rank_ref, idx_ref, val_ref, wave_ref,
    out_ref, pos_ref, col_ref, grid_ref, hot_ref
):
    slots, points = idx_ref.shape
    nproj = val_ref.shape[1]
    bands, rows, _ = wave_ref.shape
    atoms_all = rank_ref.shape[0]
    kinds = bands * nproj
    halves = [slice(j, j + LANES) for j in range(0, points, LANES)]
    me = me_ref[0]
    first = (me & (HALF - 1)) * slots
    sign = jnp.where((me & 1) == 0, 1, -1)
    lane = lax.broadcasted_iota(jnp.int32, (kinds, LANES), 1) - first
    lane_row = lax.broadcasted_iota(jnp.int32, (8, LANES), 1) - first
    out_ref[...] = jnp.zeros_like(out_ref)
    for n in range(bands):
        w = wave_ref[n].T
        big = w.astype(BF16)
        grid_ref[LANES * n : LANES * n + LANES, :rows] = big
        grid_ref[LANES * n : LANES * n + LANES, rows:] = (w - big.astype(F32)).astype(BF16)
    sub_hi = bf(lax.broadcasted_iota(jnp.int32, (rows, points), 0))

    def body(c, carry):
        for j in range(chunk):
            idx = idx_ref[pl.ds(c * chunk + j, 1), :]
            hot = jnp.where(sub_hi == bf(idx >> 7), jnp.ones((), BF16), jnp.zeros((), BF16))
            hot_ref[:rows, points * j : points * j + points] = hot
            hot_ref[rows:, points * j : points * j + points] = hot
        lines = jnp.dot(grid_ref[...], hot_ref[...], preferred_element_type=F32)
        for j in range(chunk):
            s = c * chunk + j
            atom = slot_ref[s]
            live = atom < atoms_all
            pos = rank_ref[jnp.minimum(atom, atoms_all - 1)]
            owner = pos // atoms_dev
            off = (owner - me + n_dom // 2) & (n_dom - 1)
            off = (off - n_dom // 2) * sign
            block = jnp.where(off > 0, 2 * off - 1, -2 * off)
            column = jnp.where(live, block * atoms_dev + pos - owner * atoms_dev, -1).astype(F32)
            place = jnp.where(live, pos + 1, 0).astype(F32)
            pos_ref[pl.ds(s, 1), :] = jnp.full((1, LANES), place, F32)
            col_ref[pl.ds(s, 1), :] = jnp.full((1, LANES), column, F32)
            out_ref[kinds:, :] = jnp.where(lane_row == s, place, out_ref[kinds:, :])
            idx = jnp.broadcast_to(idx_ref[pl.ds(s, 1), :], (8, points))
            tile = (idx >> 3) & 15
            sub = idx & 7
            cols = []
            for n in range(bands):
                at = LANES * n
                acc = lines[at : at + 8, points * j : points * j + points]
                for k in range(1, LANES // 8):
                    acc = jnp.where(
                        tile == k, lines[at + 8 * k : at + 8 * k + 8, points * j : points * j + points], acc
                    )
                total = None
                for h in halves:
                    pick = jnp.take_along_axis(acc[:, h], sub[:, h], axis=0, mode="promise_in_bounds")
                    prod = pick * val_ref[s, :, h]
                    total = prod if total is None else total + prod
                cols.append(jnp.sum(total, axis=1, keepdims=True))
            col = jnp.concatenate(cols, axis=0)
            out_ref[:kinds, :] = jnp.where(lane == s, col, out_ref[:kinds, :])
        return carry

    lax.fori_loop(0, slots // chunk, body, 0)


def local_kernel(me_ref, energy_ref, wave_ref, inner_ref, outer_ref, pot_ref, out_ref):
    bands, planes, ny, nz = wave_ref.shape
    even = (me_ref[0] & 1) == 0

    def side(lower, n, p):
        at = (n * 2 + p) * ny
        inner = inner_ref[at : at + ny, :]
        outer = outer_ref[at : at + ny, :]
        return jnp.where(even, outer, inner) if lower else jnp.where(even, inner, outer)

    for n in range(bands):
        padded = [side(True, n, 0), side(True, n, 1)]
        padded += [wave_ref[n, x] for x in range(planes)]
        padded += [side(False, n, 0), side(False, n, 1)]
        for x in range(planes):
            f = padded[x + 2]
            near = padded[x + 1] + padded[x + 3]
            far = padded[x] + padded[x + 4]
            near += pltpu.roll(f, 1, 0) + pltpu.roll(f, ny - 1, 0)
            near += pltpu.roll(f, 1, 1) + pltpu.roll(f, nz - 1, 1)
            far += pltpu.roll(f, 2, 0) + pltpu.roll(f, ny - 2, 0)
            far += pltpu.roll(f, 2, 1) + pltpu.roll(f, nz - 2, 1)
            scale = pot_ref[x] + (3.75 - energy_ref[n])
            out_ref[n, x] = scale * f - (2.0 / 3.0) * near + (1.0 / 24.0) * far


def scatter_kernel(
    chunk, energy_ref, own_ref, below_ref, above_ref, pos_ref, col_ref, dq_ref,
    idx_ref, val_ref, loc_ref, out_ref, a_ref, b_ref, acc_ref, w_ref
):
    slots, points = idx_ref.shape
    nproj = val_ref.shape[1]
    bands, rows, _ = loc_ref.shape
    kinds = bands * nproj
    total = None
    for ref in (own_ref, below_ref, above_ref):
        same = jnp.where(pos_ref[...] == ref[kinds : kinds + 1, :], 1.0, 0.0).astype(F32)
        part = lax.dot_general(
            ref[:kinds, :], same, (((1,), (1,)), ((), ())), precision=HIGH, preferred_element_type=F32
        )
        total = part if total is None else total + part
    window = dq_ref.shape[0]
    place = lax.broadcasted_iota(jnp.int32, (slots, LANES), 1).astype(F32)
    mine = jnp.where(col_ref[...] == place, 1.0, 0.0).astype(F32)[:, :window]
    picked = jnp.dot(mine, dq_ref[...], precision=HIGH, preferred_element_type=F32)
    matrices = picked.T
    square = nproj * nproj
    for n in range(bands):
        energy = energy_ref[n]
        mine_n = total[nproj * n : nproj * n + nproj]
        for i in range(nproj):
            at = nproj * i
            mixed = matrices[at : at + nproj] - energy * matrices[square + at : square + at + nproj]
            w_ref[nproj * n + i : nproj * n + i + 1, 0:slots] = jnp.sum(mixed * mine_n, axis=0, keepdims=True)

    lane = lax.broadcasted_iota(jnp.int32, (kinds, slots), 1)
    sub_lo = bf(lax.broadcasted_iota(jnp.int32, (LANES, points), 0))
    sub_hi = bf(lax.broadcasted_iota(jnp.int32, (rows, points), 0))
    zero = jnp.zeros((), BF16)
    one = jnp.ones((), BF16)
    piece = bands * LANES

    def build(s, base):
        idx = idx_ref[pl.ds(s, 1), :]
        lo = bf(idx & 127)
        hi = bf(idx >> 7)
        a_ref[:, base : base + points] = jnp.where(sub_hi == hi, one, zero)
        col = jnp.sum(jnp.where(lane == s, w_ref[:, 0:slots], 0.0), axis=1, keepdims=True)
        v = val_ref[s]
        hit = sub_lo == lo
        for n in range(bands):
            back = jnp.sum(col[nproj * n : nproj * n + nproj] * v, axis=0, keepdims=True)
            big = back.astype(BF16)
            small = (back - big.astype(F32)).astype(BF16)
            at = LANES * n
            b_ref[at : at + LANES, base : base + points] = jnp.where(hit, big, zero)
            b_ref[piece + at : piece + at + LANES, base : base + points] = jnp.where(hit, small, zero)

    acc_ref[...] = jnp.zeros_like(acc_ref)

    def body(c, carry):
        for j in range(chunk):
            build(c * chunk + j, points * j)
        acc_ref[...] += lax.dot_general(
            b_ref[...], a_ref[...], (((1,), (1,)), ((), ())), preferred_element_type=F32
        )
        return carry

    lax.fori_loop(0, slots // chunk, body, 0)
    for n in range(bands):
        at = LANES * n
        added = acc_ref[at : at + LANES] + acc_ref[piece + at : piece + at + LANES]
        out_ref[n] = loc_ref[n] + added.T


def swapped(value, partner):
    count = lax.axis_size("dom")
    return lax.ppermute(value, "dom", [(s, partner(s) % count) for s in range(count)])


def inner_of(d):
    return d ^ 1


def outer_of(d):
    return d + 1 if d % 2 else d - 1


def second_of(d):
    return d ^ 2


def across_of(d):
    base, y = d - d % RING, d % RING
    return base + (6, 7, 4, 5, 2, 3, 0, 1)[y]


def beyond_of(d):
    base, y = d - d % RING, d % RING
    if y < HALF:
        return base - RING + (6, 7, 4, 5)[y]
    return base + RING + (2, 3, 0, 1)[y - HALF]


def per_device(
    wave, potential, energies, proj_index, proj_values, slot_atom, atom_rank, d_matrix, q_matrix
):
    bands, planes, ny, nz = wave.shape
    slots, points = proj_index.shape
    nproj = proj_values.shape[1]
    atoms_dev = d_matrix.shape[0]
    kinds = bands * nproj
    rows = planes * ny
    n_dom = lax.axis_size("dom")
    spot = lax.axis_index("dom").astype(jnp.int32)
    me = spot.reshape(1)
    flat = wave.reshape(bands, rows, nz)
    edge = bands * 2 * ny
    height = kinds + 8

    def turned(m):
        return jnp.transpose(m, (1, 2, 0)).reshape(nproj * nproj, atoms_dev)

    inner, outer = pl.pallas_call(
        pack_kernel,
        out_shape=(jax.ShapeDtypeStruct((edge + atoms_dev, nz), F32),) * 2,
        in_specs=[SMEM, VMEM, VMEM, pl.BlockSpec(memory_space=pl.ANY)],
        out_specs=(VMEM, VMEM),
        scratch_shapes=[pltpu.SemaphoreType.DMA((2, bands))],
        compiler_params=pltpu.CompilerParams(vmem_limit_bytes=4 * MIB),
        name="pack",
    )(me, turned(d_matrix), turned(q_matrix), flat)
    matrices = inner[edge:]
    outer_got = swapped(outer, outer_of)
    inner_got = swapped(inner, inner_of)

    chunk = 8
    mine, pos, col = pl.pallas_call(
        functools.partial(gather_kernel, chunk, n_dom, atoms_dev),
        out_shape=(
            jax.ShapeDtypeStruct((height, LANES), F32),
            jax.ShapeDtypeStruct((slots, LANES), F32),
            jax.ShapeDtypeStruct((slots, LANES), F32),
        ),
        in_specs=[SMEM, SMEM, SMEM, VMEM, VMEM, VMEM],
        out_specs=(VMEM, VMEM, VMEM),
        scratch_shapes=[
            pltpu.VMEM((bands * LANES, 2 * rows), BF16),
            pltpu.VMEM((2 * rows, points * chunk), BF16),
        ],
        compiler_params=pltpu.CompilerParams(vmem_limit_bytes=24 * MIB),
        cost_estimate=pl.CostEstimate(flops=10**10, bytes_accessed=10**7, transcendentals=0),
        name="gather",
    )(me, slot_atom, atom_rank, proj_index, proj_values, flat)

    def message(a, dq):
        return jnp.concatenate([a, dq], axis=0)

    outer_dq = outer_got[edge:]
    first = swapped(message(mine, outer_dq), inner_of)
    pair = mine + first[:height]
    second = swapped(message(pair, matrices), second_of)
    half = message(pair + second[:height], matrices)
    beyond = swapped(half, beyond_of)
    across = swapped(half, across_of)

    local = pl.pallas_call(
        local_kernel,
        out_shape=jax.ShapeDtypeStruct(wave.shape, F32),
        in_specs=[SMEM, SMEM, VMEM, VMEM, VMEM, VMEM],
        out_specs=VMEM,
        compiler_params=pltpu.CompilerParams(vmem_limit_bytes=8 * MIB),
        cost_estimate=pl.CostEstimate(flops=10**8, bytes_accessed=5 * 10**6, transcendentals=0),
        name="local",
    )(me, energies, wave, inner_got, outer_got, potential)

    y = spot % RING
    ends = (y == 0) | (y == RING - 1)
    middle = (y == HALF - 1) | (y == HALF)
    last = jnp.where(ends, beyond[height:], jnp.where(middle, across[height:], second[height:]))
    window = jnp.concatenate([matrices, inner_got[edge:], outer_dq, first[height:], last], axis=0)

    chunk = 4
    result = pl.pallas_call(
        functools.partial(scatter_kernel, chunk),
        out_shape=jax.ShapeDtypeStruct((bands, rows, nz), F32),
        in_specs=[SMEM] + [VMEM] * 9,
        out_specs=VMEM,
        scratch_shapes=[
            pltpu.VMEM((rows, points * chunk), BF16),
            pltpu.VMEM((2 * bands * LANES, points * chunk), BF16),
            pltpu.VMEM((2 * bands * LANES, rows), F32),
            pltpu.VMEM((kinds, LANES), F32),
        ],
        compiler_params=pltpu.CompilerParams(vmem_limit_bytes=24 * MIB),
        name="scatter",
    )(energies, half, beyond, across, pos, col, window, proj_index, proj_values, local.reshape(bands, rows, nz))
    return result.reshape(wave.shape)


def solution(mesh):
    placed = (
        P("band", "dom", None, None),
        P("dom", None, None),
        P("band"),
        P("dom", None),
        P("dom", None, None),
        P("dom"),
        P(),
        P("dom", None, None),
        P("dom", None, None),
    )
    return jax.shard_map(
        per_device,
        mesh=mesh,
        in_specs=placed,
        out_specs=P("band", "dom", None, None),
        check_vma=False,
    )
```

time: 92.7 us -> 62.8 us (0.68)
  the two profiles are of different devices: /device:TPU:16 before, /device:TPU:8 now
where the time goes in v2:
time: 62.8 us; the launch traced here: 62.3 us
  starting transfers between devices  29.2 us (46%)
  Pallas kernels  16.8 us (27%)
  waiting for transfers between devices  11.8 us (19%)
  local copies, waits for them, and re-layouts  4.18 us (7%)
    ppermute x6, starting transfers between devices, swapped(): lax.ppermute(value, 'dom', [(s, partner(s) % count) for s in range(count)])  29.2 us
    ppermute x6, waiting for transfers between devices, swapped(): lax.ppermute(value, 'dom', [(s, partner(s) % count) for s in range(count)])  11.8 us
    pallas_call x1, Pallas kernels, per_device(): pl.pallas_call(functools.partial(scatter_kernel, chunk), out_shape=jax.Sh...  8.2 us
    pallas_call x1, Pallas kernels, per_device(): pl.pallas_call(functools.partial(gather_kernel, chunk, n_dom, atoms_dev),...  6.63 us
    unnamed x26, local copies, waits for them, and re-layouts  4.18 us
  transfers between devices with their start and end apart: 6, of which 3 were waited for; matrix products, arithmetic and copies ran while one was open for 0% of the time, Pallas kernels for 13%

profile of v2, /device:TPU:8, one launch (start us, length us, event | category | flops | bytes accessed | tf_op | source)
XLA Modules:
  0.0 62.3 jit_solution(16891967382515253433)
XLA Ops:
  0.0 1.0 %copy-done = f32[4,4,64,128]{3,2,1,0:T(8,128)S(1)} copy-done((f32[4,4,64,128]{3,2,1,0:T(8,128)S(1)}, f32[4,4,64,128]{3,2,1,0:T(8,128)}, u32[]{:S(2)}) %copy-start) | copy-done | bytes 524312
  1.0 0.8 %copy-done.6 = f32[24,8,8]{0,2,1:T(8,128)S(1)} copy-done((f32[24,8,8]{0,2,1:T(8,128)S(1)}, f32[24,8,8]{0,2,1:T(8,128)}, u32[]{:S(2)}) %copy-start.6) | copy-done | bytes 6168
  1.8 0.8 %copy-done.7 = f32[24,8,8]{0,2,1:T(8,128)S(1)} copy-done((f32[24,8,8]{0,2,1:T(8,128)S(1)}, f32[24,8,8]{0,2,1:T(8,128)}, u32[]{:S(2)}) %copy-start.7) | copy-done | bytes 6168
  2.6 0.8 %pack.1 = (f32[536,128]{1,0:T(8,128)S(1)}, f32[536,128]{1,0:T(8,128)S(1)}) custom-call(s32[1]{0:T(128)} %bitcast.me_ref, f32[64,24]{1,0:T(8,128)S(1)} %bitcast.13, f32[64,24]{1,0:T(8,128)S(1)} %bitcast.14, f32[4,256,128]{2,1,0:T(8,128)S(1)} %bitcast.10), custom_call_target="tpu_custom_call" | custom-call | tf_op jit(solution)/shard_map/pack/pallas_call | solution.py:262
  3.4 0.0 copy-start.10
  3.4 3.5 %collective-permute-start = (f32[536,128]{1,0:T(8,128)S(1)}, f32[536,128]{1,0:T(8,128)S(1)}, u32[]{:S(2)}, u32[]{:S(2)}) collective-permute-start(f32[536,128]{1,0:T(8,128)S(1)} %get-tuple-element.11), channel_id=1, source_target_pairs={{0,762},{6,12},{12,6},{18,24},{24,18},{30,36},{36,30},{42,48},{48,... | collective-permute-start | bytes 823304 | tf_op jit(solution)/shard_map/ppermute | solution.py:216
  6.9 11.9 %collective-permute-start.5 = (f32[536,128]{1,0:T(8,128)S(1)}, f32[536,128]{1,0:T(8,128)S(1)}, u32[]{:S(2)}, u32[]{:S(2)}) collective-permute-start(f32[536,128]{1,0:T(8,128)S(1)} %get-tuple-element.12), channel_id=1, source_target_pairs={{0,6},{6,0},{12,18},{18,12},{24,30},{30,24},{36,42},{42,36},{48,54... | collective-permute-start | bytes 823304 | tf_op jit(solution)/shard_map/ppermute | solution.py:216
  18.8 0.0 copy-start.2
  18.8 0.9 %copy-done.2 = f32[32,8,256]{2,1,0:T(8,128)S(1)} copy-done((f32[32,8,256]{2,1,0:T(8,128)S(1)}, f32[32,8,256]{2,1,0:T(8,128)}, u32[]{:S(2)}) %copy-start.2) | copy-done | bytes 262168
  19.8 6.6 %gather.1 = (f32[40,128]{1,0:T(8,128)S(1)}, f32[32,128]{1,0:T(8,128)S(1)}, f32[32,128]{1,0:T(8,128)S(1)}) custom-call(s32[1]{0:T(128)} %bitcast.me_ref, s32[32]{0:T(128)S(1)} %copy-done.10, s32[3072]{0:T(1024)S(1)} %copy-done.9, s32[32,256]{1,0:T(8,128)S(1)} %copy-done.5, f32[32,8,256]{2,1,0:T(8,128)S(1)} %copy-done.2, f32[4,256,128]{2,1,0:T(8,128)S(1)} %bitcast.11), custom_call_target="tpu_custom_call" | custom-call | flops 10000000000 | bytes 10000000 | tf_op jit(solution)/shard_map/gather/pallas_call | solution.py:276
  26.4 0.0 collective-permute-done.5.inner_ref
  26.4 0.0 copy-start.4
  26.5 2.7 %collective-permute-start.1 = (f32[64,128]{1,0:T(8,128)S(1)}, f32[64,128]{1,0:T(8,128)S(1)}, u32[]{:S(2)}, u32[]{:S(2)}) collective-permute-start(f32[64,128]{1,0:T(8,128)S(1)} %pad_maximum_fusion.2), channel_id=1, source_target_pairs={{0,6},{6,0},{12,18},{18,12},{24,30},{30,24},{36,42},{42,36},{48,54... | collective-permute-start | bytes 98312 | tf_op jit(solution)/shard_map/ppermute | solution.py:216
  29.2 3.2 %collective-permute-done.1 = f32[64,128]{1,0:T(8,128)S(1)} collective-permute-done((f32[64,128]{1,0:T(8,128)S(1)}, f32[64,128]{1,0:T(8,128)S(1)}, u32[]{:S(2)}, u32[]{:S(2)}) %collective-permute-start.1) | collective-permute-done | bytes 32800 | tf_op jit(solution)/shard_map/ppermute | solution.py:216
  32.4 1.9 %collective-permute-start.2 = (f32[64,128]{1,0:T(8,128)S(1)}, f32[64,128]{1,0:T(8,128)S(1)}, u32[]{:S(2)}, u32[]{:S(2)}) collective-permute-start(f32[64,128]{1,0:T(8,128)S(1)} %pad_maximum_fusion.1), channel_id=1, source_target_pairs={{0,12},{6,18},{12,0},{18,6},{24,36},{30,42},{36,24},{42,30},{48,60... | collective-permute-start | bytes 98312 | tf_op jit(solution)/shard_map/ppermute | solution.py:216
  34.4 0.0 copy-start.8
  34.4 0.6 %copy-done.8 = f32[4]{0:T(128)S(1)} copy-done((f32[4]{0:T(128)S(1)}, f32[4]{0:T(128)}, u32[]{:S(2)}) %copy-start.8) | copy-done | bytes 40
  35.0 1.2 %local.1 = f32[4,4,64,128]{3,2,1,0:T(8,128)S(1)} custom-call(s32[1]{0:T(128)} %bitcast.me_ref, f32[4]{0:T(128)S(1)} %copy-done.8, f32[4,4,64,128]{3,2,1,0:T(8,128)S(1)} %copy-done.1, f32[536,128]{1,0:T(8,128)S(1)} %collective-permute-done.5.inner_ref, f32[536,128]{1,0:T(8,128)S(1)} %collective-permute-done.outer_ref, f32[4,64,128]{2,1,0:T(8,128)S(1)} %copy-done.4), custom_call_target="tpu_custom_call" | custom-call | flops 100000000 | bytes 5000000 | tf_op jit(solution)/shard_map/local/pallas_call | solution.py:305
  36.2 2.9 %collective-permute-done.2 = f32[64,128]{1,0:T(8,128)S(1)} collective-permute-done((f32[64,128]{1,0:T(8,128)S(1)}, f32[64,128]{1,0:T(8,128)S(1)}, u32[]{:S(2)}, u32[]{:S(2)}) %collective-permute-start.2) | collective-permute-done | bytes 32800 | tf_op jit(solution)/shard_map/ppermute | solution.py:216
  39.1 1.9 %collective-permute-start.4 = (f32[64,128]{1,0:T(8,128)S(1)}, f32[64,128]{1,0:T(8,128)S(1)}, u32[]{:S(2)}, u32[]{:S(2)}) collective-permute-start(f32[64,128]{1,0:T(8,128)S(1)} %pad_maximum_fusion.own_ref), channel_id=1, source_target_pairs={{0,36},{6,42},{12,24},{18,30},{24,12},{30,18},{36,0},{42,6},{48,84... | collective-permute-start | bytes 98312 | tf_op jit(solution)/shard_map/ppermute | solution.py:216
  41.1 7.3 %collective-permute-start.3 = (f32[64,128]{1,0:T(8,128)S(1)}, f32[64,128]{1,0:T(8,128)S(1)}, u32[]{:S(2)}, u32[]{:S(2)}) collective-permute-start(f32[64,128]{1,0:T(8,128)S(1)} %pad_maximum_fusion.own_ref), channel_id=1, source_target_pairs={{0,756},{6,762},{12,744},{18,750},{24,60},{30,66},{36,48},{42,54},... | collective-permute-start | bytes 98312 | tf_op jit(solution)/shard_map/ppermute | solution.py:216
  48.4 0.0 collective-permute-done.4.above_ref
  48.4 5.6 %collective-permute-done.3.below_ref = f32[64,128]{1,0:T(8,128)S(1)} collective-permute-done((f32[64,128]{1,0:T(8,128)S(1)}, f32[64,128]{1,0:T(8,128)S(1)}, u32[]{:S(2)}, u32[]{:S(2)}) %collective-permute-start.3) | collective-permute-done | bytes 32800 | tf_op jit(solution)/shard_map/ppermute | solution.py:216
  54.1 8.2 %scatter.1 = f32[4,256,128]{2,1,0:T(8,128)} custom-call(f32[4]{0:T(128)S(1)} %copy-done.8, f32[64,128]{1,0:T(8,128)S(1)} %pad_maximum_fusion.own_ref, f32[64,128]{1,0:T(8,128)S(1)} %collective-permute-done.3.below_ref, f32[64,128]{1,0:T(8,128)S(1)} %collective-permute-done.4.above_ref, f32[32,128]{1,0:T(8,128)S(1)} %get-tuple-element.13.pos_ref, ...), custom_call_target="tpu_custom_call" | custom-call | tf_op jit(solution)/shard_map/scatter/pallas_call | solution.py:322
  (24 shorter events, 0.1 us)
Async XLA Ops:
  0.0 1.0 %copy-start = (f32[4,4,64,128]{3,2,1,0:T(8,128)S(1)}, f32[4,4,64,128]{3,2,1,0:T(8,128)}, u32[]{:S(2)}) copy-start(f32[4,4,64,128]{3,2,1,0:T(8,128)} %wave_ref.1) | copy-start | bytes 1572868
  1.0 0.8 %copy-start.6 = (f32[24,8,8]{0,2,1:T(8,128)S(1)}, f32[24,8,8]{0,2,1:T(8,128)}, u32[]{:S(2)}) copy-start(f32[24,8,8]{0,2,1:T(8,128)} %param.16) | copy-start | bytes 18436
  1.8 0.8 %copy-start.7 = (f32[24,8,8]{0,2,1:T(8,128)S(1)}, f32[24,8,8]{0,2,1:T(8,128)}, u32[]{:S(2)}) copy-start(f32[24,8,8]{0,2,1:T(8,128)} %param.17) | copy-start | bytes 18436
  2.6 16.2 %copy-start.1 = (f32[4,4,64,128]{3,2,1,0:T(8,128)S(1)}, f32[4,4,64,128]{3,2,1,0:T(8,128)}, u32[]{:S(2)}) copy-start(f32[4,4,64,128]{3,2,1,0:T(8,128)} %wave_ref.1) | copy-start | bytes 1572868
  2.6 16.2 %copy-start.5 = (s32[32,256]{1,0:T(8,128)S(1)}, s32[32,256]{1,0:T(8,128)}, u32[]{:S(2)}) copy-start(s32[32,256]{1,0:T(8,128)} %idx_ref.3) | copy-start | bytes 98308
  2.6 16.2 %copy-start.9 = (s32[3072]{0:T(1024)S(1)}, s32[3072]{0:T(1024)}, u32[]{:S(2)}) copy-start(s32[3072]{0:T(1024)} %rank_ref.1) | copy-start | bytes 36868
  3.4 15.4 %copy-start.10 = (s32[32]{0:T(128)S(1)}, s32[32]{0:T(128)}, u32[]{:S(2)}) copy-start(s32[32]{0:T(128)} %slot_ref.1) | copy-start | bytes 388
  3.4 23.0 %collective-permute-start = (f32[536,128]{1,0:T(8,128)S(1)}, f32[536,128]{1,0:T(8,128)S(1)}, u32[]{:S(2)}, u32[]{:S(2)}) collective-permute-start(f32[536,128]{1,0:T(8,128)S(1)} %get-tuple-element.11), channel_id=1, source_target_pairs={{0,762},{6,12},{12,6},{18,24},{24,18},{30,36},{36,30},{42,48},{48,... | collective-permute-start | bytes 823304 | tf_op jit(solution)/shard_map/ppermute | solution.py:216
  6.9 19.5 %collective-permute-start.5 = (f32[536,128]{1,0:T(8,128)S(1)}, f32[536,128]{1,0:T(8,128)S(1)}, u32[]{:S(2)}, u32[]{:S(2)}) collective-permute-start(f32[536,128]{1,0:T(8,128)S(1)} %get-tuple-element.12), channel_id=1, source_target_pairs={{0,6},{6,0},{12,18},{18,12},{24,30},{30,24},{36,42},{42,36},{48,54... | collective-permute-start | bytes 823304 | tf_op jit(solution)/shard_map/ppermute | solution.py:216
  18.8 1.0 %copy-start.2 = (f32[32,8,256]{2,1,0:T(8,128)S(1)}, f32[32,8,256]{2,1,0:T(8,128)}, u32[]{:S(2)}) copy-start(f32[32,8,256]{2,1,0:T(8,128)} %val_ref.3) | copy-start | bytes 786436
  26.4 8.0 %copy-start.4 = (f32[4,64,128]{2,1,0:T(8,128)S(1)}, f32[4,64,128]{2,1,0:T(8,128)}, u32[]{:S(2)}) copy-start(f32[4,64,128]{2,1,0:T(8,128)} %pot_ref.1) | copy-start | bytes 393220
  26.5 5.9 %collective-permute-start.1 = (f32[64,128]{1,0:T(8,128)S(1)}, f32[64,128]{1,0:T(8,128)S(1)}, u32[]{:S(2)}, u32[]{:S(2)}) collective-permute-start(f32[64,128]{1,0:T(8,128)S(1)} %pad_maximum_fusion.2), channel_id=1, source_target_pairs={{0,6},{6,0},{12,18},{18,12},{24,30},{30,24},{36,42},{42,36},{48,54... | collective-permute-start | bytes 98312 | tf_op jit(solution)/shard_map/ppermute | solution.py:216
  32.4 6.7 %collective-permute-start.2 = (f32[64,128]{1,0:T(8,128)S(1)}, f32[64,128]{1,0:T(8,128)S(1)}, u32[]{:S(2)}, u32[]{:S(2)}) collective-permute-start(f32[64,128]{1,0:T(8,128)S(1)} %pad_maximum_fusion.1), channel_id=1, source_target_pairs={{0,12},{6,18},{12,0},{18,6},{24,36},{30,42},{36,24},{42,30},{48,60... | collective-permute-start | bytes 98312 | tf_op jit(solution)/shard_map/ppermute | solution.py:216
  34.4 0.7 %copy-start.8 = (f32[4]{0:T(128)S(1)}, f32[4]{0:T(128)}, u32[]{:S(2)}) copy-start(f32[4]{0:T(128)} %energy_ref.3) | copy-start | bytes 52
  35.0 19.0 %copy-start.3 = (f32[32,8,256]{2,1,0:T(8,128)S(1)}, f32[32,8,256]{2,1,0:T(8,128)}, u32[]{:S(2)}) copy-start(f32[32,8,256]{2,1,0:T(8,128)} %val_ref.3) | copy-start | bytes 786436
  39.1 9.3 %collective-permute-start.4 = (f32[64,128]{1,0:T(8,128)S(1)}, f32[64,128]{1,0:T(8,128)S(1)}, u32[]{:S(2)}, u32[]{:S(2)}) collective-permute-start(f32[64,128]{1,0:T(8,128)S(1)} %pad_maximum_fusion.own_ref), channel_id=1, source_target_pairs={{0,36},{6,42},{12,24},{18,30},{24,12},{30,18},{36,0},{42,6},{48,84... | collective-permute-start | bytes 98312 | tf_op jit(solution)/shard_map/ppermute | solution.py:216
  41.1 13.0 %collective-permute-start.3 = (f32[64,128]{1,0:T(8,128)S(1)}, f32[64,128]{1,0:T(8,128)S(1)}, u32[]{:S(2)}, u32[]{:S(2)}) collective-permute-start(f32[64,128]{1,0:T(8,128)S(1)} %pad_maximum_fusion.own_ref), channel_id=1, source_target_pairs={{0,756},{6,762},{12,744},{18,750},{24,60},{30,66},{36,48},{42,54},... | collective-permute-start | bytes 98312 | tf_op jit(solution)/shard_map/ppermute | solution.py:216

commit v3 on v2

v3 whole, which is shorter than its diff:
```python
import functools

import jax
import jax.numpy as jnp
from jax import lax
from jax.experimental import pallas as pl
from jax.experimental.pallas import tpu as pltpu
from jax.sharding import PartitionSpec as P

HIGH = lax.Precision.HIGHEST
F32 = jnp.float32
BF16 = jnp.bfloat16
VMEM = pl.BlockSpec(memory_space=pltpu.VMEM)
HBM = pl.BlockSpec(memory_space=pltpu.HBM)
SMEM = pl.BlockSpec(memory_space=pltpu.SMEM)
LANES = 128
HALF = 4
RING = 8
MIB = 1 << 20


def kept(x):
    return pltpu.with_memory_space_constraint(x, pltpu.HBM)


def bf(x):
    return x.astype(F32).astype(BF16)


def pack_kernel(me_ref, wave_ref, after_ref, inner_ref, outer_ref, sems):
    bands = wave_ref.shape[0]
    edge = wave_ref.shape[1] // 2
    even = (me_ref[0] & 1) == 0
    copies = []
    for index, (ref, upper) in enumerate(((inner_ref, even), (outer_ref, jnp.logical_not(even)))):
        start = pl.multiple_of(jnp.where(upper, edge, 0), edge)
        for n in range(bands):
            copy = pltpu.make_async_copy(
                wave_ref.at[n, pl.ds(start, edge), :],
                ref.at[pl.ds(n * edge, edge), :],
                sems.at[index, n],
            )
            copy.start()
            copies.append(copy)
    for copy in copies:
        copy.wait()


def gather_kernel(
    chunk, me_ref, slot_ref, rank_ref, idx_hbm, val_hbm, wave_hbm, d_hbm, q_hbm,
    out_ref, pos_ref, col_ref,
    idx_ref, val_ref, wave_ref, d_ref, q_ref, grid_ref, hot_ref, sems
):
    slots, points = idx_ref.shape
    nproj = val_ref.shape[1]
    bands, rows, _ = wave_ref.shape
    atoms_all = rank_ref.shape[0]
    atoms_dev = d_ref.shape[1]
    kinds = bands * nproj
    height = kinds + 8
    copies = [pltpu.make_async_copy(idx_hbm, idx_ref, sems.at[0])]
    copies += [pltpu.make_async_copy(wave_hbm.at[n], wave_ref.at[n], sems.at[1 + n]) for n in range(bands)]
    copies.append(pltpu.make_async_copy(val_hbm, val_ref, sems.at[1 + bands]))
    copies.append(pltpu.make_async_copy(d_hbm, d_ref, sems.at[2 + bands]))
    copies.append(pltpu.make_async_copy(q_hbm, q_ref, sems.at[3 + bands]))
    for copy in copies:
        copy.start()
    halves = [slice(j, j + LANES) for j in range(0, points, LANES)]
    me = me_ref[0]
    first = (me & (HALF - 1)) * slots
    lane = lax.broadcasted_iota(jnp.int32, (kinds, LANES), 1) - first
    lane_row = lax.broadcasted_iota(jnp.int32, (8, LANES), 1) - first
    out_ref[:height, :] = jnp.zeros((height, LANES), F32)
    pos_ref[...] = jnp.zeros_like(pos_ref)
    col_ref[...] = jnp.full_like(col_ref, -1.0)
    sub_hi = bf(lax.broadcasted_iota(jnp.int32, (rows, points), 0))
    for n in range(bands):
        copies[1 + n].wait()
        w = wave_ref[n].T
        big = w.astype(BF16)
        grid_ref[LANES * n : LANES * n + LANES, :rows] = big
        grid_ref[LANES * n : LANES * n + LANES, rows:] = (w - big.astype(F32)).astype(BF16)
    copies[0].wait()
    for copy in copies[1 + bands :]:
        copy.wait()
    matrices = jnp.concatenate([d_ref[...], q_ref[...]], axis=0)
    matrices = jnp.concatenate(
        [matrices, jnp.zeros((matrices.shape[0], LANES - atoms_dev), F32)], axis=1
    )
    out_ref[height:, :] = matrices.T[:atoms_dev]

    def body(c, carry):
        @pl.when(slot_ref[c * chunk] < atoms_all)
        def _():
            for j in range(chunk):
                idx = idx_ref[pl.ds(c * chunk + j, 1), :]
                hot = jnp.where(sub_hi == bf(idx >> 7), jnp.ones((), BF16), jnp.zeros((), BF16))
                hot_ref[:rows, points * j : points * j + points] = hot
                hot_ref[rows:, points * j : points * j + points] = hot
            lines = jnp.dot(grid_ref[...], hot_ref[...], preferred_element_type=F32)
            for j in range(chunk):
                s = c * chunk + j
                atom = slot_ref[s]
                live = atom < atoms_all
                pos = rank_ref[jnp.minimum(atom, atoms_all - 1)]
                owner = pos // atoms_dev
                apart = owner ^ me
                block = jnp.where(apart < RING, HALF, HALF + 2) + (apart & 1)
                block = jnp.where(apart < HALF, apart, block)
                column = jnp.where(live, block * atoms_dev + pos - owner * atoms_dev, -1).astype(F32)
                place = jnp.where(live, pos + 1, 0).astype(F32)
                pos_ref[pl.ds(s, 1), :] = jnp.full((1, LANES), place, F32)
                col_ref[pl.ds(s, 1), :] = jnp.full((1, LANES), column, F32)
                out_ref[kinds:height, :] = jnp.where(lane_row == s, place, out_ref[kinds:height, :])
                idx = jnp.broadcast_to(idx_ref[pl.ds(s, 1), :], (8, points))
                tile = (idx >> 3) & 15
                sub = idx & 7
                cols = []
                for n in range(bands):
                    at = LANES * n
                    acc = lines[at : at + 8, points * j : points * j + points]
                    for k in range(1, LANES // 8):
                        acc = jnp.where(
                            tile == k, lines[at + 8 * k : at + 8 * k + 8, points * j : points * j + points], acc
                        )
                    total = None
                    for h in halves:
                        pick = jnp.take_along_axis(acc[:, h], sub[:, h], axis=0, mode="promise_in_bounds")
                        prod = pick * val_ref[s, :, h]
                        total = prod if total is None else total + prod
                    cols.append(jnp.sum(total, axis=1, keepdims=True))
                col = jnp.concatenate(cols, axis=0)
                out_ref[:kinds, :] = jnp.where(lane == s, col, out_ref[:kinds, :])

        return carry

    lax.fori_loop(0, slots // chunk, body, 0)


def finish_kernel(me_ref, energy_ref, wave_ref, inner_ref, outer_ref, pot_ref, add_ref, out_hbm, out_ref, sems):
    bands, planes, ny, nz = wave_ref.shape
    even = (me_ref[0] & 1) == 0

    def side(lower, n, p):
        at = (n * 2 + p) * ny
        inner = inner_ref[at : at + ny, :]
        outer = outer_ref[at : at + ny, :]
        return jnp.where(even, outer, inner) if lower else jnp.where(even, inner, outer)

    copies = []
    for n in range(bands):
        padded = [side(True, n, 0), side(True, n, 1)]
        padded += [wave_ref[n, x] for x in range(planes)]
        padded += [side(False, n, 0), side(False, n, 1)]
        for x in range(planes):
            f = padded[x + 2]
            near = padded[x + 1] + padded[x + 3]
            far = padded[x] + padded[x + 4]
            near += pltpu.roll(f, 1, 0) + pltpu.roll(f, ny - 1, 0)
            near += pltpu.roll(f, 1, 1) + pltpu.roll(f, nz - 1, 1)
            far += pltpu.roll(f, 2, 0) + pltpu.roll(f, ny - 2, 0)
            far += pltpu.roll(f, 2, 1) + pltpu.roll(f, nz - 2, 1)
            scale = pot_ref[x] + (3.75 - energy_ref[n])
            added = add_ref[n, ny * x : ny * x + ny, :]
            out_ref[n, x] = added + (scale * f - (2.0 / 3.0) * near + (1.0 / 24.0) * far)
        copy = pltpu.make_async_copy(out_ref.at[n], out_hbm.at[n], sems.at[n])
        copy.start()
        copies.append(copy)
    for copy in copies:
        copy.wait()


def scatter_kernel(
    chunk, atoms_all, energy_ref, slot_ref, own_ref, second_ref, across_ref, beyond_ref,
    pos_ref, col_ref, idx_ref, val_ref, out_ref, a_ref, b_ref, acc_ref, w_ref
):
    slots, points = idx_ref.shape
    nproj = val_ref.shape[1]
    bands, rows, _ = out_ref.shape
    kinds = bands * nproj
    height = kinds + 8
    total = None
    for ref in (own_ref, across_ref, beyond_ref):
        same = jnp.where(pos_ref[...] == ref[kinds : kinds + 1, :], 1.0, 0.0).astype(F32)
        part = lax.dot_general(
            ref[:kinds, :], same, (((1,), (1,)), ((), ())), precision=HIGH, preferred_element_type=F32
        )
        total = part if total is None else total + part
    window = jnp.concatenate(
        [ref[height:, :] for ref in (own_ref, second_ref, across_ref, beyond_ref)], axis=0
    )
    place = lax.broadcasted_iota(jnp.int32, (slots, window.shape[0]), 1).astype(F32)
    mine = jnp.where(col_ref[:, :1] == place, 1.0, 0.0).astype(F32)
    picked = jnp.dot(mine, window, precision=HIGH, preferred_element_type=F32)
    matrices = picked.T
    square = nproj * nproj
    for n in range(bands):
        energy = energy_ref[n]
        mine_n = total[nproj * n : nproj * n + nproj]
        for i in range(nproj):
            at = nproj * i
            mixed = matrices[at : at + nproj] - energy * matrices[square + at : square + at + nproj]
            w_ref[nproj * n + i : nproj * n + i + 1, 0:slots] = jnp.sum(mixed * mine_n, axis=0, keepdims=True)

    lane = lax.broadcasted_iota(jnp.int32, (kinds, slots), 1)
    sub_lo = bf(lax.broadcasted_iota(jnp.int32, (LANES, points), 0))
    sub_hi = bf(lax.broadcasted_iota(jnp.int32, (rows, points), 0))
    zero = jnp.zeros((), BF16)
    one = jnp.ones((), BF16)
    piece = bands * LANES

    def build(s, base):
        idx = idx_ref[pl.ds(s, 1), :]
        lo = bf(idx & 127)
        hi = bf(idx >> 7)
        a_ref[:, base : base + points] = jnp.where(sub_hi == hi, one, zero)
        col = jnp.sum(jnp.where(lane == s, w_ref[:, 0:slots], 0.0), axis=1, keepdims=True)
        v = val_ref[s]
        hit = sub_lo == lo
        for n in range(bands):
            back = jnp.sum(col[nproj * n : nproj * n + nproj] * v, axis=0, keepdims=True)
            big = back.astype(BF16)
            small = (back - big.astype(F32)).astype(BF16)
            at = LANES * n
            b_ref[at : at + LANES, base : base + points] = jnp.where(hit, big, zero)
            b_ref[piece + at : piece + at + LANES, base : base + points] = jnp.where(hit, small, zero)

    acc_ref[...] = jnp.zeros_like(acc_ref)

    def body(c, carry):
        @pl.when(slot_ref[c * chunk] < atoms_all)
        def _():
            for j in range(chunk):
                build(c * chunk + j, points * j)
            acc_ref[...] += lax.dot_general(
                b_ref[...], a_ref[...], (((1,), (1,)), ((), ())), preferred_element_type=F32
            )

        return carry

    lax.fori_loop(0, slots // chunk, body, 0)
    for n in range(bands):
        at = LANES * n
        out_ref[n] = (acc_ref[at : at + LANES] + acc_ref[piece + at : piece + at + LANES]).T


def swapped(value, partner):
    count = lax.axis_size("dom")
    return lax.ppermute(value, "dom", [(s, partner(s) % count) for s in range(count)])


def inner_of(d):
    return d ^ 1


def outer_of(d):
    return d + 1 if d % 2 else d - 1


def second_of(d):
    return d ^ 2


def across_of(d):
    base, y = d - d % RING, d % RING
    return base + (6, 7, 4, 5, 2, 3, 0, 1)[y]


def beyond_of(d):
    base, y = d - d % RING, d % RING
    if y < HALF:
        return base - RING + (6, 7, 4, 5)[y]
    return base + RING + (2, 3, 0, 1)[y - HALF]


def per_device(
    wave, potential, energies, proj_index, proj_values, slot_atom, atom_rank, d_matrix, q_matrix
):
    bands, planes, ny, nz = wave.shape
    slots, points = proj_index.shape
    nproj = proj_values.shape[1]
    atoms_dev = d_matrix.shape[0]
    atoms_all = atom_rank.shape[0]
    kinds = bands * nproj
    rows = planes * ny
    me = lax.axis_index("dom").astype(jnp.int32).reshape(1)
    flat = wave.reshape(bands, rows, nz)
    edge = bands * 2 * ny
    height = kinds + 8
    square = nproj * nproj

    def turned(m):
        return jnp.transpose(m, (1, 2, 0)).reshape(square, atoms_dev)

    chunk = 8
    mine, pos, col = pl.pallas_call(
        functools.partial(gather_kernel, chunk),
        out_shape=(
            jax.ShapeDtypeStruct((height + atoms_dev, LANES), F32),
            jax.ShapeDtypeStruct((slots, LANES), F32),
            jax.ShapeDtypeStruct((slots, LANES), F32),
        ),
        in_specs=[SMEM, SMEM, SMEM, HBM, HBM, HBM, HBM, HBM],
        out_specs=(VMEM, VMEM, VMEM),
        scratch_shapes=[
            pltpu.VMEM(proj_index.shape, jnp.int32),
            pltpu.VMEM(proj_values.shape, F32),
            pltpu.VMEM(flat.shape, F32),
            pltpu.VMEM((square, atoms_dev), F32),
            pltpu.VMEM((square, atoms_dev), F32),
            pltpu.VMEM((bands * LANES, 2 * rows), BF16),
            pltpu.VMEM((2 * rows, points * chunk), BF16),
            pltpu.SemaphoreType.DMA((4 + bands,)),
        ],
        compiler_params=pltpu.CompilerParams(vmem_limit_bytes=24 * MIB),
        cost_estimate=pl.CostEstimate(flops=10**10, bytes_accessed=10**7, transcendentals=0),
        name="gather",
    )(me, kept(slot_atom), kept(atom_rank), kept(proj_index), kept(proj_values), kept(flat), kept(turned(d_matrix)), kept(turned(q_matrix)))

    first = swapped(mine, inner_of)
    pair = mine[:height] + first[:height]
    known = [mine[height:], first[height:]]
    second = swapped(jnp.concatenate([pair] + known, axis=0), second_of)
    half = jnp.concatenate([pair + second[:height]] + known, axis=0)

    inner, outer = pl.pallas_call(
        pack_kernel,
        out_shape=(jax.ShapeDtypeStruct((edge, nz), F32),) * 2,
        in_specs=[SMEM, HBM, pl.BlockSpec(memory_space=pl.ANY)],
        out_specs=(VMEM, VMEM),
        scratch_shapes=[pltpu.SemaphoreType.DMA((2, bands))],
        compiler_params=pltpu.CompilerParams(vmem_limit_bytes=4 * MIB),
        cost_estimate=pl.CostEstimate(flops=10**6, bytes_accessed=10**6, transcendentals=0),
        name="pack",
    )(me, kept(flat), col)
    half, inner, outer = lax.optimization_barrier((half, inner, outer))
    beyond = swapped(half, beyond_of)
    across = swapped(half, across_of)
    outer_got = swapped(outer, outer_of)
    inner_got = swapped(inner, inner_of)

    chunk = 4
    added = pl.pallas_call(
        functools.partial(scatter_kernel, chunk, atoms_all),
        out_shape=jax.ShapeDtypeStruct((bands, rows, nz), F32),
        in_specs=[SMEM, SMEM] + [VMEM] * 8,
        out_specs=VMEM,
        scratch_shapes=[
            pltpu.VMEM((rows, points * chunk), BF16),
            pltpu.VMEM((2 * bands * LANES, points * chunk), BF16),
            pltpu.VMEM((2 * bands * LANES, rows), F32),
            pltpu.VMEM((kinds, LANES), F32),
        ],
        compiler_params=pltpu.CompilerParams(vmem_limit_bytes=24 * MIB),
        cost_estimate=pl.CostEstimate(flops=10**10, bytes_accessed=10**7, transcendentals=0),
        name="scatter",
    )(kept(energies), kept(slot_atom), half, second, across, beyond, pos, col, proj_index, proj_values)

    return pl.pallas_call(
        finish_kernel,
        out_shape=jax.ShapeDtypeStruct(wave.shape, F32),
        in_specs=[SMEM, SMEM, VMEM, VMEM, VMEM, VMEM, VMEM],
        out_specs=HBM,
        scratch_shapes=[pltpu.VMEM(wave.shape, F32), pltpu.SemaphoreType.DMA((bands,))],
        compiler_params=pltpu.CompilerParams(vmem_limit_bytes=8 * MIB),
        name="finish",
    )(me, energies, wave, inner_got, outer_got, potential, added)


def solution(mesh):
    placed = (
        P("band", "dom", None, None),
        P("dom", None, None),
        P("band"),
        P("dom", None),
        P("dom", None, None),
        P("dom"),
        P(),
        P("dom", None, None),
        P("dom", None, None),
    )
    return jax.shard_map(
        per_device,
        mesh=mesh,
        in_specs=placed,
        out_specs=P("band", "dom", None, None),
        check_vma=False,
    )
```

time: 62.8 us -> 55.3 us (0.88)
  the two profiles are of different devices: /device:TPU:8 before, /device:TPU:256 now
where the time goes in v3:
time: 55.3 us; the launch traced here: 54.9 us
  starting transfers between devices  34.9 us (63%)
  Pallas kernels  12.9 us (23%)
  waiting for transfers between devices  6.9 us (12%)
    ppermute x6, starting transfers between devices, swapped(): lax.ppermute(value, 'dom', [(s, partner(s) % count) for s in range(count)])  34.9 us
    ppermute x6, waiting for transfers between devices, swapped(): lax.ppermute(value, 'dom', [(s, partner(s) % count) for s in range(count)])  6.9 us
    pallas_call x1, Pallas kernels, per_device(): pl.pallas_call(functools.partial(gather_kernel, chunk), out_shape=(jax.Sh...  5.2 us
    pallas_call x1, Pallas kernels, per_device(): pl.pallas_call(functools.partial(scatter_kernel, chunk, atoms_all), out_s...  4.66 us
    pallas_call x1, Pallas kernels, per_device(): pl.pallas_call(finish_kernel, out_shape=jax.ShapeDtypeStruct(wave.shape,...  1.87 us
    pallas_call x1, Pallas kernels, per_device(): pl.pallas_call(pack_kernel, out_shape=(jax.ShapeDtypeStruct((edge, nz), F...  1.18 us
  transfers between devices with their start and end apart: 6, of which 3 were waited for; matrix products, arithmetic and copies ran while one was open for 0% of the time, Pallas kernels for 11%

profile of v3, /device:TPU:256, one launch (start us, length us, event | category | flops | bytes accessed | tf_op | source)
XLA Modules:
  0.0 54.9 jit_solution(15120509586021293001)
XLA Ops:
  0.0 5.2 %gather.1 = (f32[64,128]{1,0:T(8,128)S(1)}, f32[32,128]{1,0:T(8,128)S(1)}, f32[32,128]{1,0:T(8,128)S(1)}) custom-call(s32[1]{0:T(128)} %bitcast.me_ref, s32[32]{0:T(128)} %slot_ref.3, s32[3072]{0:T(1024)} %rank_ref.1, s32[32,256]{1,0:T(8,128)} %idx_ref.1, f32[32,8,256]{2,1,0:T(8,128)} %val_ref.1, f32[4,256,128]{2,1,0:T(8,128)} %bitcast.8, ...), custom_call_target="tpu_custom_call" | custom-call | flops 10000000000 | bytes 10000000 | tf_op jit(solution)/shard_map/gather/pallas_call | solution.py:296
  5.2 4.9 %collective-permute-start = (f32[64,128]{1,0:T(8,128)S(1)}, f32[64,128]{1,0:T(8,128)S(1)}, u32[]{:S(2)}, u32[]{:S(2)}) collective-permute-start(f32[64,128]{1,0:T(8,128)S(1)} %get-tuple-element.13), channel_id=1, source_target_pairs={{0,6},{6,0},{12,18},{18,12},{24,30},{30,24},{36,42},{42,36},{48,54... | collective-permute-start | bytes 98312 | tf_op jit(solution)/shard_map/ppermute | solution.py:249
  10.1 1.9 %collective-permute-done = f32[64,128]{1,0:T(8,128)S(1)} collective-permute-done((f32[64,128]{1,0:T(8,128)S(1)}, f32[64,128]{1,0:T(8,128)S(1)}, u32[]{:S(2)}, u32[]{:S(2)}) %collective-permute-start) | collective-permute-done | bytes 32800 | tf_op jit(solution)/shard_map/ppermute | solution.py:249
  12.0 6.3 %collective-permute-start.1 = (f32[88,128]{1,0:T(8,128)S(1)}, f32[88,128]{1,0:T(8,128)S(1)}, u32[]{:S(2)}, u32[]{:S(2)}) collective-permute-start(f32[88,128]{1,0:T(8,128)S(1)} %pad_maximum_fusion.1), channel_id=1, source_target_pairs={{0,12},{6,18},{12,0},{18,6},{24,36},{30,42},{36,24},{42,30},{48,60... | collective-permute-start | bytes 135176 | tf_op jit(solution)/shard_map/ppermute | solution.py:249
  18.4 0.0 copy-start.3
  18.4 1.2 %pack.1 = (f32[512,128]{1,0:T(8,128)S(1)}, f32[512,128]{1,0:T(8,128)S(1)}) custom-call(s32[1]{0:T(128)} %bitcast.me_ref, f32[4,256,128]{2,1,0:T(8,128)} %bitcast.9, f32[32,128]{1,0:T(8,128)S(1)} %get-tuple-element.14.after_ref.col_ref), custom_call_target="tpu_custom_call" | custom-call | flops 1000000 | bytes 1000000 | tf_op jit(solution)/shard_map/pack/pallas_call | solution.py:326
  19.6 0.8 %collective-permute-done.1.second_ref = f32[88,128]{1,0:T(8,128)S(1)} collective-permute-done((f32[88,128]{1,0:T(8,128)S(1)}, f32[88,128]{1,0:T(8,128)S(1)}, u32[]{:S(2)}, u32[]{:S(2)}) %collective-permute-start.1) | collective-permute-done | bytes 45088 | tf_op jit(solution)/shard_map/ppermute | solution.py:249
  20.4 12.5 %collective-permute-start.5 = (f32[88,128]{1,0:T(8,128)S(1)}, f32[88,128]{1,0:T(8,128)S(1)}, u32[]{:S(2)}, u32[]{:S(2)}) collective-permute-start(f32[88,128]{1,0:T(8,128)S(1)} %pad_maximum_fusion.own_ref), channel_id=1, source_target_pairs={{0,756},{6,762},{12,744},{18,750},{24,60},{30,66},{36,48},{42,54},... | collective-permute-start | bytes 135176 | tf_op jit(solution)/shard_map/ppermute | solution.py:249
  32.9 1.9 %collective-permute-start.4 = (f32[88,128]{1,0:T(8,128)S(1)}, f32[88,128]{1,0:T(8,128)S(1)}, u32[]{:S(2)}, u32[]{:S(2)}) collective-permute-start(f32[88,128]{1,0:T(8,128)S(1)} %pad_maximum_fusion.own_ref), channel_id=1, source_target_pairs={{0,36},{6,42},{12,24},{18,30},{24,12},{30,18},{36,0},{42,6},{48,84... | collective-permute-start | bytes 135176 | tf_op jit(solution)/shard_map/ppermute | solution.py:249
  34.8 3.9 %collective-permute-start.2 = (f32[512,128]{1,0:T(8,128)S(1)}, f32[512,128]{1,0:T(8,128)S(1)}, u32[]{:S(2)}, u32[]{:S(2)}) collective-permute-start(f32[512,128]{1,0:T(8,128)S(1)} %get-tuple-element.17), channel_id=1, source_target_pairs={{0,6},{6,0},{12,18},{18,12},{24,30},{30,24},{36,42},{42,36},{48,54... | collective-permute-start | bytes 786440 | tf_op jit(solution)/shard_map/ppermute | solution.py:249
  38.7 5.3 %collective-permute-start.3 = (f32[512,128]{1,0:T(8,128)S(1)}, f32[512,128]{1,0:T(8,128)S(1)}, u32[]{:S(2)}, u32[]{:S(2)}) collective-permute-start(f32[512,128]{1,0:T(8,128)S(1)} %get-tuple-element.18), channel_id=1, source_target_pairs={{0,762},{6,12},{12,6},{18,24},{24,18},{30,36},{36,30},{42,48},{48,... | collective-permute-start | bytes 786440 | tf_op jit(solution)/shard_map/ppermute | solution.py:249
  44.0 0.0 collective-permute-done.5.beyond_ref
  44.0 0.0 collective-permute-done.4.across_ref
  44.1 0.0 copy-done.3
  44.1 0.0 copy-done.4
  44.1 0.0 copy-start
  44.1 0.0 copy-start.1
  44.1 0.0 copy-start.2
  44.1 4.7 %scatter.1.add_ref = f32[4,256,128]{2,1,0:T(8,128)S(1)} custom-call(f32[4]{0:T(128)} %energy_ref.3, s32[32]{0:T(128)} %slot_ref.3, f32[88,128]{1,0:T(8,128)S(1)} %pad_maximum_fusion.own_ref, f32[88,128]{1,0:T(8,128)S(1)} %collective-permute-done.1.second_ref, f32[88,128]{1,0:T(8,128)S(1)} %collective-permute-done.4.across_ref, ...), custom_call_target="tpu_custom_call" | custom-call | flops 10000000000 | bytes 10000000 | tf_op jit(solution)/shard_map/scatter/pallas_call | solution.py:343
  48.8 0.0 collective-permute-done.2.inner_ref
  48.8 4.2 %collective-permute-done.3.outer_ref = f32[512,128]{1,0:T(8,128)S(1)} collective-permute-done((f32[512,128]{1,0:T(8,128)S(1)}, f32[512,128]{1,0:T(8,128)S(1)}, u32[]{:S(2)}, u32[]{:S(2)}) %collective-permute-start.3) | collective-permute-done | bytes 262176 | tf_op jit(solution)/shard_map/ppermute | solution.py:249
  53.0 0.0 copy-done
  53.0 0.0 copy-done.1
  53.0 1.9 %finish.1 = f32[4,4,64,128]{3,2,1,0:T(8,128)} custom-call(s32[1]{0:T(128)} %bitcast.me_ref, f32[4]{0:T(128)S(1)} %copy-done.2, f32[4,4,64,128]{3,2,1,0:T(8,128)S(1)} %copy-done, f32[512,128]{1,0:T(8,128)S(1)} %collective-permute-done.2.inner_ref, f32[512,128]{1,0:T(8,128)S(1)} %collective-permute-done.3.outer_ref, f32[4,64,128]{2,1,0:T(8,128)S(1)} %copy-done.1, ...), custom_call_target="tpu_custom_call" | custom-call | tf_op jit(solution)/shard_map/finish/pallas_call | solution.py:359
  (8 shorter events, 0.0 us)
Async XLA Ops:
  5.2 6.8 %collective-permute-start = (f32[64,128]{1,0:T(8,128)S(1)}, f32[64,128]{1,0:T(8,128)S(1)}, u32[]{:S(2)}, u32[]{:S(2)}) collective-permute-start(f32[64,128]{1,0:T(8,128)S(1)} %get-tuple-element.13), channel_id=1, source_target_pairs={{0,6},{6,0},{12,18},{18,12},{24,30},{30,24},{36,42},{42,36},{48,54... | collective-permute-start | bytes 98312 | tf_op jit(solution)/shard_map/ppermute | solution.py:249
  12.0 8.4 %collective-permute-start.1 = (f32[88,128]{1,0:T(8,128)S(1)}, f32[88,128]{1,0:T(8,128)S(1)}, u32[]{:S(2)}, u32[]{:S(2)}) collective-permute-start(f32[88,128]{1,0:T(8,128)S(1)} %pad_maximum_fusion.1), channel_id=1, source_target_pairs={{0,12},{6,18},{12,0},{18,6},{24,36},{30,42},{36,24},{42,30},{48,60... | collective-permute-start | bytes 135176 | tf_op jit(solution)/shard_map/ppermute | solution.py:249
  18.4 25.7 %copy-start.3 = (f32[32,8,256]{2,1,0:T(8,128)S(1)}, f32[32,8,256]{2,1,0:T(8,128)}, u32[]{:S(2)}) copy-start(f32[32,8,256]{2,1,0:T(8,128)} %val_ref.1) | copy-start | bytes 786436
  20.4 23.7 %copy-start.4 = (s32[32,256]{1,0:T(8,128)S(1)}, s32[32,256]{1,0:T(8,128)}, u32[]{:S(2)}) copy-start(s32[32,256]{1,0:T(8,128)} %idx_ref.1) | copy-start | bytes 98308
  20.4 23.7 %collective-permute-start.5 = (f32[88,128]{1,0:T(8,128)S(1)}, f32[88,128]{1,0:T(8,128)S(1)}, u32[]{:S(2)}, u32[]{:S(2)}) collective-permute-start(f32[88,128]{1,0:T(8,128)S(1)} %pad_maximum_fusion.own_ref), channel_id=1, source_target_pairs={{0,756},{6,762},{12,744},{18,750},{24,60},{30,66},{36,48},{42,54},... | collective-permute-start | bytes 135176 | tf_op jit(solution)/shard_map/ppermute | solution.py:249
  32.9 11.2 %collective-permute-start.4 = (f32[88,128]{1,0:T(8,128)S(1)}, f32[88,128]{1,0:T(8,128)S(1)}, u32[]{:S(2)}, u32[]{:S(2)}) collective-permute-start(f32[88,128]{1,0:T(8,128)S(1)} %pad_maximum_fusion.own_ref), channel_id=1, source_target_pairs={{0,36},{6,42},{12,24},{18,30},{24,12},{30,18},{36,0},{42,6},{48,84... | collective-permute-start | bytes 135176 | tf_op jit(solution)/shard_map/ppermute | solution.py:249
  34.8 14.0 %collective-permute-start.2 = (f32[512,128]{1,0:T(8,128)S(1)}, f32[512,128]{1,0:T(8,128)S(1)}, u32[]{:S(2)}, u32[]{:S(2)}) collective-permute-start(f32[512,128]{1,0:T(8,128)S(1)} %get-tuple-element.17), channel_id=1, source_target_pairs={{0,6},{6,0},{12,18},{18,12},{24,30},{30,24},{36,42},{42,36},{48,54... | collective-permute-start | bytes 786440 | tf_op jit(solution)/shard_map/ppermute | solution.py:249
  38.7 14.3 %collective-permute-start.3 = (f32[512,128]{1,0:T(8,128)S(1)}, f32[512,128]{1,0:T(8,128)S(1)}, u32[]{:S(2)}, u32[]{:S(2)}) collective-permute-start(f32[512,128]{1,0:T(8,128)S(1)} %get-tuple-element.18), channel_id=1, source_target_pairs={{0,762},{6,12},{12,6},{18,24},{24,18},{30,36},{36,30},{42,48},{48,... | collective-permute-start | bytes 786440 | tf_op jit(solution)/shard_map/ppermute | solution.py:249
  44.1 8.9 %copy-start = (f32[4,4,64,128]{3,2,1,0:T(8,128)S(1)}, f32[4,4,64,128]{3,2,1,0:T(8,128)}, u32[]{:S(2)}) copy-start(f32[4,4,64,128]{3,2,1,0:T(8,128)} %wave_ref.1) | copy-start | bytes 1572868
  44.1 8.9 %copy-start.1 = (f32[4,64,128]{2,1,0:T(8,128)S(1)}, f32[4,64,128]{2,1,0:T(8,128)}, u32[]{:S(2)}) copy-start(f32[4,64,128]{2,1,0:T(8,128)} %pot_ref.1) | copy-start | bytes 393220
  44.1 8.9 %copy-start.2 = (f32[4]{0:T(128)S(1)}, f32[4]{0:T(128)}, u32[]{:S(2)}) copy-start(f32[4]{0:T(128)} %energy_ref.3) | copy-start | bytes 52

commit v4 on v3

--- a/solution.py
+++ b/solution.py
@@ -6,6 +6,7 @@
 from jax.experimental import pallas as pl
 from jax.experimental.pallas import tpu as pltpu
 from jax.sharding import PartitionSpec as P
+
 
 HIGH = lax.Precision.HIGHEST
 F32 = jnp.float32
@@ -47,7 +48,7 @@
 
 
 def gather_kernel(
-    chunk, me_ref, slot_ref, rank_ref, idx_hbm, val_hbm, wave_hbm, d_hbm, q_hbm,
+    chunk, aside, me_ref, slot_ref, rank_ref, idx_hbm, val_hbm, wave_hbm, d_hbm, q_hbm,
     out_ref, pos_ref, col_ref,
     idx_ref, val_ref, wave_ref, d_ref, q_ref, grid_ref, hot_ref, sems
 ):
@@ -73,64 +74,86 @@
     out_ref[:height, :] = jnp.zeros((height, LANES), F32)
     pos_ref[...] = jnp.zeros_like(pos_ref)
     col_ref[...] = jnp.full_like(col_ref, -1.0)
-    sub_hi = bf(lax.broadcasted_iota(jnp.int32, (rows, points), 0))
-    for n in range(bands):
-        copies[1 + n].wait()
-        w = wave_ref[n].T
-        big = w.astype(BF16)
-        grid_ref[LANES * n : LANES * n + LANES, :rows] = big
-        grid_ref[LANES * n : LANES * n + LANES, rows:] = (w - big.astype(F32)).astype(BF16)
-    copies[0].wait()
-    for copy in copies[1 + bands :]:
+    sub_lo = bf(lax.broadcasted_iota(jnp.int32, (LANES, points), 0))
+    for copy in copies[2 + bands :]:
         copy.wait()
     matrices = jnp.concatenate([d_ref[...], q_ref[...]], axis=0)
     matrices = jnp.concatenate(
         [matrices, jnp.zeros((matrices.shape[0], LANES - atoms_dev), F32)], axis=1
     )
     out_ref[height:, :] = matrices.T[:atoms_dev]
+    for n in range(bands):
+        copies[1 + n].wait()
+        w = wave_ref[n]
+        big = w.astype(BF16)
+        grid_ref[rows * n : rows * n + rows, :LANES] = big
+        grid_ref[rows * n : rows * n + rows, LANES:] = (w - big.astype(F32)).astype(BF16)
+    copies[0].wait()
+    copies[1 + bands].wait()
+    dense = chunk - aside
+
+    def close(s, accs, sub):
+        atom = slot_ref[s]
+        live = atom < atoms_all
+        pos = rank_ref[jnp.minimum(atom, atoms_all - 1)]
+        owner = pos // atoms_dev
+        apart = owner ^ me
+        block = jnp.where(apart < RING, HALF, HALF + 2) + (apart & 1)
+        block = jnp.where(apart < HALF, apart, block)
+        column = jnp.where(live, block * atoms_dev + pos - owner * atoms_dev, -1).astype(F32)
+        place = jnp.where(live, pos + 1, 0).astype(F32)
+        pos_ref[pl.ds(s, 1), :] = jnp.full((1, LANES), place, F32)
+        col_ref[pl.ds(s, 1), :] = jnp.full((1, LANES), column, F32)
+        out_ref[kinds:height, :] = jnp.where(lane_row == s, place, out_ref[kinds:height, :])
+        cols = []
+        for n in range(bands):
+            total = None
+            for acc, h in zip(accs[n], halves, strict=True):
+                pick = jnp.take_along_axis(acc, sub[:, h], axis=0, mode="promise_in_bounds")
+                prod = pick * val_ref[s, :, h]
+                total = prod if total is None else total + prod
+            cols.append(jnp.sum(total, axis=1, keepdims=True))
+        col = jnp.concatenate(cols, axis=0)
+        out_ref[:kinds, :] = jnp.where(lane == s, col, out_ref[:kinds, :])
+
+    def split(s):
+        idx = jnp.broadcast_to(idx_ref[pl.ds(s, 1), :], (8, points))
+        return idx >> 10, (idx >> 7) & 7, idx & 127
 
     def body(c, carry):
         @pl.when(slot_ref[c * chunk] < atoms_all)
         def _():
-            for j in range(chunk):
+            for j in range(dense):
                 idx = idx_ref[pl.ds(c * chunk + j, 1), :]
-                hot = jnp.where(sub_hi == bf(idx >> 7), jnp.ones((), BF16), jnp.zeros((), BF16))
-                hot_ref[:rows, points * j : points * j + points] = hot
-                hot_ref[rows:, points * j : points * j + points] = hot
+                hot = jnp.where(sub_lo == bf(idx & 127), jnp.ones((), BF16), jnp.zeros((), BF16))
+                hot_ref[:LANES, points * j : points * j + points] = hot
+                hot_ref[LANES:, points * j : points * j + points] = hot
             lines = jnp.dot(grid_ref[...], hot_ref[...], preferred_element_type=F32)
-            for j in range(chunk):
+            for j in range(dense):
                 s = c * chunk + j
-                atom = slot_ref[s]
-                live = atom < atoms_all
-                pos = rank_ref[jnp.minimum(atom, atoms_all - 1)]
-                owner = pos // atoms_dev
-                apart = owner ^ me
-                block = jnp.where(apart < RING, HALF, HALF + 2) + (apart & 1)
-                block = jnp.where(apart < HALF, apart, block)
-                column = jnp.where(live, block * atoms_dev + pos - owner * atoms_dev, -1).astype(F32)
-                place = jnp.where(live, pos + 1, 0).astype(F32)
-                pos_ref[pl.ds(s, 1), :] = jnp.full((1, LANES), place, F32)
-                col_ref[pl.ds(s, 1), :] = jnp.full((1, LANES), column, F32)
-                out_ref[kinds:height, :] = jnp.where(lane_row == s, place, out_ref[kinds:height, :])
-                idx = jnp.broadcast_to(idx_ref[pl.ds(s, 1), :], (8, points))
-                tile = (idx >> 3) & 15
-                sub = idx & 7
-                cols = []
+                tile, sub, _ = split(s)
+                span = slice(points * j, points * j + points)
+                accs = []
                 for n in range(bands):
-                    at = LANES * n
-                    acc = lines[at : at + 8, points * j : points * j + points]
-                    for k in range(1, LANES // 8):
-                        acc = jnp.where(
-                            tile == k, lines[at + 8 * k : at + 8 * k + 8, points * j : points * j + points], acc
-                        )
-                    total = None
-                    for h in halves:
-                        pick = jnp.take_along_axis(acc[:, h], sub[:, h], axis=0, mode="promise_in_bounds")
-                        prod = pick * val_ref[s, :, h]
-                        total = prod if total is None else total + prod
-                    cols.append(jnp.sum(total, axis=1, keepdims=True))
-                col = jnp.concatenate(cols, axis=0)
-                out_ref[:kinds, :] = jnp.where(lane == s, col, out_ref[:kinds, :])
+                    at = rows * n
+                    acc = lines[at : at + 8, span]
+                    for k in range(1, rows // 8):
+                        acc = jnp.where(tile == k, lines[at + 8 * k : at + 8 * k + 8, span], acc)
+                    accs.append([acc[:, h] for h in halves])
+                close(s, accs, sub)
+            for j in range(dense, chunk):
+                s = c * chunk + j
+                tile, sub, lo = split(s)
+                accs = [[None] * len(halves) for _ in range(bands)]
+                for i, h in enumerate(halves):
+                    for k in range(rows // 8):
+                        hit = tile[:, h] == k
+                        for n in range(bands):
+                            line = jnp.take_along_axis(
+                                wave_ref[n, 8 * k : 8 * k + 8, :], lo[:, h], axis=1, mode="promise_in_bounds"
+                            )
+                            accs[n][i] = line if k == 0 else jnp.where(hit, line, accs[n][i])
+                close(s, accs, sub)
 
         return carry
 
@@ -292,9 +315,9 @@
     def turned(m):
         return jnp.transpose(m, (1, 2, 0)).reshape(square, atoms_dev)
 
-    chunk = 8
+    chunk, aside = 16, 4
     mine, pos, col = pl.pallas_call(
-        functools.partial(gather_kernel, chunk),
+        functools.partial(gather_kernel, chunk, aside),
         out_shape=(
             jax.ShapeDtypeStruct((height + atoms_dev, LANES), F32),
             jax.ShapeDtypeStruct((slots, LANES), F32),
@@ -308,11 +331,11 @@
             pltpu.VMEM(flat.shape, F32),
             pltpu.VMEM((square, atoms_dev), F32),
             pltpu.VMEM((square, atoms_dev), F32),
-            pltpu.VMEM((bands * LANES, 2 * rows), BF16),
-            pltpu.VMEM((2 * rows, points * chunk), BF16),
+            pltpu.VMEM((bands * rows, 2 * LANES), BF16),
+            pltpu.VMEM((2 * LANES, points * (chunk - aside)), BF16),
             pltpu.SemaphoreType.DMA((4 + bands,)),
         ],
-        compiler_params=pltpu.CompilerParams(vmem_limit_bytes=24 * MIB),
+        compiler_params=pltpu.CompilerParams(vmem_limit_bytes=40 * MIB),
         cost_estimate=pl.CostEstimate(flops=10**10, bytes_accessed=10**7, transcendentals=0),
         name="gather",
     )(me, kept(slot_atom), kept(atom_rank), kept(proj_index), kept(proj_values), kept(flat), kept(turned(d_matrix)), kept(turned(q_matrix)))
@@ -333,13 +356,12 @@
         cost_estimate=pl.CostEstimate(flops=10**6, bytes_accessed=10**6, transcendentals=0),
         name="pack",
     )(me, kept(flat), col)
-    half, inner, outer = lax.optimization_barrier((half, inner, outer))
     beyond = swapped(half, beyond_of)
     across = swapped(half, across_of)
     outer_got = swapped(outer, outer_of)
     inner_got = swapped(inner, inner_of)
 
-    chunk = 4
+    chunk = 16
     added = pl.pallas_call(
         functools.partial(scatter_kernel, chunk, atoms_all),
         out_shape=jax.ShapeDtypeStruct((bands, rows, nz), F32),
@@ -351,7 +373,7 @@
             pltpu.VMEM((2 * bands * LANES, rows), F32),
             pltpu.VMEM((kinds, LANES), F32),
         ],
-        compiler_params=pltpu.CompilerParams(vmem_limit_bytes=24 * MIB),
+        compiler_params=pltpu.CompilerParams(vmem_limit_bytes=40 * MIB),
         cost_estimate=pl.CostEstimate(flops=10**10, bytes_accessed=10**7, transcendentals=0),
         name="scatter",
     )(kept(energies), kept(slot_atom), half, second, across, beyond, pos, col, proj_index, proj_values)

time: 55.3 us -> 55.2 us (level)
  waiting for transfers between devices: 6.9 us -> 8.86 us
  Pallas kernels: 12.9 us -> 11.5 us
  starting transfers between devices: 34.9 us -> 34.3 us
    ppermute x6, waiting for transfers between devices: 6.9 us -> 8.86 us  [swapped(): lax.ppermute(value, 'dom', [(s, partner(s) % count) for s in range(count)])]
    pallas_call x1, Pallas kernels: 4.66 us -> 3.91 us  [per_device(): pl.pallas_call(functools.partial(scatter_kernel, chunk, atoms_all), out_s...]
    pallas_call x1, Pallas kernels: 5.2 us -> 4.51 us  [per_device(): pl.pallas_call(functools.partial(gather_kernel, chunk, aside), out_shape=...]
  transfers between devices with their start and end apart: 6 -> 6, of which waited for: 3 -> 3; matrix products, arithmetic and copies ran while one was open for 0% -> 0% of each run, Pallas kernels for 11% -> 9%
where the time goes in v4:
time: 55.2 us; the launch traced here: 54.9 us
  starting transfers between devices  34.3 us (62%)
  Pallas kernels  11.5 us (21%)
  waiting for transfers between devices  8.86 us (16%)
    ppermute x6, starting transfers between devices, swapped(): lax.ppermute(value, 'dom', [(s, partner(s) % count) for s in range(count)])  34.3 us
    ppermute x6, waiting for transfers between devices, swapped(): lax.ppermute(value, 'dom', [(s, partner(s) % count) for s in range(count)])  8.86 us
    pallas_call x1, Pallas kernels, per_device(): pl.pallas_call(functools.partial(gather_kernel, chunk, aside), out_shape=...  4.51 us
    pallas_call x1, Pallas kernels, per_device(): pl.pallas_call(functools.partial(scatter_kernel, chunk, atoms_all), out_s...  3.91 us
    pallas_call x1, Pallas kernels, per_device(): pl.pallas_call(finish_kernel, out_shape=jax.ShapeDtypeStruct(wave.shape,...  1.87 us
    pallas_call x1, Pallas kernels, per_device(): pl.pallas_call(pack_kernel, out_shape=(jax.ShapeDtypeStruct((edge, nz), F...  1.17 us
  transfers between devices with their start and end apart: 6, of which 3 were waited for; matrix products, arithmetic and copies ran while one was open for 0% of the time, Pallas kernels for 9%

profile of v4, /device:TPU:256, one launch (start us, length us, event | category | flops | bytes accessed | tf_op | source)
XLA Modules:
  0.0 54.9 jit_solution(3622604612462674021)
XLA Ops:
  0.0 4.5 %gather.1 = (f32[64,128]{1,0:T(8,128)S(1)}, f32[32,128]{1,0:T(8,128)S(1)}, f32[32,128]{1,0:T(8,128)S(1)}) custom-call(s32[1]{0:T(128)} %bitcast.me_ref, s32[32]{0:T(128)} %slot_ref.3, s32[3072]{0:T(1024)} %rank_ref.1, s32[32,256]{1,0:T(8,128)} %idx_ref.1, f32[32,8,256]{2,1,0:T(8,128)} %val_ref.1, f32[4,256,128]{2,1,0:T(8,128)} %bitcast.8, ...), custom_call_target="tpu_custom_call" | custom-call | flops 10000000000 | bytes 10000000 | tf_op jit(solution)/shard_map/gather/pallas_call | solution.py:319
  4.5 5.8 %collective-permute-start.2 = (f32[64,128]{1,0:T(8,128)S(1)}, f32[64,128]{1,0:T(8,128)S(1)}, u32[]{:S(2)}, u32[]{:S(2)}) collective-permute-start(f32[64,128]{1,0:T(8,128)S(1)} %get-tuple-element.13), channel_id=1, source_target_pairs={{0,6},{6,0},{12,18},{18,12},{24,30},{30,24},{36,42},{42,36},{48,54... | collective-permute-start | bytes 98312 | tf_op jit(solution)/shard_map/ppermute | solution.py:272
  10.3 1.9 %collective-permute-done.2 = f32[64,128]{1,0:T(8,128)S(1)} collective-permute-done((f32[64,128]{1,0:T(8,128)S(1)}, f32[64,128]{1,0:T(8,128)S(1)}, u32[]{:S(2)}, u32[]{:S(2)}) %collective-permute-start.2) | collective-permute-done | bytes 32800 | tf_op jit(solution)/shard_map/ppermute | solution.py:272
  12.2 4.9 %collective-permute-start.3 = (f32[88,128]{1,0:T(8,128)S(1)}, f32[88,128]{1,0:T(8,128)S(1)}, u32[]{:S(2)}, u32[]{:S(2)}) collective-permute-start(f32[88,128]{1,0:T(8,128)S(1)} %pad_maximum_fusion.1), channel_id=1, source_target_pairs={{0,12},{6,18},{12,0},{18,6},{24,36},{30,42},{36,24},{42,30},{48,60... | collective-permute-start | bytes 135176 | tf_op jit(solution)/shard_map/ppermute | solution.py:272
  17.1 2.0 %collective-permute-done.3.second_ref = f32[88,128]{1,0:T(8,128)S(1)} collective-permute-done((f32[88,128]{1,0:T(8,128)S(1)}, f32[88,128]{1,0:T(8,128)S(1)}, u32[]{:S(2)}, u32[]{:S(2)}) %collective-permute-start.3) | collective-permute-done | bytes 45088 | tf_op jit(solution)/shard_map/ppermute | solution.py:272
  19.1 12.5 %collective-permute-start.5 = (f32[88,128]{1,0:T(8,128)S(1)}, f32[88,128]{1,0:T(8,128)S(1)}, u32[]{:S(2)}, u32[]{:S(2)}) collective-permute-start(f32[88,128]{1,0:T(8,128)S(1)} %pad_maximum_fusion.own_ref), channel_id=1, source_target_pairs={{0,756},{6,762},{12,744},{18,750},{24,60},{30,66},{36,48},{42,54},... | collective-permute-start | bytes 135176 | tf_op jit(solution)/shard_map/ppermute | solution.py:272
  31.6 1.9 %collective-permute-start.4 = (f32[88,128]{1,0:T(8,128)S(1)}, f32[88,128]{1,0:T(8,128)S(1)}, u32[]{:S(2)}, u32[]{:S(2)}) collective-permute-start(f32[88,128]{1,0:T(8,128)S(1)} %pad_maximum_fusion.own_ref), channel_id=1, source_target_pairs={{0,36},{6,42},{12,24},{18,30},{24,12},{30,18},{36,0},{42,6},{48,84... | collective-permute-start | bytes 135176 | tf_op jit(solution)/shard_map/ppermute | solution.py:272
  33.6 0.0 copy-start.3
  33.6 0.0 copy-start.4
  33.6 1.2 %pack.1 = (f32[512,128]{1,0:T(8,128)S(1)}, f32[512,128]{1,0:T(8,128)S(1)}) custom-call(s32[1]{0:T(128)} %bitcast.me_ref, f32[4,256,128]{2,1,0:T(8,128)} %bitcast.9, f32[32,128]{1,0:T(8,128)S(1)} %get-tuple-element.10.after_ref.col_ref), custom_call_target="tpu_custom_call" | custom-call | flops 1000000 | bytes 1000000 | tf_op jit(solution)/shard_map/pack/pallas_call | solution.py:349
  34.8 3.9 %collective-permute-start = (f32[512,128]{1,0:T(8,128)S(1)}, f32[512,128]{1,0:T(8,128)S(1)}, u32[]{:S(2)}, u32[]{:S(2)}) collective-permute-start(f32[512,128]{1,0:T(8,128)S(1)} %get-tuple-element.11), channel_id=1, source_target_pairs={{0,6},{6,0},{12,18},{18,12},{24,30},{30,24},{36,42},{42,36},{48,54... | collective-permute-start | bytes 786440 | tf_op jit(solution)/shard_map/ppermute | solution.py:272
  38.7 5.3 %collective-permute-start.1 = (f32[512,128]{1,0:T(8,128)S(1)}, f32[512,128]{1,0:T(8,128)S(1)}, u32[]{:S(2)}, u32[]{:S(2)}) collective-permute-start(f32[512,128]{1,0:T(8,128)S(1)} %get-tuple-element.12), channel_id=1, source_target_pairs={{0,762},{6,12},{12,6},{18,24},{24,18},{30,36},{36,30},{42,48},{48,... | collective-permute-start | bytes 786440 | tf_op jit(solution)/shard_map/ppermute | solution.py:272
  44.0 0.0 collective-permute-done.5.beyond_ref
  44.0 0.0 collective-permute-done.4.across_ref
  44.0 0.0 copy-done.3
  44.0 0.0 copy-done.4
  44.0 0.0 copy-start
  44.1 0.0 copy-start.1
  44.1 0.0 copy-start.2
  44.1 3.9 %scatter.1.add_ref = f32[4,256,128]{2,1,0:T(8,128)S(1)} custom-call(f32[4]{0:T(128)} %energy_ref.3, s32[32]{0:T(128)} %slot_ref.3, f32[88,128]{1,0:T(8,128)S(1)} %pad_maximum_fusion.own_ref, f32[88,128]{1,0:T(8,128)S(1)} %collective-permute-done.3.second_ref, f32[88,128]{1,0:T(8,128)S(1)} %collective-permute-done.4.across_ref, ...), custom_call_target="tpu_custom_call" | custom-call | flops 10000000000 | bytes 10000000 | tf_op jit(solution)/shard_map/scatter/pallas_call | solution.py:365
  48.0 0.0 collective-permute-done.inner_ref
  48.0 5.0 %collective-permute-done.1.outer_ref = f32[512,128]{1,0:T(8,128)S(1)} collective-permute-done((f32[512,128]{1,0:T(8,128)S(1)}, f32[512,128]{1,0:T(8,128)S(1)}, u32[]{:S(2)}, u32[]{:S(2)}) %collective-permute-start.1) | collective-permute-done | bytes 262176 | tf_op jit(solution)/shard_map/ppermute | solution.py:272
  53.0 0.0 copy-done.2
  53.0 1.9 %finish.1 = f32[4,4,64,128]{3,2,1,0:T(8,128)} custom-call(s32[1]{0:T(128)} %bitcast.me_ref, f32[4]{0:T(128)S(1)} %copy-done.2, f32[4,4,64,128]{3,2,1,0:T(8,128)S(1)} %copy-done, f32[512,128]{1,0:T(8,128)S(1)} %collective-permute-done.inner_ref, f32[512,128]{1,0:T(8,128)S(1)} %collective-permute-done.1.outer_ref, f32[4,64,128]{2,1,0:T(8,128)S(1)} %copy-done.1, ...), custom_call_target="tpu_custom_call" | custom-call | tf_op jit(solution)/shard_map/finish/pallas_call | solution.py:381
  (8 shorter events, 0.0 us)
Async XLA Ops:
  4.5 7.7 %collective-permute-start.2 = (f32[64,128]{1,0:T(8,128)S(1)}, f32[64,128]{1,0:T(8,128)S(1)}, u32[]{:S(2)}, u32[]{:S(2)}) collective-permute-start(f32[64,128]{1,0:T(8,128)S(1)} %get-tuple-element.13), channel_id=1, source_target_pairs={{0,6},{6,0},{12,18},{18,12},{24,30},{30,24},{36,42},{42,36},{48,54... | collective-permute-start | bytes 98312 | tf_op jit(solution)/shard_map/ppermute | solution.py:272
  12.2 6.9 %collective-permute-start.3 = (f32[88,128]{1,0:T(8,128)S(1)}, f32[88,128]{1,0:T(8,128)S(1)}, u32[]{:S(2)}, u32[]{:S(2)}) collective-permute-start(f32[88,128]{1,0:T(8,128)S(1)} %pad_maximum_fusion.1), channel_id=1, source_target_pairs={{0,12},{6,18},{12,0},{18,6},{24,36},{30,42},{36,24},{42,30},{48,60... | collective-permute-start | bytes 135176 | tf_op jit(solution)/shard_map/ppermute | solution.py:272
  19.1 24.9 %collective-permute-start.5 = (f32[88,128]{1,0:T(8,128)S(1)}, f32[88,128]{1,0:T(8,128)S(1)}, u32[]{:S(2)}, u32[]{:S(2)}) collective-permute-start(f32[88,128]{1,0:T(8,128)S(1)} %pad_maximum_fusion.own_ref), channel_id=1, source_target_pairs={{0,756},{6,762},{12,744},{18,750},{24,60},{30,66},{36,48},{42,54},... | collective-permute-start | bytes 135176 | tf_op jit(solution)/shard_map/ppermute | solution.py:272
  31.6 12.4 %collective-permute-start.4 = (f32[88,128]{1,0:T(8,128)S(1)}, f32[88,128]{1,0:T(8,128)S(1)}, u32[]{:S(2)}, u32[]{:S(2)}) collective-permute-start(f32[88,128]{1,0:T(8,128)S(1)} %pad_maximum_fusion.own_ref), channel_id=1, source_target_pairs={{0,36},{6,42},{12,24},{18,30},{24,12},{30,18},{36,0},{42,6},{48,84... | collective-permute-start | bytes 135176 | tf_op jit(solution)/shard_map/ppermute | solution.py:272
  33.6 10.5 %copy-start.3 = (f32[32,8,256]{2,1,0:T(8,128)S(1)}, f32[32,8,256]{2,1,0:T(8,128)}, u32[]{:S(2)}) copy-start(f32[32,8,256]{2,1,0:T(8,128)} %val_ref.1) | copy-start | bytes 786436
  33.6 10.5 %copy-start.4 = (s32[32,256]{1,0:T(8,128)S(1)}, s32[32,256]{1,0:T(8,128)}, u32[]{:S(2)}) copy-start(s32[32,256]{1,0:T(8,128)} %idx_ref.1) | copy-start | bytes 98308
  34.8 13.2 %collective-permute-start = (f32[512,128]{1,0:T(8,128)S(1)}, f32[512,128]{1,0:T(8,128)S(1)}, u32[]{:S(2)}, u32[]{:S(2)}) collective-permute-start(f32[512,128]{1,0:T(8,128)S(1)} %get-tuple-element.11), channel_id=1, source_target_pairs={{0,6},{6,0},{12,18},{18,12},{24,30},{30,24},{36,42},{42,36},{48,54... | collective-permute-start | bytes 786440 | tf_op jit(solution)/shard_map/ppermute | solution.py:272
  38.7 14.3 %collective-permute-start.1 = (f32[512,128]{1,0:T(8,128)S(1)}, f32[512,128]{1,0:T(8,128)S(1)}, u32[]{:S(2)}, u32[]{:S(2)}) collective-permute-start(f32[512,128]{1,0:T(8,128)S(1)} %get-tuple-element.12), channel_id=1, source_target_pairs={{0,762},{6,12},{12,6},{18,24},{24,18},{30,36},{36,30},{42,48},{48,... | collective-permute-start | bytes 786440 | tf_op jit(solution)/shard_map/ppermute | solution.py:272
  44.0 8.9 %copy-start = (f32[4,4,64,128]{3,2,1,0:T(8,128)S(1)}, f32[4,4,64,128]{3,2,1,0:T(8,128)}, u32[]{:S(2)}) copy-start(f32[4,4,64,128]{3,2,1,0:T(8,128)} %wave_ref.1) | copy-start | bytes 1572868
  44.1 8.9 %copy-start.1 = (f32[4,64,128]{2,1,0:T(8,128)S(1)}, f32[4,64,128]{2,1,0:T(8,128)}, u32[]{:S(2)}) copy-start(f32[4,64,128]{2,1,0:T(8,128)} %pot_ref.1) | copy-start | bytes 393220
  44.1 8.9 %copy-start.2 = (f32[4]{0:T(128)S(1)}, f32[4]{0:T(128)}, u32[]{:S(2)}) copy-start(f32[4]{0:T(128)} %energy_ref.3) | copy-start | bytes 52

commit v5 on v4

--- a/solution.py
+++ b/solution.py
@@ -13,7 +13,6 @@
 BF16 = jnp.bfloat16
 VMEM = pl.BlockSpec(memory_space=pltpu.VMEM)
 HBM = pl.BlockSpec(memory_space=pltpu.HBM)
-SMEM = pl.BlockSpec(memory_space=pltpu.SMEM)
 LANES = 128
 HALF = 4
 RING = 8
@@ -28,29 +27,51 @@
     return x.astype(F32).astype(BF16)
 
 
-def pack_kernel(me_ref, wave_ref, after_ref, inner_ref, outer_ref, sems):
-    bands = wave_ref.shape[0]
-    edge = wave_ref.shape[1] // 2
-    even = (me_ref[0] & 1) == 0
-    copies = []
+def pack_kernel(wave_hbm, pot_hbm, col_ref, inner_ref, outer_ref, base_ref, wave_ref, pot_ref, sems, edge_sems):
+    bands, planes, ny, nz = wave_ref.shape
+    half = planes // 2
+    whole = [pltpu.make_async_copy(pot_hbm, pot_ref, sems.at[bands])]
+    whole += [pltpu.make_async_copy(wave_hbm.at[n], wave_ref.at[n], sems.at[n]) for n in range(bands)]
+    even = (lax.axis_index("dom") & 1) == 0
+    edges = []
     for index, (ref, upper) in enumerate(((inner_ref, even), (outer_ref, jnp.logical_not(even)))):
-        start = pl.multiple_of(jnp.where(upper, edge, 0), edge)
+        start = jnp.where(upper, half, 0)
         for n in range(bands):
-            copy = pltpu.make_async_copy(
-                wave_ref.at[n, pl.ds(start, edge), :],
-                ref.at[pl.ds(n * edge, edge), :],
-                sems.at[index, n],
-            )
-            copy.start()
-            copies.append(copy)
-    for copy in copies:
+            for p in range(half):
+                edges.append(
+                    pltpu.make_async_copy(
+                        wave_hbm.at[n, start + p],
+                        ref.at[pl.ds((n * half + p) * ny, ny), :],
+                        edge_sems.at[index, n, p],
+                    )
+                )
+    for copy in edges + whole:
+        copy.start()
+    whole[0].wait()
+    slots = col_ref.shape[0] - 8
+    for n in range(bands):
+        whole[1 + n].wait()
+        energy = col_ref[slots + n : slots + n + 1, :]
+        for x in range(planes):
+            f = wave_ref[n, x]
+            near = pltpu.roll(f, 1, 0) + pltpu.roll(f, ny - 1, 0)
+            near += pltpu.roll(f, 1, 1) + pltpu.roll(f, nz - 1, 1)
+            far = pltpu.roll(f, 2, 0) + pltpu.roll(f, ny - 2, 0)
+            far += pltpu.roll(f, 2, 1) + pltpu.roll(f, nz - 2, 1)
+            for step in (-1, 1):
+                if 0 <= x + step < planes:
+                    near += wave_ref[n, x + step]
+                if 0 <= x + 2 * step < planes:
+                    far += wave_ref[n, x + 2 * step]
+            base_ref[n, x] = (pot_ref[x] + (3.75 - energy)) * f - (2.0 / 3.0) * near + (1.0 / 24.0) * far
+    for copy in edges:
         copy.wait()
 
 
 def gather_kernel(
-    chunk, aside, me_ref, slot_ref, rank_ref, idx_hbm, val_hbm, wave_hbm, d_hbm, q_hbm,
+    chunk, aside, slot_hbm, rank_hbm, energy_hbm, idx_hbm, val_hbm, wave_hbm, d_hbm, q_hbm,
     out_ref, pos_ref, col_ref,
-    idx_ref, val_ref, wave_ref, d_ref, q_ref, grid_ref, hot_ref, sems
+    slot_ref, rank_ref, energy_ref, idx_ref, val_ref, wave_ref, d_ref, q_ref, grid_ref, hot_ref, sems
 ):
     slots, points = idx_ref.shape
     nproj = val_ref.shape[1]
@@ -64,10 +85,16 @@
     copies.append(pltpu.make_async_copy(val_hbm, val_ref, sems.at[1 + bands]))
     copies.append(pltpu.make_async_copy(d_hbm, d_ref, sems.at[2 + bands]))
     copies.append(pltpu.make_async_copy(q_hbm, q_ref, sems.at[3 + bands]))
-    for copy in copies:
+    scalars = [
+        pltpu.make_async_copy(source, ref, sems.at[4 + bands + k])
+        for k, (source, ref) in enumerate(
+            ((slot_hbm, slot_ref), (energy_hbm, energy_ref), (rank_hbm, rank_ref))
+        )
+    ]
+    for copy in copies + scalars:
         copy.start()
     halves = [slice(j, j + LANES) for j in range(0, points, LANES)]
-    me = me_ref[0]
+    me = lax.axis_index("dom")
     first = (me & (HALF - 1)) * slots
     lane = lax.broadcasted_iota(jnp.int32, (kinds, LANES), 1) - first
     lane_row = lax.broadcasted_iota(jnp.int32, (8, LANES), 1) - first
@@ -90,6 +117,10 @@
         grid_ref[rows * n : rows * n + rows, LANES:] = (w - big.astype(F32)).astype(BF16)
     copies[0].wait()
     copies[1 + bands].wait()
+    for copy in scalars:
+        copy.wait()
+    for n in range(bands):
+        col_ref[slots + n : slots + n + 1, :] = jnp.full((1, LANES), energy_ref[n], F32)
     dense = chunk - aside
 
     def close(s, accs, sub):
@@ -160,32 +191,28 @@
     lax.fori_loop(0, slots // chunk, body, 0)
 
 
-def finish_kernel(me_ref, energy_ref, wave_ref, inner_ref, outer_ref, pot_ref, add_ref, out_hbm, out_ref, sems):
-    bands, planes, ny, nz = wave_ref.shape
-    even = (me_ref[0] & 1) == 0
+def finish_kernel(inner_ref, outer_ref, base_ref, add_ref, out_hbm, out_ref, sems):
+    bands, planes, ny, _ = base_ref.shape
+    half = planes // 2
+    even = (lax.axis_index("dom") & 1) == 0
 
     def side(lower, n, p):
-        at = (n * 2 + p) * ny
+        at = (n * half + p) * ny
         inner = inner_ref[at : at + ny, :]
         outer = outer_ref[at : at + ny, :]
         return jnp.where(even, outer, inner) if lower else jnp.where(even, inner, outer)
 
     copies = []
     for n in range(bands):
-        padded = [side(True, n, 0), side(True, n, 1)]
-        padded += [wave_ref[n, x] for x in range(planes)]
-        padded += [side(False, n, 0), side(False, n, 1)]
+        halo = {-2: side(True, n, 0), -1: side(True, n, 1), planes: side(False, n, 0), planes + 1: side(False, n, 1)}
         for x in range(planes):
-            f = padded[x + 2]
-            near = padded[x + 1] + padded[x + 3]
-            far = padded[x] + padded[x + 4]
-            near += pltpu.roll(f, 1, 0) + pltpu.roll(f, ny - 1, 0)
-            near += pltpu.roll(f, 1, 1) + pltpu.roll(f, nz - 1, 1)
-            far += pltpu.roll(f, 2, 0) + pltpu.roll(f, ny - 2, 0)
-            far += pltpu.roll(f, 2, 1) + pltpu.roll(f, nz - 2, 1)
-            scale = pot_ref[x] + (3.75 - energy_ref[n])
-            added = add_ref[n, ny * x : ny * x + ny, :]
-            out_ref[n, x] = added + (scale * f - (2.0 / 3.0) * near + (1.0 / 24.0) * far)
+            value = add_ref[n, ny * x : ny * x + ny, :] + base_ref[n, x]
+            for step in (-1, 1):
+                if x + step in halo:
+                    value -= (2.0 / 3.0) * halo[x + step]
+                if x + 2 * step in halo:
+                    value += (1.0 / 24.0) * halo[x + 2 * step]
+            out_ref[n, x] = value
         copy = pltpu.make_async_copy(out_ref.at[n], out_hbm.at[n], sems.at[n])
         copy.start()
         copies.append(copy)
@@ -194,7 +221,7 @@
 
 
 def scatter_kernel(
-    chunk, atoms_all, energy_ref, slot_ref, own_ref, second_ref, across_ref, beyond_ref,
+    chunk, own_ref, second_ref, across_ref, beyond_ref,
     pos_ref, col_ref, idx_ref, val_ref, out_ref, a_ref, b_ref, acc_ref, w_ref
 ):
     slots, points = idx_ref.shape
@@ -202,6 +229,10 @@
     bands, rows, _ = out_ref.shape
     kinds = bands * nproj
     height = kinds + 8
+    steps = jnp.int32(0)
+    for c in range(slots // chunk):
+        live = jnp.max(pos_ref[c * chunk : c * chunk + 1, :]) > 0
+        steps = steps + live.astype(jnp.int32)
     total = None
     for ref in (own_ref, across_ref, beyond_ref):
         same = jnp.where(pos_ref[...] == ref[kinds : kinds + 1, :], 1.0, 0.0).astype(F32)
@@ -213,12 +244,12 @@
         [ref[height:, :] for ref in (own_ref, second_ref, across_ref, beyond_ref)], axis=0
     )
     place = lax.broadcasted_iota(jnp.int32, (slots, window.shape[0]), 1).astype(F32)
-    mine = jnp.where(col_ref[:, :1] == place, 1.0, 0.0).astype(F32)
+    mine = jnp.where(col_ref[:slots, :1] == place, 1.0, 0.0).astype(F32)
     picked = jnp.dot(mine, window, precision=HIGH, preferred_element_type=F32)
     matrices = picked.T
     square = nproj * nproj
     for n in range(bands):
-        energy = energy_ref[n]
+        energy = col_ref[slots + n : slots + n + 1, :slots]
         mine_n = total[nproj * n : nproj * n + nproj]
         for i in range(nproj):
             at = nproj * i
@@ -251,17 +282,14 @@
     acc_ref[...] = jnp.zeros_like(acc_ref)
 
     def body(c, carry):
-        @pl.when(slot_ref[c * chunk] < atoms_all)
-        def _():
-            for j in range(chunk):
-                build(c * chunk + j, points * j)
-            acc_ref[...] += lax.dot_general(
-                b_ref[...], a_ref[...], (((1,), (1,)), ((), ())), preferred_element_type=F32
-            )
-
+        for j in range(chunk):
+            build(c * chunk + j, points * j)
+        acc_ref[...] += lax.dot_general(
+            b_ref[...], a_ref[...], (((1,), (1,)), ((), ())), preferred_element_type=F32
+        )
         return carry
 
-    lax.fori_loop(0, slots // chunk, body, 0)
+    lax.fori_loop(0, steps, body, 0)
     for n in range(bands):
         at = LANES * n
         out_ref[n] = (acc_ref[at : at + LANES] + acc_ref[piece + at : piece + at + LANES]).T
@@ -303,10 +331,8 @@
     slots, points = proj_index.shape
     nproj = proj_values.shape[1]
     atoms_dev = d_matrix.shape[0]
-    atoms_all = atom_rank.shape[0]
     kinds = bands * nproj
     rows = planes * ny
-    me = lax.axis_index("dom").astype(jnp.int32).reshape(1)
     flat = wave.reshape(bands, rows, nz)
     edge = bands * 2 * ny
     height = kinds + 8
@@ -321,11 +347,14 @@
         out_shape=(
             jax.ShapeDtypeStruct((height + atoms_dev, LANES), F32),
             jax.ShapeDtypeStruct((slots, LANES), F32),
-            jax.ShapeDtypeStruct((slots, LANES), F32),
+            jax.ShapeDtypeStruct((slots + 8, LANES), F32),
         ),
-        in_specs=[SMEM, SMEM, SMEM, HBM, HBM, HBM, HBM, HBM],
+        in_specs=[HBM] * 8,
         out_specs=(VMEM, VMEM, VMEM),
         scratch_shapes=[
+            pltpu.SMEM(slot_atom.shape, jnp.int32),
+            pltpu.SMEM(atom_rank.shape, jnp.int32),
+            pltpu.SMEM(energies.shape, F32),
             pltpu.VMEM(proj_index.shape, jnp.int32),
             pltpu.VMEM(proj_values.shape, F32),
             pltpu.VMEM(flat.shape, F32),
@@ -333,12 +362,19 @@
             pltpu.VMEM((square, atoms_dev), F32),
             pltpu.VMEM((bands * rows, 2 * LANES), BF16),
             pltpu.VMEM((2 * LANES, points * (chunk - aside)), BF16),
-            pltpu.SemaphoreType.DMA((4 + bands,)),
+            pltpu.SemaphoreType.DMA((7 + bands,)),
         ],
         compiler_params=pltpu.CompilerParams(vmem_limit_bytes=40 * MIB),
         cost_estimate=pl.CostEstimate(flops=10**10, bytes_accessed=10**7, transcendentals=0),
         name="gather",
-    )(me, kept(slot_atom), kept(atom_rank), kept(proj_index), kept(proj_values), kept(flat), kept(turned(d_matrix)), kept(turned(q_matrix)))
+    )(
+        *[
+            kept(x)
+            for x in (
+                slot_atom, atom_rank, energies, proj_index, proj_values, flat, turned(d_matrix), turned(q_matrix)
+            )
+        ]
+    )
 
     first = swapped(mine, inner_of)
     pair = mine[:height] + first[:height]
@@ -346,16 +382,21 @@
     second = swapped(jnp.concatenate([pair] + known, axis=0), second_of)
     half = jnp.concatenate([pair + second[:height]] + known, axis=0)
 
-    inner, outer = pl.pallas_call(
+    inner, outer, base = pl.pallas_call(
         pack_kernel,
-        out_shape=(jax.ShapeDtypeStruct((edge, nz), F32),) * 2,
-        in_specs=[SMEM, HBM, pl.BlockSpec(memory_space=pl.ANY)],
-        out_specs=(VMEM, VMEM),
-        scratch_shapes=[pltpu.SemaphoreType.DMA((2, bands))],
-        compiler_params=pltpu.CompilerParams(vmem_limit_bytes=4 * MIB),
+        out_shape=(jax.ShapeDtypeStruct((edge, nz), F32),) * 2 + (jax.ShapeDtypeStruct(wave.shape, F32),),
+        in_specs=[HBM, HBM, VMEM],
+        out_specs=(VMEM, VMEM, VMEM),
+        scratch_shapes=[
+            pltpu.VMEM(wave.shape, F32),
+            pltpu.VMEM(potential.shape, F32),
+            pltpu.SemaphoreType.DMA((bands + 1,)),
+            pltpu.SemaphoreType.DMA((2, bands, planes // 2)),
+        ],
+        compiler_params=pltpu.CompilerParams(vmem_limit_bytes=8 * MIB),
         cost_estimate=pl.CostEstimate(flops=10**6, bytes_accessed=10**6, transcendentals=0),
         name="pack",
-    )(me, kept(flat), col)
+    )(kept(wave), kept(potential), col)
     beyond = swapped(half, beyond_of)
     across = swapped(half, across_of)
     outer_got = swapped(outer, outer_of)
@@ -363,9 +404,9 @@
 
     chunk = 16
     added = pl.pallas_call(
-        functools.partial(scatter_kernel, chunk, atoms_all),
+        functools.partial(scatter_kernel, chunk),
         out_shape=jax.ShapeDtypeStruct((bands, rows, nz), F32),
-        in_specs=[SMEM, SMEM] + [VMEM] * 8,
+        in_specs=[VMEM] * 8,
         out_specs=VMEM,
         scratch_shapes=[
             pltpu.VMEM((rows, points * chunk), BF16),
@@ -376,17 +417,17 @@
         compiler_params=pltpu.CompilerParams(vmem_limit_bytes=40 * MIB),
         cost_estimate=pl.CostEstimate(flops=10**10, bytes_accessed=10**7, transcendentals=0),
         name="scatter",
-    )(kept(energies), kept(slot_atom), half, second, across, beyond, pos, col, proj_index, proj_values)
+    )(half, second, across, beyond, pos, col, proj_index, proj_values)
 
     return pl.pallas_call(
         finish_kernel,
         out_shape=jax.ShapeDtypeStruct(wave.shape, F32),
-        in_specs=[SMEM, SMEM, VMEM, VMEM, VMEM, VMEM, VMEM],
+        in_specs=[VMEM] * 4,
         out_specs=HBM,
         scratch_shapes=[pltpu.VMEM(wave.shape, F32), pltpu.SemaphoreType.DMA((bands,))],
         compiler_params=pltpu.CompilerParams(vmem_limit_bytes=8 * MIB),
         name="finish",
-    )(me, energies, wave, inner_got, outer_got, potential, added)
+    )(inner_got, outer_got, base, added)
 
 
 def solution(mesh):

time: 55.2 us -> 54.4 us (0.986)
  Pallas kernels: 11.5 us -> 9.93 us
  waiting for transfers between devices: 8.86 us -> 9.7 us
    pallas_call x1, Pallas kernels: 1.17 us -> 2.28 us  [per_device(): pl.pallas_call(pack_kernel, out_shape=(jax.ShapeDtypeStruct((edge, nz), F...]
    pallas_call x1, Pallas kernels: 1.87 us -> 0.85 us  [per_device(): pl.pallas_call(finish_kernel, out_shape=jax.ShapeDtypeStruct(wave.shape,...]
    ppermute x6, waiting for transfers between devices: 8.86 us -> 9.7 us  [swapped(): lax.ppermute(value, 'dom', [(s, partner(s) % count) for s in range(count)])]
    pallas_call x1, Pallas kernels: 3.91 us -> 3.09 us  [per_device(): pl.pallas_call(functools.partial(scatter_kernel, chunk), out_shape=jax.Sh...]
    pallas_call x1, Pallas kernels: 4.51 us -> 3.7 us  [per_device(): pl.pallas_call(functools.partial(gather_kernel, chunk, aside), out_shape=...]
  transfers between devices with their start and end apart: 6 -> 6, of which waited for: 3 -> 3; matrix products, arithmetic and copies ran while one was open for 0% -> 0% of each run, Pallas kernels for 9% -> 10%
where the time goes in v5:
time: 54.4 us; the launch traced here: 54.1 us
  starting transfers between devices  34.3 us (63%)
  Pallas kernels  9.93 us (18%)
  waiting for transfers between devices  9.7 us (18%)
    ppermute x6, starting transfers between devices, swapped(): lax.ppermute(value, 'dom', [(s, partner(s) % count) for s in range(count)])  34.3 us
    ppermute x6, waiting for transfers between devices, swapped(): lax.ppermute(value, 'dom', [(s, partner(s) % count) for s in range(count)])  9.7 us
    pallas_call x1, Pallas kernels, per_device(): pl.pallas_call(functools.partial(gather_kernel, chunk, aside), out_shape=...  3.7 us
    pallas_call x1, Pallas kernels, per_device(): pl.pallas_call(functools.partial(scatter_kernel, chunk), out_shape=jax.Sh...  3.09 us
    pallas_call x1, Pallas kernels, per_device(): pl.pallas_call(pack_kernel, out_shape=(jax.ShapeDtypeStruct((edge, nz), F...  2.28 us
  transfers between devices with their start and end apart: 6, of which 3 were waited for; matrix products, arithmetic and copies ran while one was open for 0% of the time, Pallas kernels for 10%

profile of v5, /device:TPU:256, one launch (start us, length us, event | category | flops | bytes accessed | tf_op | source)
XLA Modules:
  0.0 54.1 jit_solution(2417723040101370828)
XLA Ops:
  0.0 3.7 %gather.1 = (f32[64,128]{1,0:T(8,128)S(1)}, f32[32,128]{1,0:T(8,128)S(1)}, f32[40,128]{1,0:T(8,128)S(1)}) custom-call(s32[32]{0:T(128)} %slot_hbm.1, s32[3072]{0:T(1024)} %rank_hbm.1, f32[4]{0:T(128)} %energy_hbm.1, s32[32,256]{1,0:T(8,128)} %idx_ref.1, f32[32,8,256]{2,1,0:T(8,128)} %val_ref.1, f32[4,256,128]{2,1,0:T(8,128)} %bitcast.7, f32[64,24]{1,0:T(8,128)} %bitcast.8, ...), custom_call_target="tpu_custom_call" | custom-call | flops 10000000000 | bytes 10000000 | tf_op jit(solution)/shard_map/gather/pallas_call | solution.py:345
  3.7 5.8 %collective-permute-start.2 = (f32[64,128]{1,0:T(8,128)S(1)}, f32[64,128]{1,0:T(8,128)S(1)}, u32[]{:S(2)}, u32[]{:S(2)}) collective-permute-start(f32[64,128]{1,0:T(8,128)S(1)} %get-tuple-element.15), channel_id=1, source_target_pairs={{0,6},{6,0},{12,18},{18,12},{24,30},{30,24},{36,42},{42,36},{48,54... | collective-permute-start | bytes 98312 | tf_op jit(solution)/shard_map/ppermute | solution.py:300
  9.5 1.9 %collective-permute-done.2 = f32[64,128]{1,0:T(8,128)S(1)} collective-permute-done((f32[64,128]{1,0:T(8,128)S(1)}, f32[64,128]{1,0:T(8,128)S(1)}, u32[]{:S(2)}, u32[]{:S(2)}) %collective-permute-start.2) | collective-permute-done | bytes 32800 | tf_op jit(solution)/shard_map/ppermute | solution.py:300
  11.4 4.9 %collective-permute-start.3 = (f32[88,128]{1,0:T(8,128)S(1)}, f32[88,128]{1,0:T(8,128)S(1)}, u32[]{:S(2)}, u32[]{:S(2)}) collective-permute-start(f32[88,128]{1,0:T(8,128)S(1)} %pad_maximum_fusion.1), channel_id=1, source_target_pairs={{0,12},{6,18},{12,0},{18,6},{24,36},{30,42},{36,24},{42,30},{48,60... | collective-permute-start | bytes 135176 | tf_op jit(solution)/shard_map/ppermute | solution.py:300
  16.3 2.0 %collective-permute-done.3.second_ref = f32[88,128]{1,0:T(8,128)S(1)} collective-permute-done((f32[88,128]{1,0:T(8,128)S(1)}, f32[88,128]{1,0:T(8,128)S(1)}, u32[]{:S(2)}, u32[]{:S(2)}) %collective-permute-start.3) | collective-permute-done | bytes 45088 | tf_op jit(solution)/shard_map/ppermute | solution.py:300
  18.3 12.5 %collective-permute-start.5 = (f32[88,128]{1,0:T(8,128)S(1)}, f32[88,128]{1,0:T(8,128)S(1)}, u32[]{:S(2)}, u32[]{:S(2)}) collective-permute-start(f32[88,128]{1,0:T(8,128)S(1)} %pad_maximum_fusion.own_ref), channel_id=1, source_target_pairs={{0,756},{6,762},{12,744},{18,750},{24,60},{30,66},{36,48},{42,54},... | collective-permute-start | bytes 135176 | tf_op jit(solution)/shard_map/ppermute | solution.py:300
  30.8 1.9 %collective-permute-start.4 = (f32[88,128]{1,0:T(8,128)S(1)}, f32[88,128]{1,0:T(8,128)S(1)}, u32[]{:S(2)}, u32[]{:S(2)}) collective-permute-start(f32[88,128]{1,0:T(8,128)S(1)} %pad_maximum_fusion.own_ref), channel_id=1, source_target_pairs={{0,36},{6,42},{12,24},{18,30},{24,12},{30,18},{36,0},{42,6},{48,84... | collective-permute-start | bytes 135176 | tf_op jit(solution)/shard_map/ppermute | solution.py:300
  32.7 0.0 copy-start
  32.8 0.0 copy-start.1
  32.8 2.3 %pack.1 = (f32[512,128]{1,0:T(8,128)S(1)}, f32[512,128]{1,0:T(8,128)S(1)}, f32[4,4,64,128]{3,2,1,0:T(8,128)S(1)}) custom-call(f32[4,4,64,128]{3,2,1,0:T(8,128)} %wave_hbm.1, f32[4,64,128]{2,1,0:T(8,128)} %pot_hbm.1, f32[40,128]{1,0:T(8,128)S(1)} %get-tuple-element.11.col_ref), custom_call_target="tpu_custom_call" | custom-call | flops 1000000 | bytes 1000000 | tf_op jit(solution)/shard_map/pack/pallas_call | solution.py:385
  35.1 3.9 %collective-permute-start = (f32[512,128]{1,0:T(8,128)S(1)}, f32[512,128]{1,0:T(8,128)S(1)}, u32[]{:S(2)}, u32[]{:S(2)}) collective-permute-start(f32[512,128]{1,0:T(8,128)S(1)} %get-tuple-element.12), channel_id=1, source_target_pairs={{0,6},{6,0},{12,18},{18,12},{24,30},{30,24},{36,42},{42,36},{48,54... | collective-permute-start | bytes 786440 | tf_op jit(solution)/shard_map/ppermute | solution.py:300
  39.0 5.3 %collective-permute-start.1 = (f32[512,128]{1,0:T(8,128)S(1)}, f32[512,128]{1,0:T(8,128)S(1)}, u32[]{:S(2)}, u32[]{:S(2)}) collective-permute-start(f32[512,128]{1,0:T(8,128)S(1)} %get-tuple-element.13), channel_id=1, source_target_pairs={{0,762},{6,12},{12,6},{18,24},{24,18},{30,36},{36,30},{42,48},{48,... | collective-permute-start | bytes 786440 | tf_op jit(solution)/shard_map/ppermute | solution.py:300
  44.3 0.0 collective-permute-done.5.beyond_ref
  44.3 0.0 collective-permute-done.4.across_ref
  44.3 0.0 copy-done
  44.3 0.0 copy-done.1
  44.3 3.1 %scatter.1.add_ref = f32[4,256,128]{2,1,0:T(8,128)S(1)} custom-call(f32[88,128]{1,0:T(8,128)S(1)} %pad_maximum_fusion.own_ref, f32[88,128]{1,0:T(8,128)S(1)} %collective-permute-done.3.second_ref, f32[88,128]{1,0:T(8,128)S(1)} %collective-permute-done.4.across_ref, f32[88,128]{1,0:T(8,128)S(1)} %collective-permute-done.5.beyond_ref, ...), custom_call_target="tpu_custom_call" | custom-call | flops 10000000000 | bytes 10000000 | tf_op jit(solution)/shard_map/scatter/pallas_call | solution.py:406
  47.5 0.0 collective-permute-done.inner_ref
  47.5 5.8 %collective-permute-done.1.outer_ref = f32[512,128]{1,0:T(8,128)S(1)} collective-permute-done((f32[512,128]{1,0:T(8,128)S(1)}, f32[512,128]{1,0:T(8,128)S(1)}, u32[]{:S(2)}, u32[]{:S(2)}) %collective-permute-start.1) | collective-permute-done | bytes 262176 | tf_op jit(solution)/shard_map/ppermute | solution.py:300
  53.3 0.9 %finish.1 = f32[4,4,64,128]{3,2,1,0:T(8,128)} custom-call(f32[512,128]{1,0:T(8,128)S(1)} %collective-permute-done.inner_ref, f32[512,128]{1,0:T(8,128)S(1)} %collective-permute-done.1.outer_ref, f32[4,4,64,128]{3,2,1,0:T(8,128)S(1)} %get-tuple-element.14.base_ref, f32[4,256,128]{2,1,0:T(8,128)S(1)} %scatter.1.add_ref), custom_call_target="tpu_custom_call" | custom-call | tf_op jit(solution)/shard_map/finish/pallas_call | solution.py:422
  (6 shorter events, 0.0 us)
Async XLA Ops:
  3.7 7.6 %collective-permute-start.2 = (f32[64,128]{1,0:T(8,128)S(1)}, f32[64,128]{1,0:T(8,128)S(1)}, u32[]{:S(2)}, u32[]{:S(2)}) collective-permute-start(f32[64,128]{1,0:T(8,128)S(1)} %get-tuple-element.15), channel_id=1, source_target_pairs={{0,6},{6,0},{12,18},{18,12},{24,30},{30,24},{36,42},{42,36},{48,54... | collective-permute-start | bytes 98312 | tf_op jit(solution)/shard_map/ppermute | solution.py:300
  11.4 7.0 %collective-permute-start.3 = (f32[88,128]{1,0:T(8,128)S(1)}, f32[88,128]{1,0:T(8,128)S(1)}, u32[]{:S(2)}, u32[]{:S(2)}) collective-permute-start(f32[88,128]{1,0:T(8,128)S(1)} %pad_maximum_fusion.1), channel_id=1, source_target_pairs={{0,12},{6,18},{12,0},{18,6},{24,36},{30,42},{36,24},{42,30},{48,60... | collective-permute-start | bytes 135176 | tf_op jit(solution)/shard_map/ppermute | solution.py:300
  18.3 26.0 %collective-permute-start.5 = (f32[88,128]{1,0:T(8,128)S(1)}, f32[88,128]{1,0:T(8,128)S(1)}, u32[]{:S(2)}, u32[]{:S(2)}) collective-permute-start(f32[88,128]{1,0:T(8,128)S(1)} %pad_maximum_fusion.own_ref), channel_id=1, source_target_pairs={{0,756},{6,762},{12,744},{18,750},{24,60},{30,66},{36,48},{42,54},... | collective-permute-start | bytes 135176 | tf_op jit(solution)/shard_map/ppermute | solution.py:300
  30.8 13.5 %collective-permute-start.4 = (f32[88,128]{1,0:T(8,128)S(1)}, f32[88,128]{1,0:T(8,128)S(1)}, u32[]{:S(2)}, u32[]{:S(2)}) collective-permute-start(f32[88,128]{1,0:T(8,128)S(1)} %pad_maximum_fusion.own_ref), channel_id=1, source_target_pairs={{0,36},{6,42},{12,24},{18,30},{24,12},{30,18},{36,0},{42,6},{48,84... | collective-permute-start | bytes 135176 | tf_op jit(solution)/shard_map/ppermute | solution.py:300
  32.7 11.6 %copy-start = (f32[32,8,256]{2,1,0:T(8,128)S(1)}, f32[32,8,256]{2,1,0:T(8,128)}, u32[]{:S(2)}) copy-start(f32[32,8,256]{2,1,0:T(8,128)} %val_ref.1) | copy-start | bytes 786436
  32.8 11.6 %copy-start.1 = (s32[32,256]{1,0:T(8,128)S(1)}, s32[32,256]{1,0:T(8,128)}, u32[]{:S(2)}) copy-start(s32[32,256]{1,0:T(8,128)} %idx_ref.1) | copy-start | bytes 98308
  35.1 12.4 %collective-permute-start = (f32[512,128]{1,0:T(8,128)S(1)}, f32[512,128]{1,0:T(8,128)S(1)}, u32[]{:S(2)}, u32[]{:S(2)}) collective-permute-start(f32[512,128]{1,0:T(8,128)S(1)} %get-tuple-element.12), channel_id=1, source_target_pairs={{0,6},{6,0},{12,18},{18,12},{24,30},{30,24},{36,42},{42,36},{48,54... | collective-permute-start | bytes 786440 | tf_op jit(solution)/shard_map/ppermute | solution.py:300
  39.0 14.3 %collective-permute-start.1 = (f32[512,128]{1,0:T(8,128)S(1)}, f32[512,128]{1,0:T(8,128)S(1)}, u32[]{:S(2)}, u32[]{:S(2)}) collective-permute-start(f32[512,128]{1,0:T(8,128)S(1)} %get-tuple-element.13), channel_id=1, source_target_pairs={{0,762},{6,12},{12,6},{18,24},{24,18},{30,36},{36,30},{42,48},{48,... | collective-permute-start | bytes 786440 | tf_op jit(solution)/shard_map/ppermute | solution.py:300

commit v6 on v5

--- a/solution.py
+++ b/solution.py
@@ -70,8 +70,8 @@
 
 def gather_kernel(
     chunk, aside, slot_hbm, rank_hbm, energy_hbm, idx_hbm, val_hbm, wave_hbm, d_hbm, q_hbm,
-    out_ref, pos_ref, col_ref,
-    slot_ref, rank_ref, energy_ref, idx_ref, val_ref, wave_ref, d_ref, q_ref, grid_ref, hot_ref, sems
+    many_ref, pos_ref, col_ref,
+    out_ref, slot_ref, rank_ref, energy_ref, idx_ref, val_ref, wave_ref, d_ref, q_ref, grid_ref, hot_ref, sems
 ):
     slots, points = idx_ref.shape
     nproj = val_ref.shape[1]
@@ -129,8 +129,8 @@
         pos = rank_ref[jnp.minimum(atom, atoms_all - 1)]
         owner = pos // atoms_dev
         apart = owner ^ me
-        block = jnp.where(apart < RING, HALF, HALF + 2) + (apart & 1)
-        block = jnp.where(apart < HALF, apart, block)
+        block = jnp.where(apart < RING, HALF, HALF + 2) + (owner & 1)
+        block = jnp.where(apart < HALF, owner & (HALF - 1), block)
         column = jnp.where(live, block * atoms_dev + pos - owner * atoms_dev, -1).astype(F32)
         place = jnp.where(live, pos + 1, 0).astype(F32)
         pos_ref[pl.ds(s, 1), :] = jnp.full((1, LANES), place, F32)
@@ -189,6 +189,8 @@
         return carry
 
     lax.fori_loop(0, slots // chunk, body, 0)
+    for k in range(many_ref.shape[0]):
+        many_ref[k] = out_ref[...]
 
 
 def finish_kernel(inner_ref, outer_ref, base_ref, add_ref, out_hbm, out_ref, sems):
@@ -221,7 +223,7 @@
 
 
 def scatter_kernel(
-    chunk, own_ref, second_ref, across_ref, beyond_ref,
+    chunk, own_ref, quads_ref, across_ref, beyond_ref,
     pos_ref, col_ref, idx_ref, val_ref, out_ref, a_ref, b_ref, acc_ref, w_ref
 ):
     slots, points = idx_ref.shape
@@ -241,7 +243,7 @@
         )
         total = part if total is None else total + part
     window = jnp.concatenate(
-        [ref[height:, :] for ref in (own_ref, second_ref, across_ref, beyond_ref)], axis=0
+        [quads_ref[...], across_ref[height:, :], beyond_ref[height:, :]], axis=0
     )
     place = lax.broadcasted_iota(jnp.int32, (slots, window.shape[0]), 1).astype(F32)
     mine = jnp.where(col_ref[:slots, :1] == place, 1.0, 0.0).astype(F32)
@@ -308,10 +310,6 @@
     return d + 1 if d % 2 else d - 1
 
 
-def second_of(d):
-    return d ^ 2
-
-
 def across_of(d):
     base, y = d - d % RING, d % RING
     return base + (6, 7, 4, 5, 2, 3, 0, 1)[y]
@@ -345,13 +343,14 @@
     mine, pos, col = pl.pallas_call(
         functools.partial(gather_kernel, chunk, aside),
         out_shape=(
-            jax.ShapeDtypeStruct((height + atoms_dev, LANES), F32),
+            jax.ShapeDtypeStruct((HALF, height + atoms_dev, LANES), F32),
             jax.ShapeDtypeStruct((slots, LANES), F32),
             jax.ShapeDtypeStruct((slots + 8, LANES), F32),
         ),
         in_specs=[HBM] * 8,
         out_specs=(VMEM, VMEM, VMEM),
         scratch_shapes=[
+            pltpu.VMEM((height + atoms_dev, LANES), F32),
             pltpu.SMEM(slot_atom.shape, jnp.int32),
             pltpu.SMEM(atom_rank.shape, jnp.int32),
             pltpu.SMEM(energies.shape, F32),
@@ -376,11 +375,13 @@
         ]
     )
 
-    first = swapped(mine, inner_of)
-    pair = mine[:height] + first[:height]
-    known = [mine[height:], first[height:]]
-    second = swapped(jnp.concatenate([pair] + known, axis=0), second_of)
-    half = jnp.concatenate([pair + second[:height]] + known, axis=0)
+    count = lax.axis_size("dom")
+    groups = [list(range(k, k + HALF)) for k in range(0, count, HALF)]
+    got = lax.all_to_all(mine, "dom", 0, 0, axis_index_groups=groups)
+    quads = got[:, height:].reshape(HALF * atoms_dev, LANES)
+    upper = (lax.axis_index("dom") & 2) == 2
+    duo = jnp.where(upper, quads[2 * atoms_dev :], quads[: 2 * atoms_dev])
+    half = jnp.concatenate([got[:, :height].sum(0), duo], axis=0)
 
     inner, outer, base = pl.pallas_call(
         pack_kernel,
@@ -417,7 +418,7 @@
         compiler_params=pltpu.CompilerParams(vmem_limit_bytes=40 * MIB),
         cost_estimate=pl.CostEstimate(flops=10**10, bytes_accessed=10**7, transcendentals=0),
         name="scatter",
-    )(half, second, across, beyond, pos, col, proj_index, proj_values)
+    )(half, quads, across, beyond, pos, col, proj_index, proj_values)
 
     return pl.pallas_call(
         finish_kernel,

time: 54.4 us -> 52 us (0.956)
  starting transfers between devices: 34.3 us -> 27.6 us
  waiting for transfers between devices: 9.7 us -> 13.2 us
  Pallas kernels: 9.93 us -> 10.6 us
    ppermute x6 -> x4, starting transfers between devices: 34.3 us -> 20.5 us  [swapped(): lax.ppermute(value, 'dom', [(s, partner(s) % count) for s in range(count)])]
    all_to_all x0 -> x1, starting transfers between devices: none -> 7.16 us  [per_device(): got = lax.all_to_all(mine, 'dom', 0, 0, axis_index_groups=groups)]
    all_to_all x0 -> x1, waiting for transfers between devices: none -> 6.07 us  [per_device(): got = lax.all_to_all(mine, 'dom', 0, 0, axis_index_groups=groups)]
    ppermute x6 -> x4, waiting for transfers between devices: 9.7 us -> 7.1 us  [swapped(): lax.ppermute(value, 'dom', [(s, partner(s) % count) for s in range(count)])]
    pallas_call x1, Pallas kernels: 3.7 us -> 4.36 us  [per_device(): pl.pallas_call(functools.partial(gather_kernel, chunk, aside), out_shape=...]
  transfers between devices with their start and end apart: 6 -> 5, of which waited for: 3 -> 2; matrix products, arithmetic and copies ran while one was open for 0% -> 0% of each run, Pallas kernels for 10% -> 10%
where the time goes in v6:
time: 52 us; the launch traced here: 51.6 us
  starting transfers between devices  27.6 us (53%)
  waiting for transfers between devices  13.2 us (25%)
  Pallas kernels  10.6 us (20%)
    ppermute x4, starting transfers between devices, swapped(): lax.ppermute(value, 'dom', [(s, partner(s) % count) for s in range(count)])  20.5 us
    all_to_all x1, starting transfers between devices, per_device(): got = lax.all_to_all(mine, 'dom', 0, 0, axis_index_groups=groups)  7.16 us
    ppermute x4, waiting for transfers between devices, swapped(): lax.ppermute(value, 'dom', [(s, partner(s) % count) for s in range(count)])  7.1 us
    all_to_all x1, waiting for transfers between devices, per_device(): got = lax.all_to_all(mine, 'dom', 0, 0, axis_index_groups=groups)  6.07 us
    pallas_call x1, Pallas kernels, per_device(): pl.pallas_call(functools.partial(gather_kernel, chunk, aside), out_shape=...  4.36 us
    pallas_call x1, Pallas kernels, per_device(): pl.pallas_call(functools.partial(scatter_kernel, chunk), out_shape=jax.Sh...  3.09 us
    pallas_call x1, Pallas kernels, per_device(): pl.pallas_call(pack_kernel, out_shape=(jax.ShapeDtypeStruct((edge, nz), F...  2.29 us
  transfers between devices with their start and end apart: 5, of which 2 were waited for; matrix products, arithmetic and copies ran while one was open for 0% of the time, Pallas kernels for 10%

profile of v6, /device:TPU:256, one launch (start us, length us, event | category | flops | bytes accessed | tf_op | source)
XLA Modules:
  0.0 51.6 jit_solution(3692386573372844235)
XLA Ops:
  0.0 4.4 %gather.1 = (f32[4,64,128]{2,1,0:T(8,128)}, f32[32,128]{1,0:T(8,128)S(1)}, f32[40,128]{1,0:T(8,128)S(1)}) custom-call(s32[32]{0:T(128)} %slot_hbm.1, s32[3072]{0:T(1024)} %rank_hbm.1, f32[4]{0:T(128)} %energy_hbm.1, s32[32,256]{1,0:T(8,128)} %idx_ref.1, f32[32,8,256]{2,1,0:T(8,128)} %val_ref.1, f32[4,256,128]{2,1,0:T(8,128)} %bitcast.10, f32[64,24]{1,0:T(8,128)} %bitcast.12, ...), custom_call_target="tpu_custom_call" | custom-call | flops 10000000000 | bytes 10000000 | tf_op jit(solution)/shard_map/gather/pallas_call | solution.py:343
  4.4 7.2 %all-to-all-start = ((f32[4,64,128]{2,1,0:T(8,128)}), f32[4,64,128]{2,1,0:T(8,128)S(1)}, u32[]{:S(2)}, u32[]{:S(2)}) async-start(f32[4,64,128]{2,1,0:T(8,128)} %get-tuple-element.15), calls=%async_computation | async-start | bytes 262144 | tf_op jit(solution)/shard_map/all_to_all | solution.py:380
  11.5 6.1 %all-to-all-done = f32[4,64,128]{2,1,0:T(8,128)S(1)} async-done(((f32[4,64,128]{2,1,0:T(8,128)}), f32[4,64,128]{2,1,0:T(8,128)S(1)}, u32[]{:S(2)}, u32[]{:S(2)}) %all-to-all-start) | async-done | bytes 131104 | tf_op jit(solution)/shard_map/all_to_all | solution.py:380
  17.7 10.8 %collective-permute-start.3 = (f32[88,128]{1,0:T(8,128)S(1)}, f32[88,128]{1,0:T(8,128)S(1)}, u32[]{:S(2)}, u32[]{:S(2)}) collective-permute-start(f32[88,128]{1,0:T(8,128)S(1)} %pad_maximum_fusion.own_ref), channel_id=1, source_target_pairs={{0,756},{6,762},{12,744},{18,750},{24,60},{30,66},{36,48},{42,54},... | collective-permute-start | bytes 135176 | tf_op jit(solution)/shard_map/ppermute | solution.py:302
  28.4 1.9 %collective-permute-start.2 = (f32[88,128]{1,0:T(8,128)S(1)}, f32[88,128]{1,0:T(8,128)S(1)}, u32[]{:S(2)}, u32[]{:S(2)}) collective-permute-start(f32[88,128]{1,0:T(8,128)S(1)} %pad_maximum_fusion.own_ref), channel_id=1, source_target_pairs={{0,36},{6,42},{12,24},{18,30},{24,12},{30,18},{36,0},{42,6},{48,84... | collective-permute-start | bytes 135176 | tf_op jit(solution)/shard_map/ppermute | solution.py:302
  30.4 0.0 copy-start
  30.4 2.3 %pack.1 = (f32[512,128]{1,0:T(8,128)S(1)}, f32[512,128]{1,0:T(8,128)S(1)}, f32[4,4,64,128]{3,2,1,0:T(8,128)S(1)}) custom-call(f32[4,4,64,128]{3,2,1,0:T(8,128)} %wave_hbm.1, f32[4,64,128]{2,1,0:T(8,128)} %pot_hbm.1, f32[40,128]{1,0:T(8,128)S(1)} %get-tuple-element.11.col_ref), custom_call_target="tpu_custom_call" | custom-call | flops 1000000 | bytes 1000000 | tf_op jit(solution)/shard_map/pack/pallas_call | solution.py:386
  32.7 3.2 %collective-permute-start = (f32[512,128]{1,0:T(8,128)S(1)}, f32[512,128]{1,0:T(8,128)S(1)}, u32[]{:S(2)}, u32[]{:S(2)}) collective-permute-start(f32[512,128]{1,0:T(8,128)S(1)} %get-tuple-element.12), channel_id=1, source_target_pairs={{0,6},{6,0},{12,18},{18,12},{24,30},{30,24},{36,42},{42,36},{48,54... | collective-permute-start | bytes 786440 | tf_op jit(solution)/shard_map/ppermute | solution.py:302
  35.8 0.0 copy-start.1
  35.8 4.6 %collective-permute-start.1 = (f32[512,128]{1,0:T(8,128)S(1)}, f32[512,128]{1,0:T(8,128)S(1)}, u32[]{:S(2)}, u32[]{:S(2)}) collective-permute-start(f32[512,128]{1,0:T(8,128)S(1)} %get-tuple-element.13), channel_id=1, source_target_pairs={{0,762},{6,12},{12,6},{18,24},{24,18},{30,36},{36,30},{42,48},{48,... | collective-permute-start | bytes 786440 | tf_op jit(solution)/shard_map/ppermute | solution.py:302
  40.5 0.0 collective-permute-done.3.beyond_ref
  40.5 0.0 collective-permute-done.2.across_ref
  40.5 0.0 copy-done
  40.5 0.0 copy-done.1
  40.5 3.1 %scatter.1.add_ref = f32[4,256,128]{2,1,0:T(8,128)S(1)} custom-call(f32[88,128]{1,0:T(8,128)S(1)} %pad_maximum_fusion.own_ref, f32[96,128]{1,0:T(8,128)S(1)} %bitcast.9, f32[88,128]{1,0:T(8,128)S(1)} %collective-permute-done.2.across_ref, f32[88,128]{1,0:T(8,128)S(1)} %collective-permute-done.3.beyond_ref, f32[32,128]{1,0:T(8,128)S(1)} %get-tuple-element.16.pos_ref, ...), custom_call_target="tpu_custom_call" | custom-call | flops 10000000000 | bytes 10000000 | tf_op jit(solution)/shard_map/scatter/pallas_call | solution.py:407
  43.6 0.0 collective-permute-done.inner_ref
  43.6 7.1 %collective-permute-done.1.outer_ref = f32[512,128]{1,0:T(8,128)S(1)} collective-permute-done((f32[512,128]{1,0:T(8,128)S(1)}, f32[512,128]{1,0:T(8,128)S(1)}, u32[]{:S(2)}, u32[]{:S(2)}) %collective-permute-start.1) | collective-permute-done | bytes 262176 | tf_op jit(solution)/shard_map/ppermute | solution.py:302
  50.7 0.9 %finish.1 = f32[4,4,64,128]{3,2,1,0:T(8,128)} custom-call(f32[512,128]{1,0:T(8,128)S(1)} %collective-permute-done.inner_ref, f32[512,128]{1,0:T(8,128)S(1)} %collective-permute-done.1.outer_ref, f32[4,4,64,128]{3,2,1,0:T(8,128)S(1)} %get-tuple-element.14.base_ref, f32[4,256,128]{2,1,0:T(8,128)S(1)} %scatter.1.add_ref), custom_call_target="tpu_custom_call" | custom-call | tf_op jit(solution)/shard_map/finish/pallas_call | solution.py:423
  (4 shorter events, 0.0 us)
Async XLA Ops:
  4.4 13.2 %all-to-all-start = ((f32[4,64,128]{2,1,0:T(8,128)}), f32[4,64,128]{2,1,0:T(8,128)S(1)}, u32[]{:S(2)}, u32[]{:S(2)}) async-start(f32[4,64,128]{2,1,0:T(8,128)} %get-tuple-element.15), calls=%async_computation | async-start | bytes 262144 | tf_op jit(solution)/shard_map/all_to_all | solution.py:380
  17.7 22.8 %collective-permute-start.3 = (f32[88,128]{1,0:T(8,128)S(1)}, f32[88,128]{1,0:T(8,128)S(1)}, u32[]{:S(2)}, u32[]{:S(2)}) collective-permute-start(f32[88,128]{1,0:T(8,128)S(1)} %pad_maximum_fusion.own_ref), channel_id=1, source_target_pairs={{0,756},{6,762},{12,744},{18,750},{24,60},{30,66},{36,48},{42,54},... | collective-permute-start | bytes 135176 | tf_op jit(solution)/shard_map/ppermute | solution.py:302
  28.4 12.1 %collective-permute-start.2 = (f32[88,128]{1,0:T(8,128)S(1)}, f32[88,128]{1,0:T(8,128)S(1)}, u32[]{:S(2)}, u32[]{:S(2)}) collective-permute-start(f32[88,128]{1,0:T(8,128)S(1)} %pad_maximum_fusion.own_ref), channel_id=1, source_target_pairs={{0,36},{6,42},{12,24},{18,30},{24,12},{30,18},{36,0},{42,6},{48,84... | collective-permute-start | bytes 135176 | tf_op jit(solution)/shard_map/ppermute | solution.py:302
  30.4 10.1 %copy-start = (f32[32,8,256]{2,1,0:T(8,128)S(1)}, f32[32,8,256]{2,1,0:T(8,128)}, u32[]{:S(2)}) copy-start(f32[32,8,256]{2,1,0:T(8,128)} %val_ref.1) | copy-start | bytes 786436
  32.7 11.0 %collective-permute-start = (f32[512,128]{1,0:T(8,128)S(1)}, f32[512,128]{1,0:T(8,128)S(1)}, u32[]{:S(2)}, u32[]{:S(2)}) collective-permute-start(f32[512,128]{1,0:T(8,128)S(1)} %get-tuple-element.12), channel_id=1, source_target_pairs={{0,6},{6,0},{12,18},{18,12},{24,30},{30,24},{36,42},{42,36},{48,54... | collective-permute-start | bytes 786440 | tf_op jit(solution)/shard_map/ppermute | solution.py:302
  35.8 4.7 %copy-start.1 = (s32[32,256]{1,0:T(8,128)S(1)}, s32[32,256]{1,0:T(8,128)}, u32[]{:S(2)}) copy-start(s32[32,256]{1,0:T(8,128)} %idx_ref.1) | copy-start | bytes 98308
  35.8 14.9 %collective-permute-start.1 = (f32[512,128]{1,0:T(8,128)S(1)}, f32[512,128]{1,0:T(8,128)S(1)}, u32[]{:S(2)}, u32[]{:S(2)}) collective-permute-start(f32[512,128]{1,0:T(8,128)S(1)} %get-tuple-element.13), channel_id=1, source_target_pairs={{0,762},{6,12},{12,6},{18,24},{24,18},{30,36},{36,30},{42,48},{48,... | collective-permute-start | bytes 786440 | tf_op jit(solution)/shard_map/ppermute | solution.py:302

commit v7 on v6

--- a/solution.py
+++ b/solution.py
@@ -69,7 +69,7 @@
 
 
 def gather_kernel(
-    chunk, aside, slot_hbm, rank_hbm, energy_hbm, idx_hbm, val_hbm, wave_hbm, d_hbm, q_hbm,
+    chunk, aside, n_dom, slot_hbm, rank_hbm, energy_hbm, idx_hbm, val_hbm, wave_hbm, d_hbm, q_hbm,
     many_ref, pos_ref, col_ref,
     out_ref, slot_ref, rank_ref, energy_ref, idx_ref, val_ref, wave_ref, d_ref, q_ref, grid_ref, hot_ref, sems
 ):
@@ -128,9 +128,9 @@
         live = atom < atoms_all
         pos = rank_ref[jnp.minimum(atom, atoms_all - 1)]
         owner = pos // atoms_dev
-        apart = owner ^ me
-        block = jnp.where(apart < RING, HALF, HALF + 2) + (owner & 1)
-        block = jnp.where(apart < HALF, owner & (HALF - 1), block)
+        apart = (owner + HALF) ^ (me + HALF)
+        apart &= n_dom - 1
+        block = jnp.where(apart < RING, (owner + HALF) & (RING - 1), RING + (owner & 1))
         column = jnp.where(live, block * atoms_dev + pos - owner * atoms_dev, -1).astype(F32)
         place = jnp.where(live, pos + 1, 0).astype(F32)
         pos_ref[pl.ds(s, 1), :] = jnp.full((1, LANES), place, F32)
@@ -243,7 +243,7 @@
         )
         total = part if total is None else total + part
     window = jnp.concatenate(
-        [quads_ref[...], across_ref[height:, :], beyond_ref[height:, :]], axis=0
+        [quads_ref[...], across_ref[height:, :]], axis=0
     )
     place = lax.broadcasted_iota(jnp.int32, (slots, window.shape[0]), 1).astype(F32)
     mine = jnp.where(col_ref[:slots, :1] == place, 1.0, 0.0).astype(F32)
@@ -315,13 +315,6 @@
     return base + (6, 7, 4, 5, 2, 3, 0, 1)[y]
 
 
-def beyond_of(d):
-    base, y = d - d % RING, d % RING
-    if y < HALF:
-        return base - RING + (6, 7, 4, 5)[y]
-    return base + RING + (2, 3, 0, 1)[y - HALF]
-
-
 def per_device(
     wave, potential, energies, proj_index, proj_values, slot_atom, atom_rank, d_matrix, q_matrix
 ):
@@ -341,9 +334,9 @@
 
     chunk, aside = 16, 4
     mine, pos, col = pl.pallas_call(
-        functools.partial(gather_kernel, chunk, aside),
+        functools.partial(gather_kernel, chunk, aside, lax.axis_size("dom")),
         out_shape=(
-            jax.ShapeDtypeStruct((HALF, height + atoms_dev, LANES), F32),
+            jax.ShapeDtypeStruct((RING, height + atoms_dev, LANES), F32),
             jax.ShapeDtypeStruct((slots, LANES), F32),
             jax.ShapeDtypeStruct((slots + 8, LANES), F32),
         ),
@@ -376,12 +369,15 @@
     )
 
     count = lax.axis_size("dom")
-    groups = [list(range(k, k + HALF)) for k in range(0, count, HALF)]
+    groups = [[(k + HALF + j) % count for j in range(RING)] for k in range(0, count, RING)]
     got = lax.all_to_all(mine, "dom", 0, 0, axis_index_groups=groups)
-    quads = got[:, height:].reshape(HALF * atoms_dev, LANES)
-    upper = (lax.axis_index("dom") & 2) == 2
-    duo = jnp.where(upper, quads[2 * atoms_dev :], quads[: 2 * atoms_dev])
-    half = jnp.concatenate([got[:, :height].sum(0), duo], axis=0)
+    quads = got[:, height:].reshape(RING * atoms_dev, LANES)
+    seat = (lax.axis_index("dom") + HALF) & (RING - 1)
+    duo = lax.dynamic_slice_in_dim(quads, (seat >> 1) * (2 * atoms_dev), 2 * atoms_dev, 0)
+    early, late = got[:HALF, :height].sum(0), got[HALF:, :height].sum(0)
+    upper = seat < HALF
+    half = jnp.concatenate([jnp.where(upper, early, late), duo], axis=0)
+    beyond = jnp.where(upper, late, early)
 
     inner, outer, base = pl.pallas_call(
         pack_kernel,
@@ -398,7 +394,6 @@
         cost_estimate=pl.CostEstimate(flops=10**6, bytes_accessed=10**6, transcendentals=0),
         name="pack",
     )(kept(wave), kept(potential), col)
-    beyond = swapped(half, beyond_of)
     across = swapped(half, across_of)
     outer_got = swapped(outer, outer_of)
     inner_got = swapped(inner, inner_of)

time: 52 us -> 50.5 us (0.971)
  waiting for transfers between devices: 13.2 us -> 7.36 us
  starting transfers between devices: 27.6 us -> 32 us
    all_to_all x1, starting transfers between devices: 7.16 us -> 17.6 us  [per_device(): got = lax.all_to_all(mine, 'dom', 0, 0, axis_index_groups=groups)]
    ppermute x4 -> x3, starting transfers between devices: 20.5 us -> 14.4 us  [swapped(): lax.ppermute(value, 'dom', [(s, partner(s) % count) for s in range(count)])]
    ppermute x4 -> x3, waiting for transfers between devices: 7.1 us -> 1.2 us  [swapped(): lax.ppermute(value, 'dom', [(s, partner(s) % count) for s in range(count)])]
  transfers between devices with their start and end apart: 5 -> 4, of which waited for: 2 -> 2; matrix products, arithmetic and copies ran while one was open for 0% -> 0% of each run, Pallas kernels for 10% -> 11%
where the time goes in v7:
time: 50.5 us; the launch traced here: 50.2 us
  starting transfers between devices  32 us (63%)
  Pallas kernels  10.6 us (21%)
  waiting for transfers between devices  7.36 us (15%)
    all_to_all x1, starting transfers between devices, per_device(): got = lax.all_to_all(mine, 'dom', 0, 0, axis_index_groups=groups)  17.6 us
    ppermute x3, starting transfers between devices, swapped(): lax.ppermute(value, 'dom', [(s, partner(s) % count) for s in range(count)])  14.4 us
    all_to_all x1, waiting for transfers between devices, per_device(): got = lax.all_to_all(mine, 'dom', 0, 0, axis_index_groups=groups)  6.16 us
    pallas_call x1, Pallas kernels, per_device(): pl.pallas_call(functools.partial(gather_kernel, chunk, aside, lax.axis_si...  4.42 us
    pallas_call x1, Pallas kernels, per_device(): pl.pallas_call(functools.partial(scatter_kernel, chunk), out_shape=jax.Sh...  3.09 us
    pallas_call x1, Pallas kernels, per_device(): pl.pallas_call(pack_kernel, out_shape=(jax.ShapeDtypeStruct((edge, nz), F...  2.28 us
    ppermute x3, waiting for transfers between devices, swapped(): lax.ppermute(value, 'dom', [(s, partner(s) % count) for s in range(count)])  1.2 us
  transfers between devices with their start and end apart: 4, of which 2 were waited for; matrix products, arithmetic and copies ran while one was open for 0% of the time, Pallas kernels for 11%

profile of v7, /device:TPU:256, one launch (start us, length us, event | category | flops | bytes accessed | tf_op | source)
XLA Modules:
  0.0 50.2 jit_solution(8013507969893994590)
XLA Ops:
  0.0 4.4 %gather.1 = (f32[8,64,128]{2,1,0:T(8,128)}, f32[32,128]{1,0:T(8,128)S(1)}, f32[40,128]{1,0:T(8,128)S(1)}) custom-call(s32[32]{0:T(128)} %slot_hbm.1, s32[3072]{0:T(1024)} %rank_hbm.1, f32[4]{0:T(128)} %energy_hbm.1, s32[32,256]{1,0:T(8,128)} %idx_ref.1, f32[32,8,256]{2,1,0:T(8,128)} %val_ref.1, f32[4,256,128]{2,1,0:T(8,128)} %bitcast.10, f32[64,24]{1,0:T(8,128)} %bitcast.11, ...), custom_call_target="tpu_custom_call" | custom-call | flops 10000000000 | bytes 10000000 | tf_op jit(solution)/shard_map/gather/pallas_call | solution.py:336
  4.4 17.6 %all-to-all-start = ((f32[8,64,128]{2,1,0:T(8,128)}), f32[8,64,128]{2,1,0:T(8,128)S(1)}, u32[]{:S(2)}, u32[]{:S(2)}) async-start(f32[8,64,128]{2,1,0:T(8,128)} %get-tuple-element.15), calls=%async_computation | async-start | bytes 524288 | tf_op jit(solution)/shard_map/all_to_all | solution.py:373
  22.0 6.2 %all-to-all-done = f32[8,64,128]{2,1,0:T(8,128)S(1)} async-done(((f32[8,64,128]{2,1,0:T(8,128)}), f32[8,64,128]{2,1,0:T(8,128)S(1)}, u32[]{:S(2)}, u32[]{:S(2)}) %all-to-all-start) | async-done | bytes 262176 | tf_op jit(solution)/shard_map/all_to_all | solution.py:373
  28.3 1.9 %collective-permute-start.2 = (f32[88,128]{1,0:T(8,128)S(1)}, f32[88,128]{1,0:T(8,128)S(1)}, u32[]{:S(2)}, u32[]{:S(2)}) collective-permute-start(f32[88,128]{1,0:T(8,128)S(1)} %pad_maximum_fusion.own_ref), channel_id=1, source_target_pairs={{0,36},{6,42},{12,24},{18,30},{24,12},{30,18},{36,0},{42,6},{48,84... | collective-permute-start | bytes 135176 | tf_op jit(solution)/shard_map/ppermute | solution.py:302
  30.2 0.0 copy-start
  30.2 0.0 copy-start.1
  30.2 2.3 %pack.1 = (f32[512,128]{1,0:T(8,128)S(1)}, f32[512,128]{1,0:T(8,128)S(1)}, f32[4,4,64,128]{3,2,1,0:T(8,128)S(1)}) custom-call(f32[4,4,64,128]{3,2,1,0:T(8,128)} %wave_hbm.1, f32[4,64,128]{2,1,0:T(8,128)} %pot_hbm.1, f32[40,128]{1,0:T(8,128)S(1)} %get-tuple-element.11.col_ref), custom_call_target="tpu_custom_call" | custom-call | flops 1000000 | bytes 1000000 | tf_op jit(solution)/shard_map/pack/pallas_call | solution.py:382
  32.5 2.4 %collective-permute-start = (f32[512,128]{1,0:T(8,128)S(1)}, f32[512,128]{1,0:T(8,128)S(1)}, u32[]{:S(2)}, u32[]{:S(2)}) collective-permute-start(f32[512,128]{1,0:T(8,128)S(1)} %get-tuple-element.12), channel_id=1, source_target_pairs={{0,6},{6,0},{12,18},{18,12},{24,30},{30,24},{36,42},{42,36},{48,54... | collective-permute-start | bytes 786440 | tf_op jit(solution)/shard_map/ppermute | solution.py:302
  34.9 10.1 %collective-permute-start.1 = (f32[512,128]{1,0:T(8,128)S(1)}, f32[512,128]{1,0:T(8,128)S(1)}, u32[]{:S(2)}, u32[]{:S(2)}) collective-permute-start(f32[512,128]{1,0:T(8,128)S(1)} %get-tuple-element.13), channel_id=1, source_target_pairs={{0,762},{6,12},{12,6},{18,24},{24,18},{30,36},{36,30},{42,48},{48,... | collective-permute-start | bytes 786440 | tf_op jit(solution)/shard_map/ppermute | solution.py:302
  45.0 0.0 collective-permute-done.2.across_ref
  45.0 0.0 copy-done
  45.0 0.0 copy-done.1
  45.0 3.1 %scatter.1.add_ref = f32[4,256,128]{2,1,0:T(8,128)S(1)} custom-call(f32[88,128]{1,0:T(8,128)S(1)} %pad_maximum_fusion.own_ref, f32[192,128]{1,0:T(8,128)S(1)} %bitcast.9, f32[88,128]{1,0:T(8,128)S(1)} %collective-permute-done.2.across_ref, f32[40,128]{1,0:T(8,128)S(1)} %get-tuple-element.19.beyond_ref, f32[32,128]{1,0:T(8,128)S(1)} %get-tuple-element.16.pos_ref, ...), custom_call_target="tpu_custom_call" | custom-call | flops 10000000000 | bytes 10000000 | tf_op jit(solution)/shard_map/scatter/pallas_call | solution.py:402
  48.2 0.0 collective-permute-done.inner_ref
  48.2 1.2 %collective-permute-done.1.outer_ref = f32[512,128]{1,0:T(8,128)S(1)} collective-permute-done((f32[512,128]{1,0:T(8,128)S(1)}, f32[512,128]{1,0:T(8,128)S(1)}, u32[]{:S(2)}, u32[]{:S(2)}) %collective-permute-start.1) | collective-permute-done | bytes 262176 | tf_op jit(solution)/shard_map/ppermute | solution.py:302
  49.4 0.9 %finish.1 = f32[4,4,64,128]{3,2,1,0:T(8,128)} custom-call(f32[512,128]{1,0:T(8,128)S(1)} %collective-permute-done.inner_ref, f32[512,128]{1,0:T(8,128)S(1)} %collective-permute-done.1.outer_ref, f32[4,4,64,128]{3,2,1,0:T(8,128)S(1)} %get-tuple-element.14.base_ref, f32[4,256,128]{2,1,0:T(8,128)S(1)} %scatter.1.add_ref), custom_call_target="tpu_custom_call" | custom-call | tf_op jit(solution)/shard_map/finish/pallas_call | solution.py:418
  (5 shorter events, 0.0 us)
Async XLA Ops:
  4.4 23.8 %all-to-all-start = ((f32[8,64,128]{2,1,0:T(8,128)}), f32[8,64,128]{2,1,0:T(8,128)S(1)}, u32[]{:S(2)}, u32[]{:S(2)}) async-start(f32[8,64,128]{2,1,0:T(8,128)} %get-tuple-element.15), calls=%async_computation | async-start | bytes 524288 | tf_op jit(solution)/shard_map/all_to_all | solution.py:373
  28.3 16.7 %collective-permute-start.2 = (f32[88,128]{1,0:T(8,128)S(1)}, f32[88,128]{1,0:T(8,128)S(1)}, u32[]{:S(2)}, u32[]{:S(2)}) collective-permute-start(f32[88,128]{1,0:T(8,128)S(1)} %pad_maximum_fusion.own_ref), channel_id=1, source_target_pairs={{0,36},{6,42},{12,24},{18,30},{24,12},{30,18},{36,0},{42,6},{48,84... | collective-permute-start | bytes 135176 | tf_op jit(solution)/shard_map/ppermute | solution.py:302
  30.2 14.8 %copy-start = (f32[32,8,256]{2,1,0:T(8,128)S(1)}, f32[32,8,256]{2,1,0:T(8,128)}, u32[]{:S(2)}) copy-start(f32[32,8,256]{2,1,0:T(8,128)} %val_ref.1) | copy-start | bytes 786436
  30.2 14.8 %copy-start.1 = (s32[32,256]{1,0:T(8,128)S(1)}, s32[32,256]{1,0:T(8,128)}, u32[]{:S(2)}) copy-start(s32[32,256]{1,0:T(8,128)} %idx_ref.1) | copy-start | bytes 98308
  32.5 15.6 %collective-permute-start = (f32[512,128]{1,0:T(8,128)S(1)}, f32[512,128]{1,0:T(8,128)S(1)}, u32[]{:S(2)}, u32[]{:S(2)}) collective-permute-start(f32[512,128]{1,0:T(8,128)S(1)} %get-tuple-element.12), channel_id=1, source_target_pairs={{0,6},{6,0},{12,18},{18,12},{24,30},{30,24},{36,42},{42,36},{48,54... | collective-permute-start | bytes 786440 | tf_op jit(solution)/shard_map/ppermute | solution.py:302
  34.9 14.4 %collective-permute-start.1 = (f32[512,128]{1,0:T(8,128)S(1)}, f32[512,128]{1,0:T(8,128)S(1)}, u32[]{:S(2)}, u32[]{:S(2)}) collective-permute-start(f32[512,128]{1,0:T(8,128)S(1)} %get-tuple-element.13), channel_id=1, source_target_pairs={{0,762},{6,12},{12,6},{18,24},{24,18},{30,36},{36,30},{42,48},{48,... | collective-permute-start | bytes 786440 | tf_op jit(solution)/shard_map/ppermute | solution.py:302
